TPU v7x, 256 devices: a whole 4x4x8 slice. The times are simulated.
256 devices in a mesh: slab: 32 (over x, z_hi, y), head: 8 (over z_lo, core).
Axes of the slice: x: 4, y: 4, z: 8 (z_hi: 2, z_lo: 4; z = z_hi * 4 + z_lo), core: 2. Of those that a mesh axis runs over, the one named last changes fastest.
Arguments:
- inputs: bfloat16 [32768, 1024], P('slab'), may hold values from -6 to 6
- norm_gain: float32 [1024], replicated, may hold values from 0.1 to 1.9
- query_weight: bfloat16 [1024, 1024], P('slab', 'head'), may hold values from -0.1875 to 0.1875
- key_weight: bfloat16 [1024, 1024], P('slab', 'head'), may hold values from -0.1875 to 0.1875
- value_weight: bfloat16 [1024, 1024], P('slab', 'head'), may hold values from -0.1875 to 0.1875
- out_weight: bfloat16 [1024, 1024], P('head', 'slab'), may hold values from -0.1875 to 0.1875
- logit_scale: float32 [16], P('head'), may hold values from 0.5 to 4, as said below
- grad_output: bfloat16 [32768, 1024], P('slab'), may hold values from -6 to 6
Outputs:
- grad_inputs: bfloat16 [32768, 1024], P('slab', 'head')
- grad_gain: float32 [1024], P('head')
- grad_query_weight: float32 [1024, 1024], P('slab', 'head')
- grad_key_weight: float32 [1024, 1024], P('slab', 'head')
- grad_value_weight: float32 [1024, 1024], P('slab', 'head')
- grad_out_weight: float32 [1024, 1024], P('head', 'slab')
Inputs may be any that keep to these rules, and one draw needn't show every extreme that they name: `logit_scale`: positive multipliers of each head's attention logits.
All inputs are finite; a program needn't handle non-finite values.
Results may differ from a plain program's by a relative error of at most 0.015.
The roundings to bfloat16 on the way count: a program that leaves them out, or rounds other values in their place, can miss the bound.
Values may be sent and summed in bfloat16 or wider, within the bound.
No kernel may reach another device: no remote copies, remote signals or barrier semaphores. Data moves between devices by JAX's collectives and lax.ppermute only.
A program may use at most 128 MiB of HBM per device.

v0:
```python
import math

import jax
import jax.numpy as jnp
from jax import lax
from jax.sharding import PartitionSpec as P

NX = 32
NY = 32


def rows_first(arrays, axis, dims):
    turned = [jnp.moveaxis(a, dim, 0) for a, dim in zip(arrays, dims)]
    widths = [t[0].size for t in turned]
    both = jnp.concatenate([t.reshape(-1, w) for t, w in zip(turned, widths)], axis=1)
    whole = lax.all_gather(both, axis, axis=0, tiled=True)
    pieces = jnp.split(whole, [sum(widths[:k]) for k in range(1, len(widths))], axis=1)
    return tuple(
        (
            jnp.moveaxis(b.reshape(-1, *t.shape[1:]), 0, dim)
            for b, t, dim in zip(pieces, turned, dims)
        )
    )


def sent_together(arrays, axis, split_dim, concat_dim, along):
    both = jnp.concatenate(arrays, axis=along)
    whole, at, done = (
        lax.all_to_all(both, axis, split_axis=split_dim, concat_axis=concat_dim, tiled=True),
        0,
        [],
    )
    for a in arrays:
        done.append(lax.slice_in_dim(whole, at, at + a.shape[along], axis=along))
        at += a.shape[along]
    return tuple(done)


def shortened(x):

    def short(part):
        return part.astype(jnp.bfloat16) if part.dtype == jnp.float32 else part

    return jax.tree.map(short, x)


def split_up(x, dim, size):
    lengths = x.shape
    pieces = x.reshape(*lengths[:dim], size, lengths[dim] // size, *lengths[dim + 1 :])
    return jnp.moveaxis(pieces, dim, 0)


def summed_on_arrival(x, axis, dim):
    size = lax.axis_size(axis)
    pieces = lax.all_to_all(split_up(x, dim, size), axis, 0, 0, tiled=True)
    return jnp.sum(pieces.astype(jnp.float32), axis=0)


def sent_to_all(x, axis):
    size = lax.axis_size(axis)
    return lax.all_to_all(jnp.broadcast_to(x[None], (size, *x.shape)), axis, 0, 0, tiled=True)


def over_copies(x, axis):
    everything = sent_to_all(x, axis)
    return jnp.sum(everything, axis=0)


def summed_on_arrival_2(x, axis, dim):
    size = lax.axis_size(axis)
    pieces = lax.all_to_all(split_up(x, dim, size), axis, 0, 0, tiled=True)
    return jnp.sum(pieces, axis=0)


def line_attention(queries, key_rows, values, grad_attn, scale_factor):
    line_count, length, head_count, head_dim = queries.shape
    bundle = math.gcd(line_count, max(1, 128 // length))
    block_width = length * bundle
    blocks = line_count // bundle
    query_blocks, key_blocks, value_blocks, grad_blocks = tuple(
        (
            tensor.reshape(blocks, block_width, head_count, head_dim)
            for tensor in (queries, key_rows, values, grad_attn)
        )
    )
    position = jnp.arange(block_width) // length
    same_line = position[:, None] == position[None, :]
    factor = scale_factor[None, :, None, None]
    score_matrix = (
        jnp.einsum("bqhd,bkhd->bhqk", query_blocks, key_blocks, preferred_element_type=jnp.float32)
        * factor
    )
    score_matrix = jnp.where(same_line, score_matrix, -jnp.inf)
    highest = jnp.max(score_matrix, axis=-1, keepdims=True)
    exponent = jnp.exp(score_matrix - highest)
    softmax_p = exponent / jnp.sum(exponent, axis=-1, keepdims=True)
    rounded_probability = softmax_p.astype(jnp.bfloat16)
    output_rows = jnp.einsum(
        "bhqk,bkhd->bqhd", rounded_probability, value_blocks, preferred_element_type=jnp.float32
    )
    probability_gradient = jnp.einsum(
        "bqhd,bkhd->bhqk", grad_blocks, value_blocks, preferred_element_type=jnp.float32
    )
    row_delta = jnp.einsum("bqhd,bqhd->bhq", grad_blocks.astype(jnp.float32), output_rows)
    score_gradient = (softmax_p * (probability_gradient - row_delta[..., None]) * factor).astype(
        jnp.bfloat16
    )
    query_gradient = jnp.einsum(
        "bhqk,bkhd->bqhd", score_gradient, key_blocks, preferred_element_type=jnp.float32
    )
    key_gradient = jnp.einsum(
        "bhqk,bqhd->bkhd", score_gradient, query_blocks, preferred_element_type=jnp.float32
    )
    value_gradient = jnp.einsum(
        "bhqk,bqhd->bkhd", rounded_probability, grad_blocks, preferred_element_type=jnp.float32
    )
    return tuple(
        (
            result.reshape(line_count, length, head_count, head_dim)
            for result in (output_rows, query_gradient, key_gradient, value_gradient)
        )
    )


def local_axes(grids, scale_factor, head_dim):
    planes, rows_y, rows_x, head_width = grids[0].shape
    head_count = head_width // head_dim
    along_x = line_attention(
        *[grid.reshape(planes * rows_y, rows_x, head_count, head_dim) for grid in grids],
        scale_factor
    )
    along_x = [result.reshape(planes, rows_y, rows_x, head_width) for result in along_x]
    along_y = line_attention(
        *[
            jnp.transpose(grid, (0, 2, 1, 3)).reshape(planes * rows_x, rows_y, head_count, head_dim)
            for grid in grids
        ],
        scale_factor
    )
    along_y = [
        jnp.transpose(result.reshape(planes, rows_x, rows_y, head_width), (0, 2, 1, 3))
        for result in along_y
    ]
    return tuple((along_x[index] + along_y[index] for index in range(4)))


def z_lines(grids, scale_factor, head_dim):
    depth, rows_y, rows_x, head_width = grids[0].shape
    head_count = head_width // head_dim
    results = line_attention(
        *[
            jnp.transpose(grid, (1, 2, 0, 3)).reshape(rows_y * rows_x, depth, head_count, head_dim)
            for grid in grids
        ],
        scale_factor
    )
    return tuple(
        (
            jnp.transpose(result.reshape(rows_y, rows_x, depth, head_width), (2, 0, 1, 3)).astype(
                jnp.bfloat16
            )
            for result in results
        )
    )


def body(
    inputs, norm_gain, query_weight, key_weight, value_weight, out_weight, logit_scale, grad_output
):
    rows, width = inputs.shape
    head_width = query_weight.shape[1]
    head_dim = head_width // logit_scale.shape[0]
    slab_count = lax.axis_size("slab")
    share = width // lax.axis_size("head")
    loss_scale = 1.0 / math.sqrt(rows * slab_count)
    planes = rows // (NY * NX)
    features = inputs.astype(jnp.float32)
    inv_rms = lax.rsqrt(jnp.mean(features * features, axis=1) + 1e-06)
    normed = (features * inv_rms[:, None] * norm_gain[None, :]).astype(jnp.bfloat16)
    full_query, full_key, full_value, full_out = rows_first(
        (query_weight, key_weight, value_weight, out_weight), "slab", (0, 0, 0, 1)
    )
    queries = jnp.dot(normed, full_query, preferred_element_type=jnp.float32).astype(jnp.bfloat16)
    key_rows = jnp.dot(normed, full_key, preferred_element_type=jnp.float32).astype(jnp.bfloat16)
    values = jnp.dot(normed, full_value, preferred_element_type=jnp.float32).astype(jnp.bfloat16)
    grad_attn = lax.dot_general(
        grad_output, full_out, (((1,), (1,)), ((), ())), preferred_element_type=jnp.float32
    ).astype(jnp.bfloat16)
    scale_factor = logit_scale / math.sqrt(head_dim)
    grids = tuple(
        (
            array.reshape(planes, NY, NX, head_width)
            for array in (queries, key_rows, values, grad_attn)
        )
    )
    moved = sent_together((grids[0], grids[1], grids[2]), "slab", 1, 0, 2)
    moved_grad = lax.all_to_all(grids[3], "slab", split_axis=1, concat_axis=0, tiled=True)
    z_terms = z_lines((moved[0], moved[1], moved[2], moved_grad), scale_factor, head_dim)
    z_back = jax.tree.map(
        lambda part, own: part.astype(own.dtype),
        lax.all_to_all(shortened(z_terms), "slab", split_axis=0, concat_axis=1, tiled=True),
        z_terms,
    )
    local_terms = local_axes(grids, scale_factor, head_dim)
    combined = tuple(
        (
            (local_terms[index] + z_back[index].astype(jnp.float32))
            .astype(jnp.bfloat16)
            .reshape(rows, head_width)
            for index in range(4)
        )
    )
    attn, query_gradient, key_gradient, value_gradient = combined
    contract = (((1,), (1,)), ((), ()))
    partial_sum = lax.dot_general(
        query_gradient, full_query, contract, preferred_element_type=jnp.float32
    )
    partial_sum = partial_sum + lax.dot_general(
        key_gradient, full_key, contract, preferred_element_type=jnp.float32
    )
    partial_sum = partial_sum + lax.dot_general(
        value_gradient, full_value, contract, preferred_element_type=jnp.float32
    )
    partial_sum = partial_sum.astype(jnp.bfloat16)
    first_col = lax.axis_index("head") * share
    feature_share = lax.dynamic_slice_in_dim(features, first_col, share, 1)
    gain_share = lax.dynamic_slice_in_dim(norm_gain, first_col, share, 0)
    grad_normed = summed_on_arrival(partial_sum, "head", 1)
    row_dot = over_copies(
        jnp.sum(grad_normed * feature_share * gain_share[None, :], axis=1), "head"
    )
    grad_inputs = (
        inv_rms[:, None] * gain_share[None, :] * grad_normed
        - feature_share * (inv_rms**3)[:, None] * row_dot[:, None] / width
    ).astype(jnp.bfloat16)
    grad_gain = (
        over_copies(jnp.sum(grad_normed * feature_share * inv_rms[:, None], axis=0), "slab")
        * loss_scale
    )
    grads_stack = jnp.concatenate([query_gradient, key_gradient, value_gradient], axis=1)
    tokens_contract = (((0,), (0,)), ((), ()))
    inner = lax.dot_general(
        normed, grads_stack, tokens_contract, preferred_element_type=jnp.float32
    )
    outer = lax.dot_general(grad_output, attn, tokens_contract, preferred_element_type=jnp.float32)
    reduced = summed_on_arrival_2(jnp.concatenate([inner, outer], axis=1), "slab", 0) * loss_scale
    grad_query_weight = reduced[:, :head_width]
    grad_key_weight = reduced[:, head_width : 2 * head_width]
    grad_value_weight = reduced[:, 2 * head_width : 3 * head_width]
    grad_out_weight = reduced[:, 3 * head_width :].T
    return (
        grad_inputs,
        grad_gain,
        grad_query_weight,
        grad_key_weight,
        grad_value_weight,
        grad_out_weight,
    )


def solution(mesh):
    in_specs = (
        P("slab", None),
        P(),
        P("slab", "head"),
        P("slab", "head"),
        P("slab", "head"),
        P("head", "slab"),
        P("head"),
        P("slab", None),
    )
    out_specs = (
        P("slab", "head"),
        P("head"),
        P("slab", "head"),
        P("slab", "head"),
        P("slab", "head"),
        P("head", "slab"),
    )
    return jax.shard_map(body, mesh=mesh, in_specs=in_specs, out_specs=out_specs, check_vma=False)
```

profile of v0, /device:TPU:96, one launch (start us, length us, event | category | flops | bytes accessed | tf_op | source)
XLA Modules:
  0.0 463.2 jit_solution(10997156738980183589)
XLA Ops:
  8.8 4.0 copy.273
  17.0 76.0 %all-gather.2.cloned.1.call-done = bf16[1024,512]{1,0:T(8,128)(2,1)} async-done(((bf16[32,512]{1,0:T(8,128)(2,1)}), bf16[1024,512]{1,0:T(8,128)(2,1)}) %all-gather.2.cloned.1.call-update) | async-done | bytes 1048592 | tf_op jit(solution)/shard_map/all_gather | solution.py:16
  108.8 3.0 convolution_convert_fusion.3
  120.7 2.7 fusion.65
  130.0 5.6 %all-to-all-start.1 = ((bf16[1,32,32,128]{3,2,0,1:T(8,128)(2,1)}), bf16[1,32,32,128]{3,2,0,1:T(8,128)(2,1)}, u32[]{:S(2)}, u32[]{:S(2)}) async-start(bf16[1,32,32,128]{3,2,0,1:T(8,128)(2,1)} %bitcast.29), calls=%async_computation.1 | async-start | bytes 524288 | tf_op jit(solution)/shard_map/all_to_all | solution.py:197
  142.4 2.7 convolution_bitcast_fusion.1
  148.6 10.5 %all-to-all-start = ((bf16[1,32,96,128]{3,2,0,1:T(8,128)(2,1)}), bf16[1,32,96,128]{3,2,0,1:T(8,128)(2,1)S(1)}, u32[]{:S(2)}, u32[]{:S(2)}) async-start(bf16[1,32,96,128]{3,2,0,1:T(8,128)(2,1)} %pad_maximum_fusion.1), calls=%async_computation | async-start | bytes 1572864 | tf_op jit(solution)/shard_map/all_to_all | solution.py:29
  175.1 2.7 all-to-all-done
  194.4 9.5 %all-to-all-start.3 = ((bf16[32,1,32,128]{3,2,1,0:T(8,128)(2,1)}), bf16[32,1,32,128]{3,2,1,0:T(8,128)(2,1)}, u32[]{:S(2)}, u32[]{:S(2)}) async-start(bf16[32,1,32,128]{3,2,1,0:T(8,128)(2,1)} %copy.333), calls=%async_computation.3 | async-start | bytes 524288 | tf_op jit(solution)/shard_map/all_to_all | solution.py:201
  204.0 2.6 convolution_bitcast_fusion.2
  211.9 2.6 reshape_reshape.64
  226.4 2.7 reshape_reshape.57
  246.2 12.3 %all-to-all-start.2 = ((bf16[32,1,32,128]{3,2,1,0:T(8,128)(2,1)}), bf16[32,1,32,128]{3,2,1,0:T(8,128)(2,1)}, u32[]{:S(2)}, u32[]{:S(2)}) async-start(bf16[32,1,32,128]{3,2,1,0:T(8,128)(2,1)} %copy.321), calls=%async_computation.2 | async-start | bytes 524288 | tf_op jit(solution)/shard_map/all_to_all | solution.py:201
  259.9 3.7 fusion.46
  263.6 7.9 %all-to-all-done.2 = bf16[32,1,32,128]{3,2,1,0:T(8,128)(2,1)} async-done(((bf16[32,1,32,128]{3,2,1,0:T(8,128)(2,1)}), bf16[32,1,32,128]{3,2,1,0:T(8,128)(2,1)}, u32[]{:S(2)}, u32[]{:S(2)}) %all-to-all-start.2) | async-done | bytes 262176 | tf_op jit(solution)/shard_map/all_to_all | solution.py:201
  271.5 4.6 all-to-all-start.4
  278.2 3.7 fusion.43
  281.9 7.2 %all-to-all-done.4 = bf16[32,1,32,128]{3,2,1,0:T(8,128)(2,1)} async-done(((bf16[32,1,32,128]{3,2,1,0:T(8,128)(2,1)}), bf16[32,1,32,128]{3,2,1,0:T(8,128)(2,1)}, u32[]{:S(2)}, u32[]{:S(2)}) %all-to-all-start.4) | async-done | bytes 262176 | tf_op jit(solution)/shard_map/all_to_all | solution.py:201
  289.1 5.1 %all-to-all-start.8 = ((bf16[32,1,32,128]{3,2,1,0:T(8,128)(2,1)}), bf16[32,1,32,128]{3,2,1,0:T(8,128)(2,1)}, u32[]{:S(2)}, u32[]{:S(2)}) async-start(bf16[32,1,32,128]{3,2,1,0:T(8,128)(2,1)} %copy.353), calls=%async_computation.8 | async-start | bytes 524288 | tf_op jit(solution)/shard_map/all_to_all | solution.py:201
  296.2 5.6 %add_convert_fusion = bf16[1024,1024]{0,1:T(8,128)(2,1)} fusion(f32[1024,1024]{0,1:T(8,128)} %fusion.43, f32[1024,1024]{0,1:T(8,128)} %fusion.46, bf16[1024,128]{1,0:T(8,128)(2,1)S(1)} %bitcast.227, bf16[1024,512]{1,0:T(8,128)(2,1)} %all-gather.2.cloned.1.call-done), kind=kOutput, calls=%fused_computation.4 | convolution fusion | flops 271581184 | bytes 11010048 | tf_op jit(solution)/shard_map/dot_general | solution.py:221
  301.8 5.4 %all-to-all-done.8 = bf16[32,1,32,128]{3,2,1,0:T(8,128)(2,1)} async-done(((bf16[32,1,32,128]{3,2,1,0:T(8,128)(2,1)}), bf16[32,1,32,128]{3,2,1,0:T(8,128)(2,1)}, u32[]{:S(2)}, u32[]{:S(2)}) %all-to-all-start.8) | async-done | bytes 262176 | tf_op jit(solution)/shard_map/all_to_all | solution.py:201
  307.2 7.2 %all-to-all-start.5 = ((bf16[8,1024,128]{1,2,0:T(8,128)(2,1)}), bf16[8,1024,128]{1,2,0:T(8,128)(2,1)}, u32[]{:S(2)}, u32[]{:S(2)}) async-start(bf16[8,1024,128]{1,2,0:T(8,128)(2,1)} %bitcast.202), calls=%async_computation.5 | async-start | bytes 4194304 | tf_op jit(solution)/shard_map/all_to_all | solution.py:55
  314.4 4.0 convert_element_type.164
  326.6 3.9 fusion.24
  330.5 30.6 %all-to-all-done.5 = bf16[8,1024,128]{1,2,0:T(8,128)(2,1)} async-done(((bf16[8,1024,128]{1,2,0:T(8,128)(2,1)}), bf16[8,1024,128]{1,2,0:T(8,128)(2,1)}, u32[]{:S(2)}, u32[]{:S(2)}) %all-to-all-start.5) | async-done | bytes 2097184 | tf_op jit(solution)/shard_map/all_to_all | solution.py:55
  364.8 6.6 %all-to-all-start.7 = ((f32[32,1,128]{2,1,0:T(1,128)}), f32[32,1,128]{2,1,0:T(1,128)S(1)}, u32[]{:S(2)}, u32[]{:S(2)}) async-start(f32[32,1,128]{2,1,0:T(1,128)} %broadcast_in_dim.23), calls=%async_computation.7 | async-start | bytes 32768 | tf_op jit(solution)/shard_map/all_to_all | solution.py:61
  372.0 11.7 %all-to-all-done.7 = f32[32,1,128]{2,1,0:T(1,128)S(1)} async-done(((f32[32,1,128]{2,1,0:T(1,128)}), f32[32,1,128]{2,1,0:T(1,128)S(1)}, u32[]{:S(2)}, u32[]{:S(2)}) %all-to-all-start.7) | async-done | bytes 16416 | tf_op jit(solution)/shard_map/all_to_all | solution.py:61
  384.3 5.8 %all-to-all-start.6 = ((f32[8,1,1024]{2,1,0:T(1,128)}), f32[8,1,1024]{2,1,0:T(1,128)S(1)}, u32[]{:S(2)}, u32[]{:S(2)}) async-start(f32[8,1,1024]{2,1,0:T(1,128)} %broadcast_in_dim.22), calls=%async_computation.6 | async-start | bytes 65536 | tf_op jit(solution)/shard_map/all_to_all | solution.py:61
  390.1 3.0 pad_maximum_fusion
  393.0 2.9 copy.355
  396.0 4.8 %all-to-all-start.9 = ((f32[32,32,512]{2,1,0:T(8,128)}), f32[32,32,512]{2,1,0:T(8,128)}, u32[]{:S(2)}, u32[]{:S(2)}) async-start(f32[32,32,512]{2,1,0:T(8,128)} %bitcast.201), calls=%async_computation.9 | async-start | bytes 4194304 | tf_op jit(solution)/shard_map/all_to_all | solution.py:71
  403.3 50.7 %all-to-all-done.9 = f32[32,32,512]{2,1,0:T(8,128)} async-done(((f32[32,32,512]{2,1,0:T(8,128)}), f32[32,32,512]{2,1,0:T(8,128)}, u32[]{:S(2)}, u32[]{:S(2)}) %all-to-all-start.9) | async-done | bytes 2097184 | tf_op jit(solution)/shard_map/all_to_all | solution.py:71
  (184 shorter events, 137.7 us)
Async XLA Ops:
  7.2 85.8 %copy-start = (bf16[1024,1024]{1,0:T(8,128)(2,1)S(1)}, bf16[1024,1024]{1,0:T(8,128)(2,1)}, u32[]{:S(2)}) copy-start(bf16[1024,1024]{1,0:T(8,128)(2,1)} %param.15) | copy-start | bytes 6291460
  7.2 85.8 %all-gather.2.cloned.1.call-start = ((), (), s32[]{:S(2)}) async-start(), calls=%async_computation.10 | async-start | bytes 1081344 | tf_op jit(solution)/shard_map/all_gather | solution.py:16
  8.8 4.0 copy-start.34
  101.6 4.8 %copy-start.3 = (bf16[1024,128]{1,0:T(8,128)(2,1)}, bf16[1024,128]{1,0:T(8,128)(2,1)S(1)}, u32[]{:S(2)}) copy-start(bf16[1024,128]{1,0:T(8,128)(2,1)S(1)} %convolution_convert_fusion.5) | copy-start | bytes 786436
  111.8 7.7 %copy-start.2 = (f32[8,2,128,64]{3,1,2,0:T(2,128)S(1)}, f32[8,2,128,64]{3,1,2,0:T(2,128)}, u32[]{:S(2)}) copy-start(f32[8,2,128,64]{3,1,2,0:T(2,128)} %bitcast_convert_fusion.2) | copy-start | bytes 1572868
  128.9 12.6 %copy-start.4 = (bf16[1024,128]{1,0:T(8,128)(2,1)S(1)}, bf16[1024,128]{1,0:T(8,128)(2,1)}, u32[]{:S(2)}) copy-start(bf16[1024,128]{1,0:T(8,128)(2,1)} %copy-done.3) | copy-start | bytes 786436
  128.9 12.6 %copy-start.6 = (bf16[1024,128]{1,0:T(8,128)(2,1)S(1)}, bf16[1024,128]{1,0:T(8,128)(2,1)}, u32[]{:S(2)}) copy-start(bf16[1024,128]{1,0:T(8,128)(2,1)} %copy-done.5) | copy-start | bytes 786436
  128.9 12.6 %copy-start.7 = (bf16[1024,128]{1,0:T(8,128)(2,1)S(1)}, bf16[1024,128]{1,0:T(8,128)(2,1)}, u32[]{:S(2)}) copy-start(bf16[1024,128]{1,0:T(8,128)(2,1)} %convolution_convert_fusion.3) | copy-start | bytes 786436
  130.0 18.6 %all-to-all-start.1 = ((bf16[1,32,32,128]{3,2,0,1:T(8,128)(2,1)}), bf16[1,32,32,128]{3,2,0,1:T(8,128)(2,1)}, u32[]{:S(2)}, u32[]{:S(2)}) async-start(bf16[1,32,32,128]{3,2,0,1:T(8,128)(2,1)} %bitcast.29), calls=%async_computation.1 | async-start | bytes 524288 | tf_op jit(solution)/shard_map/all_to_all | solution.py:197
  136.8 8.3 %copy-start.13 = (bf16[8,128,2,64]{1,3,2,0:T(8,128)(2,1)}, bf16[8,128,2,64]{1,3,2,0:T(8,128)(2,1)S(1)}, u32[]{:S(2)}) copy-start(bf16[8,128,2,64]{1,3,2,0:T(8,128)(2,1)S(1)} %copy.276) | copy-start | bytes 786436
  139.6 2.9 copy-start.18
  146.7 14.3 %copy-start.14 = (bf16[8,128,2,64]{1,3,2,0:T(8,128)(2,1)S(1)}, bf16[8,128,2,64]{1,3,2,0:T(8,128)(2,1)}, u32[]{:S(2)}) copy-start(bf16[8,128,2,64]{1,3,2,0:T(8,128)(2,1)} %copy-done.13) | copy-start | bytes 786436
  148.6 29.2 %all-to-all-start = ((bf16[1,32,96,128]{3,2,0,1:T(8,128)(2,1)}), bf16[1,32,96,128]{3,2,0,1:T(8,128)(2,1)S(1)}, u32[]{:S(2)}, u32[]{:S(2)}) async-start(bf16[1,32,96,128]{3,2,0,1:T(8,128)(2,1)} %pad_maximum_fusion.1), calls=%async_computation | async-start | bytes 1572864 | tf_op jit(solution)/shard_map/all_to_all | solution.py:29
  180.7 3.9 copy-start.23
  181.1 5.0 %copy-start.11 = (f32[8,2,128,64]{2,3,1,0:T(8,128)S(1)}, f32[8,2,128,64]{2,3,1,0:T(8,128)}, u32[]{:S(2)}) copy-start(f32[8,2,128,64]{2,3,1,0:T(8,128)} %copy.382) | copy-start | bytes 1572868
  184.6 3.4 copy-start.20
  184.6 3.4 copy-start.21
  184.6 3.4 copy-start.27
  189.2 14.7 %copy-start.15 = (bf16[8,128,2,64]{1,3,2,0:T(8,128)(2,1)S(1)}, bf16[8,128,2,64]{1,3,2,0:T(8,128)(2,1)}, u32[]{:S(2)}) copy-start(bf16[8,128,2,64]{1,3,2,0:T(8,128)(2,1)} %copy-done.13) | copy-start | bytes 786436
  194.4 51.8 %all-to-all-start.3 = ((bf16[32,1,32,128]{3,2,1,0:T(8,128)(2,1)}), bf16[32,1,32,128]{3,2,1,0:T(8,128)(2,1)}, u32[]{:S(2)}, u32[]{:S(2)}) async-start(bf16[32,1,32,128]{3,2,1,0:T(8,128)(2,1)} %copy.333), calls=%async_computation.3 | async-start | bytes 524288 | tf_op jit(solution)/shard_map/all_to_all | solution.py:201
  226.4 7.5 %copy-start.22 = (bf16[8,128,2,64]{1,3,2,0:T(8,128)(2,1)S(1)}, bf16[8,128,2,64]{1,3,2,0:T(8,128)(2,1)}, u32[]{:S(2)}) copy-start(bf16[8,128,2,64]{1,3,2,0:T(8,128)(2,1)} %copy.313) | copy-start | bytes 786436
  239.9 18.6 %copy-start.10 = (f32[1,32,32,128]{3,2,1,0:T(8,128)S(1)}, f32[1,32,32,128]{3,2,1,0:T(8,128)}, u32[]{:S(2)}) copy-start(f32[1,32,32,128]{3,2,1,0:T(8,128)} %reshape_reshape.63) | copy-start | bytes 1572868
  246.2 25.3 %all-to-all-start.2 = ((bf16[32,1,32,128]{3,2,1,0:T(8,128)(2,1)}), bf16[32,1,32,128]{3,2,1,0:T(8,128)(2,1)}, u32[]{:S(2)}, u32[]{:S(2)}) async-start(bf16[32,1,32,128]{3,2,1,0:T(8,128)(2,1)} %copy.321), calls=%async_computation.2 | async-start | bytes 524288 | tf_op jit(solution)/shard_map/all_to_all | solution.py:201
  259.9 16.2 %copy-start.9 = (f32[1,32,32,128]{3,2,1,0:T(8,128)S(1)}, f32[1,32,32,128]{3,2,1,0:T(8,128)}, u32[]{:S(2)}) copy-start(f32[1,32,32,128]{3,2,1,0:T(8,128)} %reshape_reshape.57) | copy-start | bytes 1572868
  271.5 17.6 %all-to-all-start.4 = ((bf16[32,1,32,128]{3,2,1,0:T(8,128)(2,1)}), bf16[32,1,32,128]{3,2,1,0:T(8,128)(2,1)}, u32[]{:S(2)}, u32[]{:S(2)}) async-start(bf16[32,1,32,128]{3,2,1,0:T(8,128)(2,1)} %copy.345), calls=%async_computation.4 | async-start | bytes 524288 | tf_op jit(solution)/shard_map/all_to_all | solution.py:201
  278.2 16.0 %copy-start.8 = (f32[1,32,32,128]{3,2,1,0:T(8,128)S(1)}, f32[1,32,32,128]{3,2,1,0:T(8,128)}, u32[]{:S(2)}) copy-start(f32[1,32,32,128]{3,2,1,0:T(8,128)} %reshape_reshape.64) | copy-start | bytes 1572868
  289.1 18.1 %all-to-all-start.8 = ((bf16[32,1,32,128]{3,2,1,0:T(8,128)(2,1)}), bf16[32,1,32,128]{3,2,1,0:T(8,128)(2,1)}, u32[]{:S(2)}, u32[]{:S(2)}) async-start(bf16[32,1,32,128]{3,2,1,0:T(8,128)(2,1)} %copy.353), calls=%async_computation.8 | async-start | bytes 524288 | tf_op jit(solution)/shard_map/all_to_all | solution.py:201
  307.2 53.8 %all-to-all-start.5 = ((bf16[8,1024,128]{1,2,0:T(8,128)(2,1)}), bf16[8,1024,128]{1,2,0:T(8,128)(2,1)}, u32[]{:S(2)}, u32[]{:S(2)}) async-start(bf16[8,1024,128]{1,2,0:T(8,128)(2,1)} %bitcast.202), calls=%async_computation.5 | async-start | bytes 4194304 | tf_op jit(solution)/shard_map/all_to_all | solution.py:55
  330.5 41.0 %copy-start.30 = (bf16[1,32,32,128]{3,2,1,0:T(8,128)(2,1)S(1)}, bf16[1,32,32,128]{3,2,1,0:T(8,128)(2,1)}, u32[]{:S(2)}) copy-start(bf16[1,32,32,128]{3,2,1,0:T(8,128)(2,1)} %fusion.30) | copy-start | bytes 786436
  364.8 18.8 %all-to-all-start.7 = ((f32[32,1,128]{2,1,0:T(1,128)}), f32[32,1,128]{2,1,0:T(1,128)S(1)}, u32[]{:S(2)}, u32[]{:S(2)}) async-start(f32[32,1,128]{2,1,0:T(1,128)} %broadcast_in_dim.23), calls=%async_computation.7 | async-start | bytes 32768 | tf_op jit(solution)/shard_map/all_to_all | solution.py:61
  384.3 11.7 %all-to-all-start.6 = ((f32[8,1,1024]{2,1,0:T(1,128)}), f32[8,1,1024]{2,1,0:T(1,128)S(1)}, u32[]{:S(2)}, u32[]{:S(2)}) async-start(f32[8,1,1024]{2,1,0:T(1,128)} %broadcast_in_dim.22), calls=%async_computation.6 | async-start | bytes 65536 | tf_op jit(solution)/shard_map/all_to_all | solution.py:61
  396.0 58.0 %all-to-all-start.9 = ((f32[32,32,512]{2,1,0:T(8,128)}), f32[32,32,512]{2,1,0:T(8,128)}, u32[]{:S(2)}, u32[]{:S(2)}) async-start(f32[32,32,512]{2,1,0:T(8,128)} %bitcast.201), calls=%async_computation.9 | async-start | bytes 4194304 | tf_op jit(solution)/shard_map/all_to_all | solution.py:71
  (14 other events, 27.2 us)
Sparse Core Ops, SparseCore 0:
  12.0 80.9 all-gather.1
where the time goes:
time: 469 us; the launch traced here: 463 us
  waiting for transfers between devices  194 us (41%)
  local copies, waits for them, and re-layouts  91.6 us (20%)
  starting transfers between devices  72 us (15%)
  matrix products  58.2 us (12%)
  other arithmetic  32.8 us (7%)
  between operations  14.6 us (3%)
    all_gather x1, waiting for transfers between devices, rows_first(): whole = lax.all_gather(both, axis, axis=0, tiled=True)  76 us
    all_to_all x1, waiting for transfers between devices, summed_on_arrival_2(): pieces = lax.all_to_all(split_up(x, dim, size), axis, 0, 0, tiled=True)  50.7 us
    all_to_all x4, starting transfers between devices, body(): lax.all_to_all(shortened(z_terms), 'slab', split_axis=0, concat_axis=1, t...  31.4 us
    all_to_all x1, waiting for transfers between devices, summed_on_arrival(): pieces = lax.all_to_all(split_up(x, dim, size), axis, 0, 0, tiled=True)  30.6 us
    another operation x22, local copies, waits for them, and re-layouts, line_attention(): tensor.reshape(blocks, block_width, head_count, head_dim)  22.1 us
    all_to_all x4, waiting for transfers between devices, body(): lax.all_to_all(shortened(z_terms), 'slab', split_axis=0, concat_axis=1, t...  20.5 us
    convert_element_type x12, local copies, waits for them, and re-layouts, z_lines(): jnp.transpose(result.reshape(rows_y, rows_x, depth, head_width), (2, 0, 1...  13.7 us
    all_to_all x2, starting transfers between devices, sent_to_all(): lax.all_to_all(jnp.broadcast_to(x[None], (size, *x.shape)), axis, 0, 0, t...  12.5 us
  transfers between devices with their start and end apart: 11, of which 9 were waited for; matrix products, arithmetic and copies ran while one was open for 26% of the time, Pallas kernels for 0%

commit v1 on v0

v1 whole, which is shorter than its diff:
```python
import functools
import math

import jax
import jax.numpy as jnp
from jax import lax
from jax.experimental import pallas as pl
from jax.experimental.pallas import tpu as pltpu
from jax.sharding import PartitionSpec as P

BF = jnp.bfloat16
F32 = jnp.float32
SIDE = 32
LANES = 128
TOK = SIDE * SIDE
NEG = -1e30
VM = 40 << 20


def dot(a, b, ca, cb):
    return lax.dot_general(a, b, (((ca,), (cb,)), ((), ())), preferred_element_type=F32)


def call(body, outs, name, **kw):
    return pl.pallas_call(
        body,
        out_shape=outs,
        name=name,
        compiler_params=pltpu.CompilerParams(vmem_limit_bytes=VM),
        **kw,
    )


def shape(dims, kind):
    return jax.ShapeDtypeStruct(dims, kind)


def spread_body(q_ref, k_ref, v_ref, o_ref, out_ref):
    for j, ref in enumerate((q_ref, k_ref, v_ref)):
        out_ref[:, :, j * LANES : (j + 1) * LANES] = jnp.broadcast_to(
            ref[...][None], (SIDE, SIDE, LANES)
        )
    turned = o_ref[...].astype(F32).T.astype(BF)
    out_ref[:, :, 3 * LANES :] = jnp.broadcast_to(turned[None], (SIDE, SIDE, LANES))


def project_body(x_ref, go_ref, gain_ref, w_ref, out_ref, normed_ref, inv_ref):
    x = x_ref[...].astype(F32)
    rows, width = x.shape
    inv = lax.rsqrt(jnp.sum(x * x, axis=1, keepdims=True) / width + 1e-06)
    normed = (x * inv * gain_ref[...]).astype(BF)
    normed_ref[...] = normed
    inv_ref[...] = jnp.broadcast_to(inv, inv_ref.shape)
    three = dot(normed, w_ref[:, : 3 * LANES], 1, 0)
    last = dot(go_ref[...], w_ref[:, 3 * LANES :], 1, 0)
    for j in range(4):
        part = three[:, j * LANES : (j + 1) * LANES] if j < 3 else last
        out_ref[:, j] = part.astype(BF).reshape(rows // SIDE, SIDE, LANES)


def first_head(rows):
    return lax.broadcasted_iota(jnp.int32, (rows, LANES), 1) < LANES // 2


def stacked(a):
    rows = a.shape[0]
    keep = first_head(rows)
    zero = jnp.zeros_like(a)
    return jnp.concatenate([jnp.where(keep, a, zero), jnp.where(keep, zero, a)], axis=0)


def folded(a):
    rows = a.shape[0] // 2
    return jnp.where(first_head(rows), a[:rows], a[rows:])


def attend(q, k, v, g, factors, bias):
    rows = q.shape[0]
    k2, v2 = stacked(k), stacked(v)
    s = dot(q, k2, 1, 1)
    dp = dot(g, v2, 1, 1)
    probs = []
    for h in range(2):
        sh = s[:, h * rows : (h + 1) * rows] * factors[h] + bias
        top = jnp.max(sh, axis=1, keepdims=True)
        e = jnp.exp(sh - top)
        probs.append(e / jnp.sum(e, axis=1, keepdims=True))
    pb = jnp.concatenate([p.astype(BF) for p in probs], axis=1)
    out = dot(pb, v2, 1, 0)
    go = g.astype(F32) * out
    keep = first_head(rows)
    grads = []
    for h in range(2):
        mine = jnp.where(keep, go, 0.0) if h == 0 else jnp.where(keep, 0.0, go)
        delta = jnp.sum(mine, axis=1, keepdims=True)
        dh = dp[:, h * rows : (h + 1) * rows]
        grads.append((probs[h] * (dh - delta) * factors[h]).astype(BF))
    ds = jnp.concatenate(grads, axis=1)
    gq = dot(ds, k2, 1, 0)
    gk = folded(dot(ds, q, 0, 0))
    gv = folded(dot(pb, g, 0, 0))
    return out, gq, gk, gv


def same_line(rows, line):
    a = line(lax.broadcasted_iota(jnp.int32, (rows, rows), 0))
    b = line(lax.broadcasted_iota(jnp.int32, (rows, rows), 1))
    return jnp.where(a == b, 0.0, NEG).astype(F32)


def strided_lines(in_ref, f_ref, wide_ref, bias_ref, add):
    for j in range(4):
        wide_ref[j] = in_ref[:, j].astype(F32).reshape(SIDE, 4, 8, LANES)
    rows = 8 * SIDE
    bias_ref[...] = same_line(rows, lambda i: i % 8)
    factors = (f_ref[0], f_ref[1])

    def step(b, _):
        parts = [wide_ref[j, :, b].reshape(rows, LANES).astype(BF) for j in range(4)]
        for j, r in enumerate(attend(*parts, factors, bias_ref[...])):
            add(j, b, r.reshape(SIDE, 8, LANES))
        return 0

    lax.fori_loop(0, 4, step, 0)


def plane_body(in_ref, f_ref, out_ref, wide_ref, bias_ref, bias_x_ref):
    rows = 4 * SIDE
    bias_x_ref[...] = same_line(rows, lambda i: i // SIDE)
    factors = (f_ref[0], f_ref[1])

    def step(b, _):
        parts = [in_ref[pl.ds(4 * b, 4), j].reshape(rows, LANES) for j in range(4)]
        for j, r in enumerate(attend(*parts, factors, bias_x_ref[...])):
            out_ref[j, pl.ds(4 * b, 4)] = r.reshape(4, 4, 8, LANES)
        return 0

    lax.fori_loop(0, 8, step, 0)

    def add(j, b, r):
        out_ref[j, :, b] += r

    strided_lines(in_ref, f_ref, wide_ref, bias_ref, add)


def depth_body(in_ref, f_ref, out_ref, wide_ref, res_ref, bias_ref):
    def add(j, b, r):
        res_ref[j, :, b] = r

    strided_lines(in_ref, f_ref, wide_ref, bias_ref, add)
    for j in range(4):
        out_ref[:, j] = res_ref[j].reshape(SIDE, SIDE, LANES).astype(BF)


def halves(a):
    high = a.astype(BF)
    return high, (a - high.astype(F32)).astype(BF)


def combine_body(
    h_ref, loc_ref, back_ref, proj_ref, normed_ref, go_ref, w_ref,
    away_ref, keep_ref, dots_ref, wg_ref, g_ref,
):
    zl, core = h_ref[0] // 2, h_ref[0] % 2
    total = jnp.zeros((TOK, LANES), F32)
    for j in range(4):
        part = loc_ref[j].reshape(TOK, LANES) + back_ref[:, j].astype(F32).reshape(TOK, LANES)
        part = part.astype(BF)
        at = (j - 1) % 4
        g_ref[:, at * LANES : (at + 1) * LANES] = part
        if j > 0:
            total += part.astype(F32) * proj_ref[:, j - 1].astype(F32).reshape(TOK, LANES)
    rows = [
        jnp.sum(total[i * LANES : (i + 1) * LANES].T, axis=0, keepdims=True) for i in range(8)
    ]
    dots = jnp.concatenate(rows, axis=0)
    dots_ref[...] = dots
    high, low = halves(dots)
    away_ref[4 * TOK : 4 * TOK + 8] = high
    away_ref[4 * TOK + 8 :] = low

    def block(h):
        w = w_ref[pl.ds(pl.multiple_of(h * LANES, LANES), LANES), : 3 * LANES]
        return dot(g_ref[:, : 3 * LANES], w, 1, 1).astype(BF)

    def step(i, _):
        away_ref[pl.ds(pl.multiple_of(i * TOK, TOK), TOK)] = block(2 * i + 1 - core)
        keep_ref[i] = block(2 * i + core)
        return 0

    lax.fori_loop(0, 4, step, 0)

    def wstep(i, _):
        at = pl.ds(pl.multiple_of(i * 256, 256), 256)
        three = dot(normed_ref[:, at], g_ref[:, : 3 * LANES], 0, 0)
        last = dot(go_ref[:, at], g_ref[:, 3 * LANES :], 0, 0)
        for j in range(4):
            part = three[:, j * LANES : (j + 1) * LANES] if j < 3 else last
            wg_ref[pl.ds(8 * i, 8), j] = part.astype(BF).reshape(8, SIDE, LANES)
        return 0

    lax.fori_loop(0, 4, wstep, 0)


def pair_body(h_ref, got_ref, keep_ref, dots_ref, s1_ref, s2_ref, s3_ref, own_ref, both_ref):
    zl = h_ref[0] // 2
    dots = dots_ref[...] + got_ref[4 * TOK : 4 * TOK + 8].astype(F32)
    dots = dots + got_ref[4 * TOK + 8 :].astype(F32)
    both_ref[...] = dots
    high, low = halves(dots)

    def block(i):
        mine = keep_ref[i].astype(F32)
        return mine + got_ref[pl.ds(pl.multiple_of(i * TOK, TOK), TOK)].astype(F32)

    for d, ref in enumerate((s1_ref, s2_ref, s3_ref)):
        ref[:TOK] = block((zl + d + 1) % 4).astype(BF)
        ref[TOK : TOK + 8] = high
        ref[TOK + 8 :] = low
    own_ref[...] = block(zl)


def norm_body(
    h_ref, x_ref, gain_ref, own_ref, r1_ref, r2_ref, r3_ref, dots_ref, inv_ref, gx_ref, tail_ref
):
    grad = own_ref[...]
    dots = dots_ref[...]
    for ref in (r1_ref, r2_ref, r3_ref):
        grad = grad + ref[:TOK].astype(F32)
        dots = dots + ref[TOK : TOK + 8].astype(F32) + ref[TOK + 8 :].astype(F32)
    cols = [
        jnp.broadcast_to(dots[i : i + 1], (LANES, LANES)).T for i in range(8)
    ]
    row_dot = jnp.concatenate(cols, axis=0)
    x = x_ref[...].astype(F32)
    inv = inv_ref[...]
    gx = inv * gain_ref[...] * grad - x * (inv * inv) * row_dot * (1.0 / 1024)
    gx_ref[...] = gx.astype(BF)
    gain = jnp.sum(grad * x * inv, axis=0, keepdims=True)
    high, low = halves(gain)
    first = lax.broadcasted_iota(jnp.int32, (8, LANES), 0) == 0
    zero = jnp.zeros((8, LANES), F32)
    tail_ref[...] = jnp.concatenate(
        [
            jnp.where(first, jnp.broadcast_to(high.astype(F32), (8, LANES)), zero),
            jnp.where(first, jnp.broadcast_to(low.astype(F32), (8, LANES)), zero),
        ],
        axis=0,
    ).astype(BF)


def sum_body(in_ref, q_ref, k_ref, v_ref, o_ref, gain_ref, *, scale):
    acc = in_ref[0].astype(F32)
    for i in range(1, SIDE):
        acc = acc + in_ref[i].astype(F32)
    acc = acc * scale
    for j, ref in enumerate((q_ref, k_ref, v_ref)):
        ref[...] = acc[j * SIDE : (j + 1) * SIDE]
    o_ref[...] = acc[3 * SIDE : 4 * SIDE].T
    gain_ref[...] = acc[4 * SIDE : 4 * SIDE + 1] + acc[4 * SIDE + 8 : 4 * SIDE + 9]


SMEM = pl.BlockSpec(memory_space=pltpu.SMEM)
VMEM = pl.BlockSpec(memory_space=pltpu.VMEM)


def body(
    inputs, norm_gain, query_weight, key_weight, value_weight, out_weight, logit_scale, grad_output
):
    rows, width = inputs.shape
    head_dim = 64
    head = lax.axis_index("head").astype(jnp.int32).reshape(1)
    gain = norm_gain.reshape(1, width)
    factors = logit_scale / math.sqrt(head_dim)

    spread = call(spread_body, shape((SIDE, SIDE, 4 * LANES), BF), "spread")(
        query_weight, key_weight, value_weight, out_weight
    )
    weights = lax.all_to_all(spread, "slab", 0, 0, tiled=True).reshape(width, 4 * LANES)

    blk = 256
    proj, normed, inv = call(
        project_body,
        (
            shape((SIDE, 4, SIDE, LANES), BF),
            shape((rows, width), BF),
            shape((rows, LANES), F32),
        ),
        "project",
        grid=(rows // blk,),
        in_specs=[
            pl.BlockSpec((blk, width), lambda i: (i, 0)),
            pl.BlockSpec((blk, width), lambda i: (i, 0)),
            pl.BlockSpec((1, width), lambda i: (0, 0)),
            pl.BlockSpec((width, 4 * LANES), lambda i: (0, 0)),
        ],
        out_specs=(
            pl.BlockSpec((blk // SIDE, 4, SIDE, LANES), lambda i: (i, 0, 0, 0)),
            pl.BlockSpec((blk, width), lambda i: (i, 0)),
            pl.BlockSpec((blk, LANES), lambda i: (i, 0)),
        ),
    )(inputs, grad_output, gain, weights)

    moved = lax.all_to_all(proj, "slab", 0, 0, tiled=True)
    big = (4, SIDE, 4, 8, LANES)
    local = call(
        plane_body,
        shape(big, F32),
        "plane",
        in_specs=[VMEM, SMEM],
        scratch_shapes=[
            pltpu.VMEM(big, F32),
            pltpu.VMEM((256, 256), F32),
            pltpu.VMEM((128, 128), F32),
        ],
    )(proj, factors)
    z_terms = call(
        depth_body,
        shape((SIDE, 4, SIDE, LANES), BF),
        "depth",
        in_specs=[VMEM, SMEM],
        scratch_shapes=[
            pltpu.VMEM(big, F32),
            pltpu.VMEM(big, F32),
            pltpu.VMEM((256, 256), F32),
        ],
    )(moved, factors)
    back = lax.all_to_all(z_terms, "slab", 0, 0, tiled=True)

    away, keep, dots, wg = call(
        combine_body,
        (
            shape((4 * TOK + 16, LANES), BF),
            shape((4, TOK, LANES), BF),
            shape((8, LANES), F32),
            shape((SIDE, 4, SIDE, LANES), BF),
        ),
        "combine",
        in_specs=[SMEM] + [VMEM] * 6,
        scratch_shapes=[pltpu.VMEM((TOK, 4 * LANES), BF)],
    )(head, local, back, proj, normed, grad_output, weights)

    got = lax.ppermute(away, "head", [(i, i ^ 1) for i in range(8)])
    piece = shape((TOK + 16, LANES), BF)
    s1, s2, s3, own, dots = call(
        pair_body,
        (piece, piece, piece, shape((TOK, LANES), F32), shape((8, LANES), F32)),
        "pair",
        in_specs=[SMEM] + [VMEM] * 3,
    )(head, got, keep, dots)
    r1, r2, r3 = (
        lax.ppermute(s, "head", [(i, (i + 2 * d) % 8) for i in range(8)])
        for d, s in ((1, s1), (2, s2), (3, s3))
    )

    whole = lambda dims: pl.BlockSpec(dims, lambda i, h: (0,) * len(dims))
    grad_inputs, tail = pl.pallas_call(
        norm_body,
        out_shape=(shape((rows, LANES), BF), shape((16, LANES), BF)),
        name="norm_back",
        grid_spec=pltpu.PrefetchScalarGridSpec(
            num_scalar_prefetch=1,
            grid=(1,),
            in_specs=[
                pl.BlockSpec((rows, LANES), lambda i, h: (0, h[0])),
                pl.BlockSpec((1, LANES), lambda i, h: (0, h[0])),
                whole((TOK, LANES)),
                whole((TOK + 16, LANES)),
                whole((TOK + 16, LANES)),
                whole((TOK + 16, LANES)),
                whole((8, LANES)),
                whole((TOK, LANES)),
            ],
            out_specs=(whole((rows, LANES)), whole((16, LANES))),
        ),
        compiler_params=pltpu.CompilerParams(vmem_limit_bytes=VM),
    )(head, inputs, gain, own, r1, r2, r3, dots, inv)

    sent = jnp.concatenate(
        [wg.reshape(SIDE, 4 * SIDE, LANES), jnp.broadcast_to(tail[None], (SIDE, 16, LANES))],
        axis=1,
    )
    pieces = lax.all_to_all(sent, "slab", 0, 0, tiled=True)
    part = shape((SIDE, LANES), F32)
    gqw, gkw, gvw, gow, ggain = call(
        functools.partial(sum_body, scale=1.0 / math.sqrt(rows * SIDE)),
        (part, part, part, shape((LANES, SIDE), F32), shape((1, LANES), F32)),
        "slab_sum",
    )(pieces)
    return grad_inputs, ggain.reshape(LANES), gqw, gkw, gvw, gow


def solution(mesh):
    in_specs = (
        P("slab", None),
        P(),
        P("slab", "head"),
        P("slab", "head"),
        P("slab", "head"),
        P("head", "slab"),
        P("head"),
        P("slab", None),
    )
    out_specs = (
        P("slab", "head"),
        P("head"),
        P("slab", "head"),
        P("slab", "head"),
        P("slab", "head"),
        P("head", "slab"),
    )
    return jax.shard_map(body, mesh=mesh, in_specs=in_specs, out_specs=out_specs, check_vma=False)
```

time: 469 us -> 200 us (0.43); the launches traced: 463 us -> 199 us
  waiting for transfers between devices: 194 us -> 44.9 us
  local copies, waits for them, and re-layouts: 91.6 us -> 12.9 us
  blocking collectives: 0 us -> 71.6 us
  matrix products: 58.2 us -> 0 us
  other arithmetic: 32.8 us -> 0.09 us
  starting transfers between devices: 72 us -> 39.4 us
  Pallas kernels: 0 us -> 29.5 us
  between operations: 14.6 us -> 0.78 us
    all_to_all x10 -> x2, waiting for transfers between devices: 118 us -> 19.9 us  [the longest x1 16.2 us: body(): moved = lax.all_to_all(proj, 'slab', 0, 0, tiled=True)]
    all_gather x1 -> x0, waiting for transfers between devices: 76 us -> none  [rows_first(): whole = lax.all_gather(both, axis, axis=0, tiled=True)]
    all_to_all x0 -> x2, blocking collectives: none -> 71.6 us  [the longest x1 37.6 us: body(): pieces = lax.all_to_all(sent, 'slab', 0, 0, tiled=True)]
    dot_general x24 -> x0, matrix products: 51.4 us -> none  [the longest x3 6.99 us: line_attention(): jnp.einsum('bhqk,bkhd->bqhd', rounded_probability, value_blocks, preferre...]
    all_to_all x10 -> x2, starting transfers between devices: 71.9 us -> 23.9 us  [the longest x1 13.8 us: body(): back = lax.all_to_all(z_terms, 'slab', 0, 0, tiled=True)]
    another operation x30 -> x0, local copies, waits for them, and re-layouts: 39.9 us -> none  [the longest x22 22.1 us: line_attention(): tensor.reshape(blocks, block_width, head_count, head_dim)]
    pallas_call x0 -> x8, Pallas kernels: none -> 29.5 us  [the longest x1 11.3 us: body(): call(plane_body, shape(big, F32), 'plane', in_specs=[VMEM, SMEM], scratch...]
    ppermute x0 -> x4, waiting for transfers between devices: none -> 25 us  [the longest x3 22.4 us: body(): lax.ppermute(s, 'head', [(i, (i + 2 * d) % 8) for i in range(8)])]
  transfers between devices with their start and end apart: 11 -> 6, of which waited for: 9 -> 5; matrix products, arithmetic and copies ran while one was open for 26% -> 0% of each run, Pallas kernels for 0% -> 6%
where the time goes in v1:
time: 200 us; the launch traced here: 199 us
  blocking collectives  71.6 us (36%)
  waiting for transfers between devices  44.9 us (22%)
  starting transfers between devices  39.4 us (20%)
  Pallas kernels  29.5 us (15%)
  local copies, waits for them, and re-layouts  12.9 us (6%)
    all_to_all x1, blocking collectives, body(): pieces = lax.all_to_all(sent, 'slab', 0, 0, tiled=True)  37.6 us
    all_to_all x1, blocking collectives, body(): lax.all_to_all(spread, 'slab', 0, 0, tiled=True).reshape(width, 4 * LANES)  33.9 us
    ppermute x3, waiting for transfers between devices, body(): lax.ppermute(s, 'head', [(i, (i + 2 * d) % 8) for i in range(8)])  22.4 us
    all_to_all x1, waiting for transfers between devices, body(): moved = lax.all_to_all(proj, 'slab', 0, 0, tiled=True)  16.2 us
    ppermute x3, starting transfers between devices, body(): lax.ppermute(s, 'head', [(i, (i + 2 * d) % 8) for i in range(8)])  15.4 us
    all_to_all x1, starting transfers between devices, body(): back = lax.all_to_all(z_terms, 'slab', 0, 0, tiled=True)  13.8 us
    unnamed x32, local copies, waits for them, and re-layouts  12.9 us
    pallas_call x1, Pallas kernels, body(): call(plane_body, shape(big, F32), 'plane', in_specs=[VMEM, SMEM], scratch...  11.3 us
  transfers between devices with their start and end apart: 6, of which 5 were waited for; matrix products, arithmetic and copies ran while one was open for 0% of the time, Pallas kernels for 6%

profile of v1, /device:TPU:96, one launch (start us, length us, event | category | flops | bytes accessed | tf_op | source)
XLA Modules:
  0.0 199.2 jit_solution(4749791460459019501)
XLA Ops:
  0.7 1.0 copy.14.o_ref
  1.6 0.7 copy-done.11
  2.3 0.7 copy-done.12
  3.0 0.7 copy-done.13
  3.7 0.2 spread.1
  3.9 33.9 %all_to_all.20 = bf16[32,32,512]{2,1,0:T(8,128)(2,1)S(1)} all-to-all(bf16[32,32,512]{2,1,0:T(8,128)(2,1)S(1)} %spread.1), channel_id=1, replica_groups=mesh['slab'=32,'head'=8] {'slab'}, dimensions={0} | all-to-all | bytes 2097152 | tf_op jit(solution)/shard_map/all_to_all | solution.py:279
  37.8 1.6 copy-done.3
  39.4 3.5 %project.1 = (bf16[32,4,32,128]{3,2,1,0:T(8,128)(2,1)}, bf16[1024,1024]{1,0:T(8,128)(2,1)S(1)}, f32[1024,128]{1,0:T(8,128)S(1)}) custom-call(bf16[1024,1024]{1,0:T(8,128)(2,1)S(1)} %copy-done.3, bf16[1024,1024]{1,0:T(8,128)(2,1)S(1)} %copy-done, f32[1,1024]{1,0:T(1,128)S(1)} %bitcast.8, bf16[1024,512]{1,0:T(8,128)(2,1)S(1)} %bitcast.5), custom_call_target="tpu_custom_call" | custom-call | tf_op jit(solution)/shard_map/project/pallas_call | solution.py:282
  43.0 1.3 copy-done.6
  44.3 0.8 copy-done.8
  45.1 10.1 %all-to-all-start.1 = ((bf16[32,4,32,128]{3,2,1,0:T(8,128)(2,1)}), bf16[32,4,32,128]{3,2,1,0:T(8,128)(2,1)}, u32[]{:S(2)}, u32[]{:S(2)}) async-start(bf16[32,4,32,128]{3,2,1,0:T(8,128)(2,1)} %get-tuple-element.25.in_ref.proj_ref), calls=%async_computation.1 | async-start | bytes 2097152 | tf_op jit(solution)/shard_map/all_to_all | solution.py:304
  55.2 16.2 %all-to-all-done.1.in_ref = bf16[32,4,32,128]{3,2,1,0:T(8,128)(2,1)} async-done(((bf16[32,4,32,128]{3,2,1,0:T(8,128)(2,1)}), bf16[32,4,32,128]{3,2,1,0:T(8,128)(2,1)}, u32[]{:S(2)}, u32[]{:S(2)}) %all-to-all-start.1) | async-done | bytes 1048608 | tf_op jit(solution)/shard_map/all_to_all | solution.py:304
  71.5 5.4 %depth.1 = bf16[32,4,32,128]{3,2,1,0:T(8,128)(2,1)S(1)} custom-call(bf16[32,4,32,128]{3,2,1,0:T(8,128)(2,1)} %all-to-all-done.1.in_ref, f32[2]{0:T(128)S(1)} %broadcast_multiply_fusion.f_ref), custom_call_target="tpu_custom_call" | custom-call | tf_op jit(solution)/shard_map/depth/pallas_call | solution.py:317
  76.9 1.0 copy-done.5
  77.8 13.8 %all-to-all-start.2 = ((bf16[32,4,32,128]{3,2,1,0:T(8,128)(2,1)}), bf16[32,4,32,128]{3,2,1,0:T(8,128)(2,1)}, u32[]{:S(2)}, u32[]{:S(2)}) async-start(bf16[32,4,32,128]{3,2,1,0:T(8,128)(2,1)} %copy-done.5), calls=%async_computation.2 | async-start | bytes 2097152 | tf_op jit(solution)/shard_map/all_to_all | solution.py:328
  91.7 11.3 %plane.1.loc_ref = f32[4,32,4,8,128]{4,3,2,1,0:T(8,128)S(1)} custom-call(bf16[32,4,32,128]{3,2,1,0:T(8,128)(2,1)} %get-tuple-element.25.in_ref.proj_ref, f32[2]{0:T(128)S(1)} %broadcast_multiply_fusion.f_ref), custom_call_target="tpu_custom_call" | custom-call | tf_op jit(solution)/shard_map/plane/pallas_call | solution.py:306
  103.0 1.3 copy-done.1
  104.3 3.6 %all-to-all-done.2.back_ref = bf16[32,4,32,128]{3,2,1,0:T(8,128)(2,1)} async-done(((bf16[32,4,32,128]{3,2,1,0:T(8,128)(2,1)}), bf16[32,4,32,128]{3,2,1,0:T(8,128)(2,1)}, u32[]{:S(2)}, u32[]{:S(2)}) %all-to-all-start.2) | async-done | bytes 1048608 | tf_op jit(solution)/shard_map/all_to_all | solution.py:328
  107.9 1.6 copy-done.2
  109.5 1.6 copy-done.7
  111.1 7.0 %combine.1 = (bf16[4112,128]{1,0:T(8,128)(2,1)S(1)}, bf16[4,1024,128]{2,1,0:T(8,128)(2,1)S(1)}, f32[8,128]{1,0:T(8,128)S(1)}, bf16[32,4,32,128]{3,2,1,0:T(8,128)(2,1)S(1)}) custom-call(s32[1]{0:T(128)} %bitcast.h_ref, f32[4,32,4,8,128]{4,3,2,1,0:T(8,128)S(1)} %copy-done.2, bf16[32,4,32,128]{3,2,1,0:T(8,128)(2,1)} %all-to-all-done.2.back_ref, ...), custom_call_target="tpu_custom_call" | custom-call | tf_op jit(solution)/shard_map/combine/pallas_call | solution.py:330
  118.2 2.7 %collective-permute-done.got_ref = bf16[4112,128]{1,0:T(8,128)(2,1)S(1)} collective-permute-done((bf16[4112,128]{1,0:T(8,128)(2,1)S(1)}, bf16[4112,128]{1,0:T(8,128)(2,1)S(1)}, u32[]{:S(2)}, u32[]{:S(2)}) %collective-permute-start) | collective-permute-done | bytes 1052704 | tf_op jit(solution)/shard_map/ppermute | solution.py:343
  120.9 0.2 pair.1
  121.1 1.8 collective-permute-start.1
  123.0 12.4 %collective-permute-start.2 = (bf16[1040,128]{1,0:T(8,128)(2,1)S(1)}, bf16[1040,128]{1,0:T(8,128)(2,1)S(1)}, u32[]{:S(2)}, u32[]{:S(2)}) collective-permute-start(bf16[1040,128]{1,0:T(8,128)(2,1)S(1)} %get-tuple-element.32), channel_id=1, source_target_pairs={{0,4},{1,5},{2,6},{3,7},{4,0},{5,1},{6,2},{7,3},{8,12},{9,13},{10,... | collective-permute-start | bytes 798728 | tf_op jit(solution)/shard_map/ppermute | solution.py:352
  135.4 1.2 collective-permute-start.3
  136.6 4.1 %collective-permute-done.1.r1_ref = bf16[1040,128]{1,0:T(8,128)(2,1)S(1)} collective-permute-done((bf16[1040,128]{1,0:T(8,128)(2,1)S(1)}, bf16[1040,128]{1,0:T(8,128)(2,1)S(1)}, u32[]{:S(2)}, u32[]{:S(2)}) %collective-permute-start.1) | collective-permute-done | bytes 266272 | tf_op jit(solution)/shard_map/ppermute | solution.py:352
  140.6 18.3 %collective-permute-done.2.r2_ref = bf16[1040,128]{1,0:T(8,128)(2,1)S(1)} collective-permute-done((bf16[1040,128]{1,0:T(8,128)(2,1)S(1)}, bf16[1040,128]{1,0:T(8,128)(2,1)S(1)}, u32[]{:S(2)}, u32[]{:S(2)}) %collective-permute-start.2) | collective-permute-done | bytes 266272 | tf_op jit(solution)/shard_map/ppermute | solution.py:352
  159.0 1.0 norm_back.1
  160.1 37.6 %all_to_all.21.in_ref = bf16[32,144,128]{2,1,0:T(8,128)(2,1)S(1)} all-to-all(bf16[32,144,128]{2,1,0:T(8,128)(2,1)S(1)} %pad_maximum_fusion), channel_id=1, replica_groups=mesh['slab'=32,'head'=8] {'slab'}, dimensions={0} | all-to-all | bytes 2359296 | tf_op jit(solution)/shard_map/all_to_all | solution.py:383
  197.7 0.8 slab_sum.1
  198.5 0.7 copy.15
  (25 shorter events, 0.2 us)
Async XLA Ops:
  0.6 37.2 %copy-start = (bf16[1024,1024]{1,0:T(8,128)(2,1)S(1)}, bf16[1024,1024]{1,0:T(8,128)(2,1)}, u32[]{:S(2)}) copy-start(bf16[1024,1024]{1,0:T(8,128)(2,1)} %go_ref.3) | copy-start | bytes 6291460
  0.6 37.2 %copy-start.10 = (f32[1024]{0:T(1024)S(1)}, f32[1024]{0:T(1024)}, u32[]{:S(2)}) copy-start(f32[1024]{0:T(1024)} %param.9) | copy-start | bytes 12292
  1.6 0.7 copy-start.11
  2.3 0.7 copy-start.12
  3.0 0.7 copy-start.13
  37.8 1.6 copy-start.3
  43.0 1.3 copy-start.6
  44.3 0.8 copy-start.8
  45.1 10.1 %copy-start.14 = (f32[2]{0:T(128)S(1)}, f32[2]{0:T(128)}, u32[]{:S(2)}) copy-start(f32[2]{0:T(128)} %param.14) | copy-start | bytes 28
  45.1 26.4 %all-to-all-start.1 = ((bf16[32,4,32,128]{3,2,1,0:T(8,128)(2,1)}), bf16[32,4,32,128]{3,2,1,0:T(8,128)(2,1)}, u32[]{:S(2)}, u32[]{:S(2)}) async-start(bf16[32,4,32,128]{3,2,1,0:T(8,128)(2,1)} %get-tuple-element.25.in_ref.proj_ref), calls=%async_computation.1 | async-start | bytes 2097152 | tf_op jit(solution)/shard_map/all_to_all | solution.py:304
  76.9 1.0 copy-start.5
  77.8 30.1 %all-to-all-start.2 = ((bf16[32,4,32,128]{3,2,1,0:T(8,128)(2,1)}), bf16[32,4,32,128]{3,2,1,0:T(8,128)(2,1)}, u32[]{:S(2)}, u32[]{:S(2)}) async-start(bf16[32,4,32,128]{3,2,1,0:T(8,128)(2,1)} %copy-done.5), calls=%async_computation.2 | async-start | bytes 2097152 | tf_op jit(solution)/shard_map/all_to_all | solution.py:328
  103.0 1.3 copy-start.1
  107.9 1.6 copy-start.2
  109.5 1.6 copy-start.7
  111.1 47.9 %copy-start.9 = (f32[1024,128]{1,0:T(8,128)S(1)}, f32[1024,128]{1,0:T(8,128)}, u32[]{:S(2)}) copy-start(f32[1024,128]{1,0:T(8,128)} %copy-done.8) | copy-start | bytes 1572868
  118.1 40.8 %copy-start.4 = (bf16[1024,1024]{1,0:T(8,128)(2,1)S(1)}, bf16[1024,1024]{1,0:T(8,128)(2,1)}, u32[]{:S(2)}) copy-start(bf16[1024,1024]{1,0:T(8,128)(2,1)} %x_ref.3) | copy-start | bytes 6291460
  118.1 2.8 %collective-permute-start = (bf16[4112,128]{1,0:T(8,128)(2,1)S(1)}, bf16[4112,128]{1,0:T(8,128)(2,1)S(1)}, u32[]{:S(2)}, u32[]{:S(2)}) collective-permute-start(bf16[4112,128]{1,0:T(8,128)(2,1)S(1)} %get-tuple-element.27), channel_id=1, source_target_pairs={{0,1},{1,0},{2,3},{3,2},{4,5},{5,4},{6,7},{7,6},{8,9},{9,8},{10,11... | collective-permute-start | bytes 3158024 | tf_op jit(solution)/shard_map/ppermute | solution.py:343
  121.1 19.5 %collective-permute-start.1 = (bf16[1040,128]{1,0:T(8,128)(2,1)S(1)}, bf16[1040,128]{1,0:T(8,128)(2,1)S(1)}, u32[]{:S(2)}, u32[]{:S(2)}) collective-permute-start(bf16[1040,128]{1,0:T(8,128)(2,1)S(1)} %get-tuple-element.31), channel_id=1, source_target_pairs={{0,2},{1,3},{2,4},{3,5},{4,6},{5,7},{6,0},{7,1},{8,10},{9,11},{10,... | collective-permute-start | bytes 798728 | tf_op jit(solution)/shard_map/ppermute | solution.py:352
  123.0 36.0 %collective-permute-start.2 = (bf16[1040,128]{1,0:T(8,128)(2,1)S(1)}, bf16[1040,128]{1,0:T(8,128)(2,1)S(1)}, u32[]{:S(2)}, u32[]{:S(2)}) collective-permute-start(bf16[1040,128]{1,0:T(8,128)(2,1)S(1)} %get-tuple-element.32), channel_id=1, source_target_pairs={{0,4},{1,5},{2,6},{3,7},{4,0},{5,1},{6,2},{7,3},{8,12},{9,13},{10,... | collective-permute-start | bytes 798728 | tf_op jit(solution)/shard_map/ppermute | solution.py:352
  135.4 23.5 %collective-permute-start.3 = (bf16[1040,128]{1,0:T(8,128)(2,1)S(1)}, bf16[1040,128]{1,0:T(8,128)(2,1)S(1)}, u32[]{:S(2)}, u32[]{:S(2)}) collective-permute-start(bf16[1040,128]{1,0:T(8,128)(2,1)S(1)} %get-tuple-element.33), channel_id=1, source_target_pairs={{0,6},{1,7},{2,0},{3,1},{4,2},{5,3},{6,4},{7,5},{8,14},{9,15},{10,... | collective-permute-start | bytes 798728 | tf_op jit(solution)/shard_map/ppermute | solution.py:352

commit v2 on v1

v2 whole, which is shorter than its diff:
```python
import functools
import math

import jax
import jax.numpy as jnp
from jax import lax
from jax.experimental import pallas as pl
from jax.experimental.pallas import tpu as pltpu
from jax.sharding import PartitionSpec as P

BF = jnp.bfloat16
F32 = jnp.float32
SIDE = 32
LANES = 128
TOK = SIDE * SIDE
NEG = -1e30
VM = 20 << 20


def dot(a, b, ca, cb):
    return lax.dot_general(a, b, (((ca,), (cb,)), ((), ())), preferred_element_type=F32)


def call(body, outs, name, **kw):
    return pl.pallas_call(
        body,
        out_shape=outs,
        name=name,
        compiler_params=pltpu.CompilerParams(vmem_limit_bytes=VM),
        **kw,
    )


def shape(dims, kind):
    return jax.ShapeDtypeStruct(dims, kind)


def places(at_ref):
    head, slab = at_ref[0], at_ref[1]
    return head // 2, head % 2, slab // 8, (slab // 4) % 2, slab % 4


def rows_at(i, count):
    return pl.ds(pl.multiple_of(i * count, count), count)


def pack_body(q_ref, k_ref, v_ref, o_ref, out_ref, o_buf, part_buf, sems):
    copies = [
        pltpu.make_async_copy(src, part_buf.at[j], sems.at[j])
        for j, src in enumerate((q_ref, k_ref, v_ref))
    ] + [pltpu.make_async_copy(o_ref, o_buf, sems.at[3])]
    for c in copies:
        c.start()
    for c in copies:
        c.wait()
    for j in range(3):
        out_ref[:, j * LANES : (j + 1) * LANES] = part_buf[j]
    out_ref[:, 3 * LANES :] = o_buf[...].astype(F32).T.astype(BF)


def pair_up_body(at_ref, mine_ref, got_ref, one_ref, two_ref):
    _, _, _, zh, _ = places(at_ref)
    for place, ref in ((zh, mine_ref), (1 - zh, got_ref)):
        one_ref[rows_at(place, SIDE)] = ref[:, : 2 * LANES]
        two_ref[rows_at(place, SIDE)] = ref[:, 2 * LANES :]


def line_up_body(at_ref, *refs):
    _, _, x, _, y = places(at_ref)
    for n, place in enumerate((x, y)):
        for d in range(4):
            refs[8 + n][rows_at((place + 4 - d) % 4, 2 * SIDE)] = refs[4 * n + d][...]


def norm_stats_body(x_ref, gain_ref, normed_ref, inv_ref):
    x = x_ref[...].astype(F32)
    width = x.shape[1]
    inv = lax.rsqrt(jnp.sum(x * x, axis=1, keepdims=True) / width + 1e-06)
    normed_ref[...] = (x * inv * gain_ref[...]).astype(BF)
    inv_ref[...] = jnp.broadcast_to(inv, inv_ref.shape)


def project_body(at_ref, normed_ref, go_ref, *refs):
    pieces, out_ref, w_ref = refs[:8], refs[8], refs[9]
    _, _, x, _, y = places(at_ref)
    for d in range(4):
        far_y, far_x = (y + 4 - d) % 4, (x + 4 - d) % 4
        for near in range(4):
            for zh in range(2):
                rows = slice((near * 2 + zh) * SIDE, (near * 2 + zh + 1) * SIDE)
                at = rows_at(near * 8 + zh * 4 + far_y, SIDE)
                w_ref[at, : 2 * LANES] = pieces[d][rows]
                at = rows_at(far_x * 8 + zh * 4 + near, SIDE)
                w_ref[at, 2 * LANES :] = pieces[4 + d][rows]

    def step(i, _):
        at = rows_at(i, 256)
        three = dot(normed_ref[at], w_ref[:, : 3 * LANES], 1, 0)
        last = dot(go_ref[at], w_ref[:, 3 * LANES :], 1, 0)
        for j in range(4):
            part = three[:, j * LANES : (j + 1) * LANES] if j < 3 else last
            out_ref[pl.ds(8 * i, 8), j] = part.astype(BF).reshape(8, SIDE, LANES)
        return 0

    lax.fori_loop(0, 4, step, 0)


def first_head(rows):
    return lax.broadcasted_iota(jnp.int32, (rows, LANES), 1) < LANES // 2


def stacked(a):
    rows = a.shape[0]
    keep = first_head(rows)
    zero = jnp.zeros_like(a)
    return jnp.concatenate([jnp.where(keep, a, zero), jnp.where(keep, zero, a)], axis=0)


def folded(a):
    rows = a.shape[0] // 2
    return jnp.where(first_head(rows), a[:rows], a[rows:])


def attend(q, k, v, g, factors, bias):
    rows = q.shape[0]
    k2, v2 = stacked(k), stacked(v)
    s = dot(q, k2, 1, 1)
    dp = dot(g, v2, 1, 1)
    probs = []
    for h in range(2):
        sh = s[:, h * rows : (h + 1) * rows] * factors[h] + bias
        top = jnp.max(sh, axis=1, keepdims=True)
        e = jnp.exp(sh - top)
        probs.append(e / jnp.sum(e, axis=1, keepdims=True))
    pb = jnp.concatenate([p.astype(BF) for p in probs], axis=1)
    out = dot(pb, v2, 1, 0)
    go = g.astype(F32) * out
    keep = first_head(rows)
    grads = []
    for h in range(2):
        mine = jnp.where(keep, go, 0.0) if h == 0 else jnp.where(keep, 0.0, go)
        delta = jnp.sum(mine, axis=1, keepdims=True)
        dh = dp[:, h * rows : (h + 1) * rows]
        grads.append((probs[h] * (dh - delta) * factors[h]).astype(BF))
    ds = jnp.concatenate(grads, axis=1)
    gq = dot(ds, k2, 1, 0)
    gk = folded(dot(ds, q, 0, 0))
    gv = folded(dot(pb, g, 0, 0))
    return out, gq, gk, gv


def same_line(rows, line):
    a = line(lax.broadcasted_iota(jnp.int32, (rows, rows), 0))
    b = line(lax.broadcasted_iota(jnp.int32, (rows, rows), 1))
    return jnp.where(a == b, 0.0, NEG).astype(F32)


def strided_lines(in_ref, f_ref, wide_ref, bias_ref, add):
    for j in range(4):
        wide_ref[j] = in_ref[:, j].astype(F32).reshape(SIDE, 4, 8, LANES)
    rows = 8 * SIDE
    bias_ref[...] = same_line(rows, lambda i: i % 8)
    factors = (f_ref[0], f_ref[1])

    def step(b, _):
        parts = [wide_ref[j, :, b].reshape(rows, LANES).astype(BF) for j in range(4)]
        for j, r in enumerate(attend(*parts, factors, bias_ref[...])):
            add(j, b, r.reshape(SIDE, 8, LANES))
        return 0

    lax.fori_loop(0, 4, step, 0)


def plane_body(in_ref, f_ref, out_ref, wide_ref, bias_ref, bias_x_ref):
    rows = 4 * SIDE
    bias_x_ref[...] = same_line(rows, lambda i: i // SIDE)
    factors = (f_ref[0], f_ref[1])

    def step(b, _):
        parts = [in_ref[pl.ds(4 * b, 4), j].reshape(rows, LANES) for j in range(4)]
        for j, r in enumerate(attend(*parts, factors, bias_x_ref[...])):
            out_ref[j, pl.ds(4 * b, 4)] = r.reshape(4, 4, 8, LANES)
        return 0

    lax.fori_loop(0, 8, step, 0)

    def add(j, b, r):
        out_ref[j, :, b] += r

    strided_lines(in_ref, f_ref, wide_ref, bias_ref, add)


def depth_body(in_ref, f_ref, out_ref, wide_ref, res_ref, bias_ref):
    def add(j, b, r):
        res_ref[j, :, b] = r

    strided_lines(in_ref, f_ref, wide_ref, bias_ref, add)
    for j in range(4):
        out_ref[:, j] = res_ref[j].reshape(SIDE, SIDE, LANES).astype(BF)


def halves(a):
    high = a.astype(BF)
    return high, (a - high.astype(F32)).astype(BF)


def combine_body(
    at_ref, loc_ref, back_ref, proj_ref, normed_ref, gain_ref, w_ref,
    away_ref, keep_ref, small_ref, g_ref,
):
    _, core, _, _, _ = places(at_ref)
    total = jnp.zeros((TOK, LANES), F32)
    for j in range(4):
        part = loc_ref[j].reshape(TOK, LANES) + back_ref[:, j].astype(F32).reshape(TOK, LANES)
        part = part.astype(BF)
        at = (j - 1) % 4
        g_ref[:, at * LANES : (at + 1) * LANES] = part
        if j > 0:
            total += part.astype(F32) * proj_ref[:, j - 1].astype(F32).reshape(TOK, LANES)
    for i in range(8):
        row = jnp.sum(total[i * LANES : (i + 1) * LANES].T, axis=0, keepdims=True)
        small_ref[i : i + 1] = row

    def block(h):
        w = w_ref[rows_at(h, LANES), : 3 * LANES]
        part = dot(g_ref[:, : 3 * LANES], w, 1, 1).astype(BF)
        n = normed_ref[:, rows_at(h, LANES)].astype(F32)
        gain = jnp.sum(part.astype(F32) * n, axis=0, keepdims=True) / gain_ref[pl.ds(h, 1)]
        return part, gain

    def step(i, _):
        part, gain = block(2 * i + 1 - core)
        away_ref[rows_at(i, TOK)] = part
        small_ref[pl.ds(8 + i, 1)] = gain
        part, gain = block(2 * i + core)
        keep_ref[rows_at(i, TOK)] = part
        small_ref[pl.ds(12 + i, 1)] = gain
        return 0

    lax.fori_loop(0, 4, step, 0)
    high, low = halves(small_ref[...])
    away_ref[4 * TOK : 4 * TOK + 16] = high
    away_ref[4 * TOK + 16 :] = low


def pair_body(at_ref, got_ref, keep_ref, small_ref, *refs):
    sends, tinies, own_ref, both_ref, gown_ref, gain_buf = (
        refs[:3], refs[3:6], refs[6], refs[7], refs[8], refs[9]
    )
    zl = places(at_ref)[0]
    got = got_ref[4 * TOK : 4 * TOK + 16].astype(F32) + got_ref[4 * TOK + 16 :].astype(F32)
    dots = small_ref[:8] + got[:8]
    both_ref[...] = dots
    high, low = halves(dots)
    gain_buf[...] = jnp.concatenate([small_ref[12:16] + got[8:12]] * 2, axis=0)

    def block(i):
        return keep_ref[rows_at(i, TOK)].astype(F32) + got_ref[rows_at(i, TOK)].astype(F32)

    def gain(i):
        return jnp.broadcast_to(gain_buf[pl.ds(i, 1)], (8, LANES))

    for d, (ref, tiny) in enumerate(zip(sends, tinies)):
        to = (zl + d + 1) % 4
        ref[:TOK] = block(to).astype(BF)
        ref[TOK : TOK + 16] = jnp.concatenate([high, low], axis=0)
        tiny[...] = jnp.concatenate(halves(gain(to)), axis=0)
    own_ref[...] = block(zl)
    gown_ref[...] = gain(zl)


def tail_of(ref, at):
    return ref[at : at + 8].astype(F32) + ref[at + 8 : at + 16].astype(F32)


def weights_body(at_ref, normed_ref, go_ref, g_ref, gown_ref, *refs):
    tinies, along_x, along_y = refs[:3], refs[3:7], refs[7:11]
    gsum_ref, wg_ref = refs[11], refs[12]
    _, _, x, _, y = places(at_ref)
    gain = gown_ref[...]
    for ref in tinies:
        gain = gain + tail_of(ref, 0)
    gsum_ref[...] = gain
    tail = jnp.concatenate(halves(gain), axis=0)

    def step(i, _):
        at = rows_at(i, 256)
        three = dot(normed_ref[:, at], g_ref[:, : 3 * LANES], 0, 0)
        last = dot(go_ref[:, at], g_ref[:, 3 * LANES :], 0, 0)
        for j in range(4):
            part = three[:, j * LANES : (j + 1) * LANES] if j < 3 else last
            wg_ref[pl.ds(8 * i, 8), rows_at(j, SIDE)] = part.astype(BF).reshape(8, SIDE, LANES)
        return 0

    lax.fori_loop(0, 4, step, 0)
    for d in range(4):
        to = (x + d) % 4
        along_x[d][: 8 * 64] = wg_ref[pl.ds(8 * to, 8), :64].reshape(8 * 64, LANES)
        if d > 0:
            along_x[d][8 * 64 :] = tail
        to = (y + d) % 4
        for i in range(8):
            along_y[d][i * 64 : (i + 1) * 64] = wg_ref[4 * i + to, 64:]


def gather_sum(refs, rows):
    acc = refs[0][:rows].astype(F32)
    for ref in refs[1:]:
        acc = acc + ref[:rows].astype(F32)
    return acc


def second_body(at_ref, gsum_ref, *refs):
    xs, ys = refs[:4], refs[4:8]
    along_y, along_x, gout_ref, one, two = refs[8:12], refs[12:16], refs[16], refs[17], refs[18]
    _, _, x, _, y = places(at_ref)
    one[...] = gather_sum(xs, 512)
    two[...] = gather_sum(ys, 512)
    gain = gsum_ref[...]
    for ref in xs[1:]:
        gain = gain + tail_of(ref, 512)
    gout_ref[...] = gain
    tail = jnp.concatenate(halves(gain), axis=0)
    for d in range(4):
        kind = along_y[d].dtype
        for zh in range(2):
            along_y[d][zh * 64 : (zh + 1) * 64] = one[
                rows_at(4 * zh + (y + d) % 4, 64)
            ].astype(kind)
        if d > 0:
            along_y[d][128:] = tail
        along_x[d][...] = two[rows_at((x + d) % 4, 128)].astype(kind)


def third_body(at_ref, gsum_ref, *refs):
    ys, xs = refs[:4], refs[4:8]
    send_ref, own_ref, gout_ref, buf = refs[8:]
    _, _, _, zh, _ = places(at_ref)
    buf[:128] = gather_sum(ys, 128)
    buf[128:] = gather_sum(xs, 128)
    gain = gsum_ref[...]
    for ref in ys[1:]:
        gain = gain + tail_of(ref, 128)
    gout_ref[...] = gain
    for half in range(2):
        at = slice(half * 64, half * 64 + 64)
        send_ref[at] = buf[rows_at(2 * half + 1 - zh, 64)].astype(BF)
        own_ref[at] = buf[rows_at(2 * half + zh, 64)]
    send_ref[128:] = jnp.concatenate(halves(gain), axis=0)


def last_body(own_ref, got_ref, gain_ref, q_ref, k_ref, v_ref, o_ref, gout_ref, *, scale):
    acc = (own_ref[...] + got_ref[:128].astype(F32)) * scale
    for j, ref in enumerate((q_ref, k_ref, v_ref)):
        ref[...] = acc[j * SIDE : (j + 1) * SIDE]
    o_ref[...] = acc[3 * SIDE :].T
    gain = (gain_ref[...] + tail_of(got_ref, 128)) * scale
    gout_ref[...] = gain[:1]


def norm_body(at_ref, x_ref, gain_ref, own_ref, r1_ref, r2_ref, r3_ref, dots_ref, inv_ref, gx_ref):
    grad = own_ref[...]
    dots = dots_ref[...]
    for ref in (r1_ref, r2_ref, r3_ref):
        grad = grad + ref[:TOK].astype(F32)
        dots = dots + tail_of(ref, TOK)
    cols = [jnp.broadcast_to(dots[i : i + 1], (LANES, LANES)).T for i in range(8)]
    row_dot = jnp.concatenate(cols, axis=0)
    x = x_ref[...].astype(F32)
    inv = inv_ref[...]
    gx = inv * gain_ref[...] * grad - x * (inv * inv) * row_dot * (1.0 / 1024)
    gx_ref[...] = gx.astype(BF)


SMEM = pl.BlockSpec(memory_space=pltpu.SMEM)
VMEM = pl.BlockSpec(memory_space=pltpu.VMEM)


def along(slab_to):
    return [(s, slab_to(s)) for s in range(SIDE)]


def to_x(d):
    return along(lambda s: (s // 8 + d) % 4 * 8 + s % 8)


def to_y(d):
    return along(lambda s: s // 4 * 4 + (s + d) % 4)


def move(a, pairs, axis="slab"):
    return lax.ppermute(a, axis, pairs)


def moved(arrays, to):
    return [move(a, to(d + 1)) for d, a in enumerate(arrays)]


def body(
    inputs, norm_gain, query_weight, key_weight, value_weight, out_weight, logit_scale, grad_output
):
    rows, width = inputs.shape
    head_dim = 64
    at = jnp.stack([lax.axis_index("head"), lax.axis_index("slab")]).astype(jnp.int32)
    factors = logit_scale / math.sqrt(head_dim)
    over_z = along(lambda s: s ^ 4)

    mine = call(
        pack_body,
        shape((SIDE, 4 * LANES), BF),
        "pack",
        in_specs=[pl.BlockSpec(memory_space=pl.ANY)] * 4,
        scratch_shapes=[
            pltpu.VMEM((LANES, SIDE), BF),
            pltpu.VMEM((3, SIDE, LANES), BF),
            pltpu.SemaphoreType.DMA((4,)),
        ],
    )(query_weight, key_weight, value_weight, out_weight)
    half = shape((2 * SIDE, 2 * LANES), BF)
    one, two = call(pair_up_body, (half, half), "pair_up", in_specs=[SMEM, VMEM, VMEM])(
        at, mine, move(mine, over_z)
    )
    got = [one] + moved([one] * 3, to_x) + [two] + moved([two] * 3, to_y)
    half = shape((8 * SIDE, 2 * LANES), BF)
    one, two = call(line_up_body, (half, half), "line_up", in_specs=[SMEM] + [VMEM] * 8)(at, *got)
    pieces = [one] + moved([one] * 3, to_y) + [two] + moved([two] * 3, to_x)

    blk = 256
    normed, inv = call(
        norm_stats_body,
        (shape((rows, width), BF), shape((rows, LANES), F32)),
        "norm_stats",
        grid=(rows // blk,),
        in_specs=[
            pl.BlockSpec((blk, width), lambda i: (i, 0)),
            pl.BlockSpec((1, width), lambda i: (0, 0)),
        ],
        out_specs=(
            pl.BlockSpec((blk, width), lambda i: (i, 0)),
            pl.BlockSpec((blk, LANES), lambda i: (i, 0)),
        ),
    )(inputs, norm_gain.reshape(1, width))
    proj, weights = call(
        project_body,
        (shape((SIDE, 4, SIDE, LANES), BF), shape((width, 4 * LANES), BF)),
        "project",
        in_specs=[SMEM] + [VMEM] * 10,
    )(at, normed, grad_output, *pieces)

    z_in = lax.all_to_all(proj, "slab", 0, 0, tiled=True)
    big = (4, SIDE, 4, 8, LANES)
    local = call(
        plane_body,
        shape(big, F32),
        "plane",
        in_specs=[VMEM, SMEM],
        scratch_shapes=[
            pltpu.VMEM(big, F32),
            pltpu.VMEM((256, 256), F32),
            pltpu.VMEM((128, 128), F32),
        ],
    )(proj, factors)
    z_terms = call(
        depth_body,
        shape((SIDE, 4, SIDE, LANES), BF),
        "depth",
        in_specs=[VMEM, SMEM],
        scratch_shapes=[
            pltpu.VMEM(big, F32),
            pltpu.VMEM(big, F32),
            pltpu.VMEM((256, 256), F32),
        ],
    )(z_in, factors)
    back = lax.all_to_all(z_terms, "slab", 0, 0, tiled=True)

    away, keep, small, grads = call(
        combine_body,
        (
            shape((4 * TOK + 32, LANES), BF),
            shape((4 * TOK, LANES), BF),
            shape((16, LANES), F32),
            shape((TOK, 4 * LANES), BF),
        ),
        "combine",
        in_specs=[SMEM] + [VMEM] * 6,
    )(at, local, back, proj, normed, norm_gain.reshape(8, LANES), weights)

    got = move(away, [(i, i ^ 1) for i in range(8)], "head")
    piece, tiny, row8 = (
        shape((TOK + 16, LANES), BF),
        shape((16, LANES), BF),
        shape((8, LANES), F32),
    )
    *sends, own, dots, gown = call(
        pair_body,
        (piece,) * 3 + (tiny,) * 3 + (shape((TOK, LANES), F32), row8, row8),
        "pair",
        in_specs=[SMEM] + [VMEM] * 3,
        scratch_shapes=[pltpu.VMEM((8, LANES), F32)],
    )(at, got, keep, small)
    to_zl = lambda d: [(i, (i + 2 * d) % 8) for i in range(8)]
    tinies = [move(s, to_zl(d + 1), "head") for d, s in enumerate(sends[3:])]
    parts = [move(s, to_zl(d + 1), "head") for d, s in enumerate(sends[:3])]

    first = shape((528, LANES), BF)
    plain = shape((512, LANES), BF)
    *sends, gsum = call(
        weights_body,
        (plain,) + (first,) * 3 + (plain,) * 4 + (row8,),
        "weight_grads",
        in_specs=[SMEM] + [VMEM] * 7,
        scratch_shapes=[pltpu.VMEM((SIDE, LANES, LANES), BF)],
    )(at, normed, grad_output, grads, gown, *tinies)
    got = [sends[0]] + moved(sends[1:4], to_x) + [sends[4]] + moved(sends[5:8], to_y)
    sq = shape((LANES, LANES), BF)
    sqf = shape((LANES, LANES), F32)
    tall = shape((LANES + 16, LANES), BF)
    *sends, gsum = call(
        second_body,
        (sqf,) + (tall,) * 3 + (sqf,) + (sq,) * 3 + (row8,),
        "slab_second",
        in_specs=[SMEM] + [VMEM] * 9,
        scratch_shapes=[pltpu.VMEM((512, LANES), F32)] * 2,
    )(at, gsum, *got)
    got = [sends[0]] + moved(sends[1:4], to_y) + [sends[4]] + moved(sends[5:8], to_x)
    send, mine, gsum = call(
        third_body,
        (tall, sqf, row8),
        "slab_third",
        in_specs=[SMEM] + [VMEM] * 9,
        scratch_shapes=[pltpu.VMEM((256, LANES), F32)],
    )(at, gsum, *got)
    part = shape((SIDE, LANES), F32)
    gqw, gkw, gvw, gow, ggain = call(
        functools.partial(last_body, scale=1.0 / math.sqrt(rows * SIDE)),
        (part, part, part, shape((LANES, SIDE), F32), shape((1, LANES), F32)),
        "slab_last",
    )(mine, move(send, over_z), gsum)

    whole = lambda dims: pl.BlockSpec(dims, lambda i, h: (0,) * len(dims))
    grad_inputs = pl.pallas_call(
        norm_body,
        out_shape=shape((rows, LANES), BF),
        name="norm_back",
        grid_spec=pltpu.PrefetchScalarGridSpec(
            num_scalar_prefetch=1,
            grid=(1,),
            in_specs=[
                pl.BlockSpec((rows, LANES), lambda i, h: (0, h[0])),
                pl.BlockSpec((1, LANES), lambda i, h: (0, h[0])),
                whole((TOK, LANES)),
                whole((TOK + 16, LANES)),
                whole((TOK + 16, LANES)),
                whole((TOK + 16, LANES)),
                whole((8, LANES)),
                whole((TOK, LANES)),
            ],
            out_specs=whole((rows, LANES)),
        ),
        compiler_params=pltpu.CompilerParams(vmem_limit_bytes=VM),
    )(at, inputs, norm_gain.reshape(1, width), own, *parts, dots, inv)
    return grad_inputs, ggain.reshape(LANES), gqw, gkw, gvw, gow


def solution(mesh):
    in_specs = (
        P("slab", None),
        P(),
        P("slab", "head"),
        P("slab", "head"),
        P("slab", "head"),
        P("head", "slab"),
        P("head"),
        P("slab", None),
    )
    out_specs = (
        P("slab", "head"),
        P("head"),
        P("slab", "head"),
        P("slab", "head"),
        P("slab", "head"),
        P("head", "slab"),
    )
    return jax.shard_map(body, mesh=mesh, in_specs=in_specs, out_specs=out_specs, check_vma=False)
```

time: 200 us -> 186 us (0.930); the launches traced: 199 us -> 182 us
  blocking collectives: 71.6 us -> 0 us
  starting transfers between devices: 39.4 us -> 76.6 us
  waiting for transfers between devices: 44.9 us -> 52.8 us
  Pallas kernels: 29.5 us -> 34.5 us
  local copies, waits for them, and re-layouts: 12.9 us -> 17.7 us
    all_to_all x2 -> x0, blocking collectives: 71.6 us -> none  [the longest x1 37.6 us: body(): pieces = lax.all_to_all(sent, 'slab', 0, 0, tiled=True)]
    ppermute x4 -> x33, starting transfers between devices: 15.5 us -> 57.1 us  [move(): return lax.ppermute(a, axis, pairs)]
    pallas_call x6 -> x12, Pallas kernels: 12.8 us -> 18.5 us  [the longest x1 4.11 us: body(): call(combine_body, (shape((4 * TOK + 32, LANES), BF), shape((4 * TOK, LAN...]
    ppermute x4 -> x33, waiting for transfers between devices: 25 us -> 30.2 us  [move(): return lax.ppermute(a, axis, pairs)]
    unnamed x32 -> x44, local copies, waits for them, and re-layouts: 12.9 us -> 17.7 us
    all_to_all x1, starting transfers between devices: 13.8 us -> 9.74 us  [body(): back = lax.all_to_all(z_terms, 'slab', 0, 0, tiled=True)]
  transfers between devices with their start and end apart: 6 -> 35, of which waited for: 5 -> 18; matrix products, arithmetic and copies ran while one was open for 0% -> 0% of each run, Pallas kernels for 6% -> 8%
where the time goes in v2:
time: 186 us; the launch traced here: 182 us
  starting transfers between devices  76.6 us (41%)
  waiting for transfers between devices  52.8 us (28%)
  Pallas kernels  34.5 us (19%)
  local copies, waits for them, and re-layouts  17.7 us (10%)
    ppermute x33, starting transfers between devices, move(): return lax.ppermute(a, axis, pairs)  57.1 us
    ppermute x33, waiting for transfers between devices, move(): return lax.ppermute(a, axis, pairs)  30.2 us
    all_to_all x1, waiting for transfers between devices, body(): z_in = lax.all_to_all(proj, 'slab', 0, 0, tiled=True)  17.8 us
    unnamed x44, local copies, waits for them, and re-layouts  17.7 us
    pallas_call x1, Pallas kernels, body(): call(plane_body, shape(big, F32), 'plane', in_specs=[VMEM, SMEM], scratch...  11.3 us
    all_to_all x1, starting transfers between devices, body(): z_in = lax.all_to_all(proj, 'slab', 0, 0, tiled=True)  9.74 us
    all_to_all x1, starting transfers between devices, body(): back = lax.all_to_all(z_terms, 'slab', 0, 0, tiled=True)  9.74 us
    all_to_all x1, waiting for transfers between devices, body(): back = lax.all_to_all(z_terms, 'slab', 0, 0, tiled=True)  4.76 us
  transfers between devices with their start and end apart: 35, of which 18 were waited for; matrix products, arithmetic and copies ran while one was open for 0% of the time, Pallas kernels for 8%

profile of v2, /device:TPU:96, one launch (start us, length us, event | category | flops | bytes accessed | tf_op | source)
XLA Modules:
  0.0 182.5 jit_solution(2134299903971322174)
XLA Ops:
  3.7 4.6 %collective-permute-start = (bf16[32,512]{1,0:T(8,128)(2,1)S(1)}, bf16[32,512]{1,0:T(8,128)(2,1)S(1)}, u32[]{:S(2)}, u32[]{:S(2)}) collective-permute-start(bf16[32,512]{1,0:T(8,128)(2,1)S(1)} %pack.1.mine_ref), channel_id=1, source_target_pairs={{0,32},{8,40},{16,48},{24,56},{32,0},{40,8},{48,16},{56,24},{64,96... | collective-permute-start | bytes 98312 | tf_op jit(solution)/shard_map/ppermute | solution.py:392
  8.4 3.3 %collective-permute-done.got_ref = bf16[32,512]{1,0:T(8,128)(2,1)S(1)} collective-permute-done((bf16[32,512]{1,0:T(8,128)(2,1)S(1)}, bf16[32,512]{1,0:T(8,128)(2,1)S(1)}, u32[]{:S(2)}, u32[]{:S(2)}) %collective-permute-start) | collective-permute-done | bytes 32800 | tf_op jit(solution)/shard_map/ppermute | solution.py:392
  12.2 2.8 %collective-permute-start.3 = (bf16[64,256]{1,0:T(8,128)(2,1)S(1)}, bf16[64,256]{1,0:T(8,128)(2,1)S(1)}, u32[]{:S(2)}, u32[]{:S(2)}) collective-permute-start(bf16[64,256]{1,0:T(8,128)(2,1)S(1)} %get-tuple-element.54.refs_0_), channel_id=1, source_target_pairs={{0,192},{8,200},{16,208},{24,216},{32,224},{40,232},{48,240},{56,2... | collective-permute-start | bytes 98312 | tf_op jit(solution)/shard_map/ppermute | solution.py:392
  16.7 3.0 %collective-permute-start.6 = (bf16[64,256]{1,0:T(8,128)(2,1)S(1)}, bf16[64,256]{1,0:T(8,128)(2,1)S(1)}, u32[]{:S(2)}, u32[]{:S(2)}) collective-permute-start(bf16[64,256]{1,0:T(8,128)(2,1)S(1)} %get-tuple-element.55.refs_4_), channel_id=1, source_target_pairs={{0,24},{8,0},{16,8},{24,16},{32,56},{40,32},{48,40},{56,48},{64,88... | collective-permute-start | bytes 98312 | tf_op jit(solution)/shard_map/ppermute | solution.py:392
  21.3 3.8 %collective-permute-done.5.refs_6_ = bf16[64,256]{1,0:T(8,128)(2,1)S(1)} collective-permute-done((bf16[64,256]{1,0:T(8,128)(2,1)S(1)}, bf16[64,256]{1,0:T(8,128)(2,1)S(1)}, u32[]{:S(2)}, u32[]{:S(2)}) %collective-permute-start.5) | collective-permute-done | bytes 32800 | tf_op jit(solution)/shard_map/ppermute | solution.py:392
  29.3 2.4 %collective-permute-start.12 = (bf16[256,256]{1,0:T(8,128)(2,1)S(1)}, bf16[256,256]{1,0:T(8,128)(2,1)S(1)}, u32[]{:S(2)}, u32[]{:S(2)}) collective-permute-start(bf16[256,256]{1,0:T(8,128)(2,1)S(1)} %get-tuple-element.57.refs_4_), channel_id=1, source_target_pairs={{0,192},{8,200},{16,208},{24,216},{32,224},{40,232},{48,240},{56,2... | collective-permute-start | bytes 393224 | tf_op jit(solution)/shard_map/ppermute | solution.py:392
  39.5 3.9 %project.1 = (bf16[32,4,32,128]{3,2,1,0:T(8,128)(2,1)}, bf16[1024,512]{1,0:T(8,128)(2,1)S(1)}) custom-call(s32[2]{0:T(128)S(1)} %pad_add_fusion.at_ref, bf16[1024,1024]{1,0:T(8,128)(2,1)S(1)} %get-tuple-element.53.normed_ref, bf16[1024,1024]{1,0:T(8,128)(2,1)S(1)} %copy-done.4, bf16[256,256]{1,0:T(8,128)(2,1)S(1)} %get-tuple-element.56.refs_0_, ...), custom_call_target="tpu_custom_call" | custom-call | tf_op jit(solution)/shard_map/project/pallas_call | solution.py:443
  44.4 9.7 %all-to-all-start = ((bf16[32,4,32,128]{3,2,1,0:T(8,128)(2,1)}), bf16[32,4,32,128]{3,2,1,0:T(8,128)(2,1)S(1)}, u32[]{:S(2)}, u32[]{:S(2)}) async-start(bf16[32,4,32,128]{3,2,1,0:T(8,128)(2,1)} %get-tuple-element.58.in_ref.proj_ref), calls=%async_computation | async-start | bytes 2097152 | tf_op jit(solution)/shard_map/all_to_all | solution.py:450
  54.2 17.8 %all-to-all-done.in_ref = bf16[32,4,32,128]{3,2,1,0:T(8,128)(2,1)S(1)} async-done(((bf16[32,4,32,128]{3,2,1,0:T(8,128)(2,1)}), bf16[32,4,32,128]{3,2,1,0:T(8,128)(2,1)S(1)}, u32[]{:S(2)}, u32[]{:S(2)}) %all-to-all-start) | async-done | bytes 1048608 | tf_op jit(solution)/shard_map/all_to_all | solution.py:450
  72.0 4.7 %depth.1 = bf16[32,4,32,128]{3,2,1,0:T(8,128)(2,1)S(1)} custom-call(bf16[32,4,32,128]{3,2,1,0:T(8,128)(2,1)S(1)} %all-to-all-done.in_ref, f32[2]{0:T(128)S(1)} %broadcast_multiply_fusion.f_ref), custom_call_target="tpu_custom_call" | custom-call | tf_op jit(solution)/shard_map/depth/pallas_call | solution.py:463
  77.7 9.7 %all-to-all-start.1 = ((bf16[32,4,32,128]{3,2,1,0:T(8,128)(2,1)}), bf16[32,4,32,128]{3,2,1,0:T(8,128)(2,1)S(1)}, u32[]{:S(2)}, u32[]{:S(2)}) async-start(bf16[32,4,32,128]{3,2,1,0:T(8,128)(2,1)} %copy-done.6), calls=%async_computation.1 | async-start | bytes 2097152 | tf_op jit(solution)/shard_map/all_to_all | solution.py:474
  87.5 11.3 %plane.1.loc_ref = f32[4,32,4,8,128]{4,3,2,1,0:T(8,128)S(1)} custom-call(bf16[32,4,32,128]{3,2,1,0:T(8,128)(2,1)} %get-tuple-element.58.in_ref.proj_ref, f32[2]{0:T(128)S(1)} %broadcast_multiply_fusion.f_ref), custom_call_target="tpu_custom_call" | custom-call | tf_op jit(solution)/shard_map/plane/pallas_call | solution.py:452
  100.1 4.8 %all-to-all-done.1.back_ref = bf16[32,4,32,128]{3,2,1,0:T(8,128)(2,1)S(1)} async-done(((bf16[32,4,32,128]{3,2,1,0:T(8,128)(2,1)}), bf16[32,4,32,128]{3,2,1,0:T(8,128)(2,1)S(1)}, u32[]{:S(2)}, u32[]{:S(2)}) %all-to-all-start.1) | async-done | bytes 1048608 | tf_op jit(solution)/shard_map/all_to_all | solution.py:474
  107.7 4.1 %combine.1 = (bf16[4128,128]{1,0:T(8,128)(2,1)S(1)}, bf16[4096,128]{1,0:T(8,128)(2,1)S(1)}, f32[16,128]{1,0:T(8,128)S(1)}, bf16[1024,512]{1,0:T(8,128)(2,1)S(1)}) custom-call(s32[2]{0:T(128)S(1)} %pad_add_fusion.at_ref, f32[4,32,4,8,128]{4,3,2,1,0:T(8,128)S(1)} %copy-done.1, bf16[32,4,32,128]{3,2,1,0:T(8,128)(2,1)S(1)} %all-to-all-done.1.back_ref, ...), custom_call_target="tpu_custom_call" | custom-call | tf_op jit(solution)/shard_map/combine/pallas_call | solution.py:476
  111.9 2.7 %collective-permute-done.13.got_ref = bf16[4128,128]{1,0:T(8,128)(2,1)S(1)} collective-permute-done((bf16[4128,128]{1,0:T(8,128)(2,1)S(1)}, bf16[4128,128]{1,0:T(8,128)(2,1)S(1)}, u32[]{:S(2)}, u32[]{:S(2)}) %collective-permute-start.13) | collective-permute-done | bytes 1056800 | tf_op jit(solution)/shard_map/ppermute | solution.py:392
  114.6 1.6 pair.1
  116.2 10.0 %collective-permute-start.17 = (bf16[16,128]{1,0:T(8,128)(2,1)S(1)}, bf16[16,128]{1,0:T(8,128)(2,1)S(1)}, u32[]{:S(2)}, u32[]{:S(2)}) collective-permute-start(bf16[16,128]{1,0:T(8,128)(2,1)S(1)} %get-tuple-element.71), channel_id=1, source_target_pairs={{0,2},{1,3},{2,4},{3,5},{4,6},{5,7},{6,0},{7,1},{8,10},{9,11},{10,... | collective-permute-start | bytes 12296 | tf_op jit(solution)/shard_map/ppermute | solution.py:392
  127.1 2.0 %collective-permute-start.19 = (bf16[16,128]{1,0:T(8,128)(2,1)S(1)}, bf16[16,128]{1,0:T(8,128)(2,1)S(1)}, u32[]{:S(2)}, u32[]{:S(2)}) collective-permute-start(bf16[16,128]{1,0:T(8,128)(2,1)S(1)} %get-tuple-element.73), channel_id=1, source_target_pairs={{0,6},{1,7},{2,0},{3,1},{4,2},{5,3},{6,4},{7,5},{8,14},{9,15},{10,... | collective-permute-start | bytes 12296 | tf_op jit(solution)/shard_map/ppermute | solution.py:392
  129.1 1.6 collective-permute-done.18.refs_1_
  130.7 1.8 collective-permute-done.19.refs_2_
  132.5 3.2 %weight_grads.1 = (bf16[512,128]{1,0:T(8,128)(2,1)S(1)}, bf16[528,128]{1,0:T(8,128)(2,1)S(1)}, bf16[528,128]{1,0:T(8,128)(2,1)S(1)}, bf16[528,128]{1,0:T(8,128)(...) custom-call(s32[2]{0:T(128)S(1)} %pad_add_fusion.at_ref, ...), custom_call_target="tpu_custom_call" | custom-call | tf_op jit(solution)/shard_map/weight_grads/pallas_call | solution.py:507
  135.7 1.7 collective-permute-start.23
  137.8 1.6 collective-permute-start.24
  139.4 1.7 collective-permute-start.25
  141.1 2.3 %collective-permute-start.21 = (bf16[528,128]{1,0:T(8,128)(2,1)S(1)}, bf16[528,128]{1,0:T(8,128)(2,1)S(1)}, u32[]{:S(2)}, u32[]{:S(2)}) collective-permute-start(bf16[528,128]{1,0:T(8,128)(2,1)S(1)} %get-tuple-element.77), channel_id=1, source_target_pairs={{0,128},{8,136},{16,144},{24,152},{32,160},{40,168},{48,176},{56,1... | collective-permute-start | bytes 405512 | tf_op jit(solution)/shard_map/ppermute | solution.py:392
  147.6 2.0 %collective-permute-done.22.refs_3_ = bf16[528,128]{1,0:T(8,128)(2,1)S(1)} collective-permute-done((bf16[528,128]{1,0:T(8,128)(2,1)S(1)}, bf16[528,128]{1,0:T(8,128)(2,1)S(1)}, u32[]{:S(2)}, u32[]{:S(2)}) %collective-permute-start.22) | collective-permute-done | bytes 135200 | tf_op jit(solution)/shard_map/ppermute | solution.py:392
  151.0 3.6 %collective-permute-start.30 = (bf16[128,128]{1,0:T(8,128)(2,1)S(1)}, bf16[128,128]{1,0:T(8,128)(2,1)S(1)}, u32[]{:S(2)}, u32[]{:S(2)}) collective-permute-start(bf16[128,128]{1,0:T(8,128)(2,1)S(1)} %get-tuple-element.90), channel_id=1, source_target_pairs={{0,128},{8,136},{16,144},{24,152},{32,160},{40,168},{48,176},{56,1... | collective-permute-start | bytes 98312 | tf_op jit(solution)/shard_map/ppermute | solution.py:392
  156.8 2.3 %collective-permute-start.31 = (bf16[128,128]{1,0:T(8,128)(2,1)S(1)}, bf16[128,128]{1,0:T(8,128)(2,1)S(1)}, u32[]{:S(2)}, u32[]{:S(2)}) collective-permute-start(bf16[128,128]{1,0:T(8,128)(2,1)S(1)} %get-tuple-element.91), channel_id=1, source_target_pairs={{0,192},{8,200},{16,208},{24,216},{32,224},{40,232},{48,240},{56,2... | collective-permute-start | bytes 98312 | tf_op jit(solution)/shard_map/ppermute | solution.py:392
  159.1 1.6 collective-permute-done.31.refs_7_
  163.2 3.0 %collective-permute-done.27.refs_2_ = bf16[144,128]{1,0:T(8,128)(2,1)S(1)} collective-permute-done((bf16[144,128]{1,0:T(8,128)(2,1)S(1)}, bf16[144,128]{1,0:T(8,128)(2,1)S(1)}, u32[]{:S(2)}, u32[]{:S(2)}) %collective-permute-start.27) | collective-permute-done | bytes 36896 | tf_op jit(solution)/shard_map/ppermute | solution.py:392
  166.8 3.9 %collective-permute-start.32 = (bf16[144,128]{1,0:T(8,128)(2,1)S(1)}, bf16[144,128]{1,0:T(8,128)(2,1)S(1)}, u32[]{:S(2)}, u32[]{:S(2)}) collective-permute-start(bf16[144,128]{1,0:T(8,128)(2,1)S(1)} %get-tuple-element.93), channel_id=1, source_target_pairs={{0,32},{8,40},{16,48},{24,56},{32,0},{40,8},{48,16},{56,24},{64,96... | collective-permute-start | bytes 110600 | tf_op jit(solution)/shard_map/ppermute | solution.py:392
  170.7 4.0 %collective-permute-done.32.got_ref = bf16[144,128]{1,0:T(8,128)(2,1)S(1)} collective-permute-done((bf16[144,128]{1,0:T(8,128)(2,1)S(1)}, bf16[144,128]{1,0:T(8,128)(2,1)S(1)}, u32[]{:S(2)}, u32[]{:S(2)}) %collective-permute-start.32) | collective-permute-done | bytes 36896 | tf_op jit(solution)/shard_map/ppermute | solution.py:392
  (98 shorter events, 45.1 us)
Async XLA Ops:
  3.7 7.9 %collective-permute-start = (bf16[32,512]{1,0:T(8,128)(2,1)S(1)}, bf16[32,512]{1,0:T(8,128)(2,1)S(1)}, u32[]{:S(2)}, u32[]{:S(2)}) collective-permute-start(bf16[32,512]{1,0:T(8,128)(2,1)S(1)} %pack.1.mine_ref), channel_id=1, source_target_pairs={{0,32},{8,40},{16,48},{24,56},{32,0},{40,8},{48,16},{56,24},{64,96... | collective-permute-start | bytes 98312 | tf_op jit(solution)/shard_map/ppermute | solution.py:392
  12.2 8.2 %collective-permute-start.3 = (bf16[64,256]{1,0:T(8,128)(2,1)S(1)}, bf16[64,256]{1,0:T(8,128)(2,1)S(1)}, u32[]{:S(2)}, u32[]{:S(2)}) collective-permute-start(bf16[64,256]{1,0:T(8,128)(2,1)S(1)} %get-tuple-element.54.refs_0_), channel_id=1, source_target_pairs={{0,192},{8,200},{16,208},{24,216},{32,224},{40,232},{48,240},{56,2... | collective-permute-start | bytes 98312 | tf_op jit(solution)/shard_map/ppermute | solution.py:392
  15.0 6.3 %collective-permute-start.2 = (bf16[64,256]{1,0:T(8,128)(2,1)S(1)}, bf16[64,256]{1,0:T(8,128)(2,1)S(1)}, u32[]{:S(2)}, u32[]{:S(2)}) collective-permute-start(bf16[64,256]{1,0:T(8,128)(2,1)S(1)} %get-tuple-element.54.refs_0_), channel_id=1, source_target_pairs={{0,128},{8,136},{16,144},{24,152},{32,160},{40,168},{48,176},{56,1... | collective-permute-start | bytes 98312 | tf_op jit(solution)/shard_map/ppermute | solution.py:392
  15.8 5.5 %collective-permute-start.1 = (bf16[64,256]{1,0:T(8,128)(2,1)S(1)}, bf16[64,256]{1,0:T(8,128)(2,1)S(1)}, u32[]{:S(2)}, u32[]{:S(2)}) collective-permute-start(bf16[64,256]{1,0:T(8,128)(2,1)S(1)} %get-tuple-element.54.refs_0_), channel_id=1, source_target_pairs={{0,64},{8,72},{16,80},{24,88},{32,96},{40,104},{48,112},{56,120},{... | collective-permute-start | bytes 98312 | tf_op jit(solution)/shard_map/ppermute | solution.py:392
  16.7 4.6 %collective-permute-start.6 = (bf16[64,256]{1,0:T(8,128)(2,1)S(1)}, bf16[64,256]{1,0:T(8,128)(2,1)S(1)}, u32[]{:S(2)}, u32[]{:S(2)}) collective-permute-start(bf16[64,256]{1,0:T(8,128)(2,1)S(1)} %get-tuple-element.55.refs_4_), channel_id=1, source_target_pairs={{0,24},{8,0},{16,8},{24,16},{32,56},{40,32},{48,40},{56,48},{64,88... | collective-permute-start | bytes 98312 | tf_op jit(solution)/shard_map/ppermute | solution.py:392
  19.7 5.4 %collective-permute-start.5 = (bf16[64,256]{1,0:T(8,128)(2,1)S(1)}, bf16[64,256]{1,0:T(8,128)(2,1)S(1)}, u32[]{:S(2)}, u32[]{:S(2)}) collective-permute-start(bf16[64,256]{1,0:T(8,128)(2,1)S(1)} %get-tuple-element.55.refs_4_), channel_id=1, source_target_pairs={{0,16},{8,24},{16,0},{24,8},{32,48},{40,56},{48,32},{56,40},{64,80... | collective-permute-start | bytes 98312 | tf_op jit(solution)/shard_map/ppermute | solution.py:392
  20.4 5.1 %collective-permute-start.4 = (bf16[64,256]{1,0:T(8,128)(2,1)S(1)}, bf16[64,256]{1,0:T(8,128)(2,1)S(1)}, u32[]{:S(2)}, u32[]{:S(2)}) collective-permute-start(bf16[64,256]{1,0:T(8,128)(2,1)S(1)} %get-tuple-element.55.refs_4_), channel_id=1, source_target_pairs={{0,8},{8,16},{16,24},{24,0},{32,40},{40,48},{48,56},{56,32},{64,72... | collective-permute-start | bytes 98312 | tf_op jit(solution)/shard_map/ppermute | solution.py:392
  26.1 7.1 %collective-permute-start.9 = (bf16[256,256]{1,0:T(8,128)(2,1)S(1)}, bf16[256,256]{1,0:T(8,128)(2,1)S(1)}, u32[]{:S(2)}, u32[]{:S(2)}) collective-permute-start(bf16[256,256]{1,0:T(8,128)(2,1)S(1)} %get-tuple-element.56.refs_0_), channel_id=1, source_target_pairs={{0,24},{8,0},{16,8},{24,16},{32,56},{40,32},{48,40},{56,48},{64,88... | collective-permute-start | bytes 393224 | tf_op jit(solution)/shard_map/ppermute | solution.py:392
  26.7 10.4 %collective-permute-start.8 = (bf16[256,256]{1,0:T(8,128)(2,1)S(1)}, bf16[256,256]{1,0:T(8,128)(2,1)S(1)}, u32[]{:S(2)}, u32[]{:S(2)}) collective-permute-start(bf16[256,256]{1,0:T(8,128)(2,1)S(1)} %get-tuple-element.56.refs_0_), channel_id=1, source_target_pairs={{0,16},{8,24},{16,0},{24,8},{32,48},{40,56},{48,32},{56,40},{64,80... | collective-permute-start | bytes 393224 | tf_op jit(solution)/shard_map/ppermute | solution.py:392
  28.0 9.1 %collective-permute-start.7 = (bf16[256,256]{1,0:T(8,128)(2,1)S(1)}, bf16[256,256]{1,0:T(8,128)(2,1)S(1)}, u32[]{:S(2)}, u32[]{:S(2)}) collective-permute-start(bf16[256,256]{1,0:T(8,128)(2,1)S(1)} %get-tuple-element.56.refs_0_), channel_id=1, source_target_pairs={{0,8},{8,16},{16,24},{24,0},{32,40},{40,48},{48,56},{56,32},{64,72... | collective-permute-start | bytes 393224 | tf_op jit(solution)/shard_map/ppermute | solution.py:392
  29.3 7.9 %collective-permute-start.12 = (bf16[256,256]{1,0:T(8,128)(2,1)S(1)}, bf16[256,256]{1,0:T(8,128)(2,1)S(1)}, u32[]{:S(2)}, u32[]{:S(2)}) collective-permute-start(bf16[256,256]{1,0:T(8,128)(2,1)S(1)} %get-tuple-element.57.refs_4_), channel_id=1, source_target_pairs={{0,192},{8,200},{16,208},{24,216},{32,224},{40,232},{48,240},{56,2... | collective-permute-start | bytes 393224 | tf_op jit(solution)/shard_map/ppermute | solution.py:392
  31.6 6.5 %collective-permute-start.11 = (bf16[256,256]{1,0:T(8,128)(2,1)S(1)}, bf16[256,256]{1,0:T(8,128)(2,1)S(1)}, u32[]{:S(2)}, u32[]{:S(2)}) collective-permute-start(bf16[256,256]{1,0:T(8,128)(2,1)S(1)} %get-tuple-element.57.refs_4_), channel_id=1, source_target_pairs={{0,128},{8,136},{16,144},{24,152},{32,160},{40,168},{48,176},{56,1... | collective-permute-start | bytes 393224 | tf_op jit(solution)/shard_map/ppermute | solution.py:392
  33.1 6.4 %collective-permute-start.10 = (bf16[256,256]{1,0:T(8,128)(2,1)S(1)}, bf16[256,256]{1,0:T(8,128)(2,1)S(1)}, u32[]{:S(2)}, u32[]{:S(2)}) collective-permute-start(bf16[256,256]{1,0:T(8,128)(2,1)S(1)} %get-tuple-element.57.refs_4_), channel_id=1, source_target_pairs={{0,64},{8,72},{16,80},{24,88},{32,96},{40,104},{48,112},{56,120},{... | collective-permute-start | bytes 393224 | tf_op jit(solution)/shard_map/ppermute | solution.py:392
  44.4 27.6 %all-to-all-start = ((bf16[32,4,32,128]{3,2,1,0:T(8,128)(2,1)}), bf16[32,4,32,128]{3,2,1,0:T(8,128)(2,1)S(1)}, u32[]{:S(2)}, u32[]{:S(2)}) async-start(bf16[32,4,32,128]{3,2,1,0:T(8,128)(2,1)} %get-tuple-element.58.in_ref.proj_ref), calls=%async_computation | async-start | bytes 2097152 | tf_op jit(solution)/shard_map/all_to_all | solution.py:450
  77.7 27.2 %all-to-all-start.1 = ((bf16[32,4,32,128]{3,2,1,0:T(8,128)(2,1)}), bf16[32,4,32,128]{3,2,1,0:T(8,128)(2,1)S(1)}, u32[]{:S(2)}, u32[]{:S(2)}) async-start(bf16[32,4,32,128]{3,2,1,0:T(8,128)(2,1)} %copy-done.6), calls=%async_computation.1 | async-start | bytes 2097152 | tf_op jit(solution)/shard_map/all_to_all | solution.py:474
  116.2 12.9 %collective-permute-start.17 = (bf16[16,128]{1,0:T(8,128)(2,1)S(1)}, bf16[16,128]{1,0:T(8,128)(2,1)S(1)}, u32[]{:S(2)}, u32[]{:S(2)}) collective-permute-start(bf16[16,128]{1,0:T(8,128)(2,1)S(1)} %get-tuple-element.71), channel_id=1, source_target_pairs={{0,2},{1,3},{2,4},{3,5},{4,6},{5,7},{6,0},{7,1},{8,10},{9,11},{10,... | collective-permute-start | bytes 12296 | tf_op jit(solution)/shard_map/ppermute | solution.py:392
  126.2 4.5 %collective-permute-start.18 = (bf16[16,128]{1,0:T(8,128)(2,1)S(1)}, bf16[16,128]{1,0:T(8,128)(2,1)S(1)}, u32[]{:S(2)}, u32[]{:S(2)}) collective-permute-start(bf16[16,128]{1,0:T(8,128)(2,1)S(1)} %get-tuple-element.72), channel_id=1, source_target_pairs={{0,4},{1,5},{2,6},{3,7},{4,0},{5,1},{6,2},{7,3},{8,12},{9,13},{10,... | collective-permute-start | bytes 12296 | tf_op jit(solution)/shard_map/ppermute | solution.py:392
  127.1 5.4 %collective-permute-start.19 = (bf16[16,128]{1,0:T(8,128)(2,1)S(1)}, bf16[16,128]{1,0:T(8,128)(2,1)S(1)}, u32[]{:S(2)}, u32[]{:S(2)}) collective-permute-start(bf16[16,128]{1,0:T(8,128)(2,1)S(1)} %get-tuple-element.73), channel_id=1, source_target_pairs={{0,6},{1,7},{2,0},{3,1},{4,2},{5,3},{6,4},{7,5},{8,14},{9,15},{10,... | collective-permute-start | bytes 12296 | tf_op jit(solution)/shard_map/ppermute | solution.py:392
  135.7 8.8 %collective-permute-start.23 = (bf16[512,128]{1,0:T(8,128)(2,1)S(1)}, bf16[512,128]{1,0:T(8,128)(2,1)S(1)}, u32[]{:S(2)}, u32[]{:S(2)}) collective-permute-start(bf16[512,128]{1,0:T(8,128)(2,1)S(1)} %get-tuple-element.80), channel_id=1, source_target_pairs={{0,8},{8,16},{16,24},{24,0},{32,40},{40,48},{48,56},{56,32},{64,72... | collective-permute-start | bytes 393224 | tf_op jit(solution)/shard_map/ppermute | solution.py:392
  137.4 9.2 %collective-permute-start.20 = (bf16[528,128]{1,0:T(8,128)(2,1)S(1)}, bf16[528,128]{1,0:T(8,128)(2,1)S(1)}, u32[]{:S(2)}, u32[]{:S(2)}) collective-permute-start(bf16[528,128]{1,0:T(8,128)(2,1)S(1)} %get-tuple-element.76), channel_id=1, source_target_pairs={{0,64},{8,72},{16,80},{24,88},{32,96},{40,104},{48,112},{56,120},{... | collective-permute-start | bytes 405512 | tf_op jit(solution)/shard_map/ppermute | solution.py:392
  137.8 7.1 %collective-permute-start.24 = (bf16[512,128]{1,0:T(8,128)(2,1)S(1)}, bf16[512,128]{1,0:T(8,128)(2,1)S(1)}, u32[]{:S(2)}, u32[]{:S(2)}) collective-permute-start(bf16[512,128]{1,0:T(8,128)(2,1)S(1)} %get-tuple-element.81), channel_id=1, source_target_pairs={{0,16},{8,24},{16,0},{24,8},{32,48},{40,56},{48,32},{56,40},{64,80... | collective-permute-start | bytes 393224 | tf_op jit(solution)/shard_map/ppermute | solution.py:392
  139.4 6.0 %collective-permute-start.25 = (bf16[512,128]{1,0:T(8,128)(2,1)S(1)}, bf16[512,128]{1,0:T(8,128)(2,1)S(1)}, u32[]{:S(2)}, u32[]{:S(2)}) collective-permute-start(bf16[512,128]{1,0:T(8,128)(2,1)S(1)} %get-tuple-element.82), channel_id=1, source_target_pairs={{0,24},{8,0},{16,8},{24,16},{32,56},{40,32},{48,40},{56,48},{64,88... | collective-permute-start | bytes 393224 | tf_op jit(solution)/shard_map/ppermute | solution.py:392
  141.1 6.5 %collective-permute-start.21 = (bf16[528,128]{1,0:T(8,128)(2,1)S(1)}, bf16[528,128]{1,0:T(8,128)(2,1)S(1)}, u32[]{:S(2)}, u32[]{:S(2)}) collective-permute-start(bf16[528,128]{1,0:T(8,128)(2,1)S(1)} %get-tuple-element.77), channel_id=1, source_target_pairs={{0,128},{8,136},{16,144},{24,152},{32,160},{40,168},{48,176},{56,1... | collective-permute-start | bytes 405512 | tf_op jit(solution)/shard_map/ppermute | solution.py:392
  144.5 5.1 %collective-permute-start.22 = (bf16[528,128]{1,0:T(8,128)(2,1)S(1)}, bf16[528,128]{1,0:T(8,128)(2,1)S(1)}, u32[]{:S(2)}, u32[]{:S(2)}) collective-permute-start(bf16[528,128]{1,0:T(8,128)(2,1)S(1)} %get-tuple-element.78), channel_id=1, source_target_pairs={{0,192},{8,200},{16,208},{24,216},{32,224},{40,232},{48,240},{56,2... | collective-permute-start | bytes 405512 | tf_op jit(solution)/shard_map/ppermute | solution.py:392
  144.9 31.2 %collective-permute-start.14 = (bf16[1040,128]{1,0:T(8,128)(2,1)}, bf16[1040,128]{1,0:T(8,128)(2,1)S(1)}, u32[]{:S(2)}, u32[]{:S(2)}) collective-permute-start(bf16[1040,128]{1,0:T(8,128)(2,1)} %get-tuple-element.64), channel_id=1, source_target_pairs={{0,2},{1,3},{2,4},{3,5},{4,6},{5,7},{6,0},{7,1},{8,10},{9,11},{10,... | collective-permute-start | bytes 798728 | tf_op jit(solution)/shard_map/ppermute | solution.py:392
  145.5 30.6 %collective-permute-start.15 = (bf16[1040,128]{1,0:T(8,128)(2,1)}, bf16[1040,128]{1,0:T(8,128)(2,1)S(1)}, u32[]{:S(2)}, u32[]{:S(2)}) collective-permute-start(bf16[1040,128]{1,0:T(8,128)(2,1)} %get-tuple-element.65), channel_id=1, source_target_pairs={{0,4},{1,5},{2,6},{3,7},{4,0},{5,1},{6,2},{7,3},{8,12},{9,13},{10,... | collective-permute-start | bytes 798728 | tf_op jit(solution)/shard_map/ppermute | solution.py:392
  146.6 30.2 %collective-permute-start.16 = (bf16[1040,128]{1,0:T(8,128)(2,1)}, bf16[1040,128]{1,0:T(8,128)(2,1)S(1)}, u32[]{:S(2)}, u32[]{:S(2)}) collective-permute-start(bf16[1040,128]{1,0:T(8,128)(2,1)} %get-tuple-element.66), channel_id=1, source_target_pairs={{0,6},{1,7},{2,0},{3,1},{4,2},{5,3},{6,4},{7,5},{8,14},{9,15},{10,... | collective-permute-start | bytes 798728 | tf_op jit(solution)/shard_map/ppermute | solution.py:392
  150.3 5.2 %collective-permute-start.29 = (bf16[128,128]{1,0:T(8,128)(2,1)S(1)}, bf16[128,128]{1,0:T(8,128)(2,1)S(1)}, u32[]{:S(2)}, u32[]{:S(2)}) collective-permute-start(bf16[128,128]{1,0:T(8,128)(2,1)S(1)} %get-tuple-element.89), channel_id=1, source_target_pairs={{0,64},{8,72},{16,80},{24,88},{32,96},{40,104},{48,112},{56,120},{... | collective-permute-start | bytes 98312 | tf_op jit(solution)/shard_map/ppermute | solution.py:392
  151.0 5.8 %collective-permute-start.30 = (bf16[128,128]{1,0:T(8,128)(2,1)S(1)}, bf16[128,128]{1,0:T(8,128)(2,1)S(1)}, u32[]{:S(2)}, u32[]{:S(2)}) collective-permute-start(bf16[128,128]{1,0:T(8,128)(2,1)S(1)} %get-tuple-element.90), channel_id=1, source_target_pairs={{0,128},{8,136},{16,144},{24,152},{32,160},{40,168},{48,176},{56,1... | collective-permute-start | bytes 98312 | tf_op jit(solution)/shard_map/ppermute | solution.py:392
  155.6 6.3 %collective-permute-start.26 = (bf16[144,128]{1,0:T(8,128)(2,1)S(1)}, bf16[144,128]{1,0:T(8,128)(2,1)S(1)}, u32[]{:S(2)}, u32[]{:S(2)}) collective-permute-start(bf16[144,128]{1,0:T(8,128)(2,1)S(1)} %get-tuple-element.85), channel_id=1, source_target_pairs={{0,8},{8,16},{16,24},{24,0},{32,40},{40,48},{48,56},{56,32},{64,72... | collective-permute-start | bytes 110600 | tf_op jit(solution)/shard_map/ppermute | solution.py:392
  160.7 5.5 %collective-permute-start.27 = (bf16[144,128]{1,0:T(8,128)(2,1)S(1)}, bf16[144,128]{1,0:T(8,128)(2,1)S(1)}, u32[]{:S(2)}, u32[]{:S(2)}) collective-permute-start(bf16[144,128]{1,0:T(8,128)(2,1)S(1)} %get-tuple-element.86), channel_id=1, source_target_pairs={{0,16},{8,24},{16,0},{24,8},{32,48},{40,56},{48,32},{56,40},{64,80... | collective-permute-start | bytes 110600 | tf_op jit(solution)/shard_map/ppermute | solution.py:392
  166.8 8.0 %collective-permute-start.32 = (bf16[144,128]{1,0:T(8,128)(2,1)S(1)}, bf16[144,128]{1,0:T(8,128)(2,1)S(1)}, u32[]{:S(2)}, u32[]{:S(2)}) collective-permute-start(bf16[144,128]{1,0:T(8,128)(2,1)S(1)} %get-tuple-element.93), channel_id=1, source_target_pairs={{0,32},{8,40},{16,48},{24,56},{32,0},{40,8},{48,16},{56,24},{64,96... | collective-permute-start | bytes 110600 | tf_op jit(solution)/shard_map/ppermute | solution.py:392
  (24 other events, 124.1 us)

commit v3 on v2

v3 whole, which is shorter than its diff:
```python
import functools
import math

import jax
import jax.numpy as jnp
from jax import lax
from jax.experimental import pallas as pl
from jax.experimental.pallas import tpu as pltpu
from jax.sharding import PartitionSpec as P


BF = jnp.bfloat16
F32 = jnp.float32
SIDE = 32
LANES = 128
TOK = SIDE * SIDE
NEG = -1e30
VM = 20 << 20


def dot(a, b, ca, cb):
    return lax.dot_general(a, b, (((ca,), (cb,)), ((), ())), preferred_element_type=F32)


def call(body, outs, **kw):
    return pl.pallas_call(
        body,
        out_shape=outs,
        compiler_params=pltpu.CompilerParams(vmem_limit_bytes=VM),
        **kw,
    )


def shape(dims, kind):
    return jax.ShapeDtypeStruct(dims, kind)


def far(dims, kind):
    return pltpu.HBM(dims, kind)


def stay(a):
    return pltpu.with_memory_space_constraint(a, pltpu.HBM)


def places(at_ref):
    head, slab = at_ref[0], at_ref[1]
    return head // 2, head % 2, slab // 8, (slab // 4) % 2, slab % 4


def rows_at(i, count):
    return pl.ds(pl.multiple_of(i * count, count), count)


def pack_body(q_ref, k_ref, v_ref, o_ref, out_ref, buf, sems):
    copies = [
        pltpu.make_async_copy(src, buf.at[j], sems.at[j])
        for j, src in enumerate((q_ref, k_ref, v_ref, o_ref))
    ]
    for c in copies:
        c.start()
    for c in copies:
        c.wait()
    for j in range(4):
        out_ref[:, j * LANES : (j + 1) * LANES] = buf[j]


def pair_up_body(at_ref, mine_ref, got_ref, out_ref):
    _, _, _, zh, _ = places(at_ref)
    for place, ref in ((zh, mine_ref), (1 - zh, got_ref)):
        out_ref[:, rows_at(place, SIDE)] = jnp.broadcast_to(ref[...][None], (16, *ref.shape))


def norm_stats_body(x_ref, gain_ref, normed_ref, inv_ref):
    x = x_ref[...].astype(F32)
    width = x.shape[1]
    inv = lax.rsqrt(jnp.sum(x * x, axis=1, keepdims=True) / width + 1e-06)
    normed_ref[...] = (x * inv * gain_ref[...]).astype(BF)
    inv_ref[...] = jnp.broadcast_to(inv, inv_ref.shape)


def project_body(normed_ref, go_ref, pieces_ref, out_ref, w_ref):
    @pl.when(pl.program_id(0) == 0)
    def _():
        for x in range(4):
            for zh in range(2):
                for y in range(4):
                    d = x * 8 + zh * 4 + y
                    w_ref[d * SIDE : (d + 1) * SIDE] = pieces_ref[
                        x * 4 + y, zh * SIDE : (zh + 1) * SIDE
                    ]

    rows = normed_ref.shape[0]
    three = dot(normed_ref[...], w_ref[:, : 3 * LANES], 1, 0)
    last = dot(go_ref[...], w_ref[:, 3 * LANES :], 1, 0)
    for j in range(4):
        part = three[:, j * LANES : (j + 1) * LANES] if j < 3 else last
        out_ref[:, j] = part.astype(BF).reshape(rows // SIDE, SIDE, LANES)


def first_head(rows):
    return lax.broadcasted_iota(jnp.int32, (rows, LANES), 1) < LANES // 2


def stacked(a):
    rows = a.shape[0]
    keep = first_head(rows)
    zero = jnp.zeros_like(a)
    return jnp.concatenate([jnp.where(keep, a, zero), jnp.where(keep, zero, a)], axis=0)


def folded(a):
    rows = a.shape[0] // 2
    return jnp.where(first_head(rows), a[:rows], a[rows:])


def attend(q, k, v, g, factors, bias):
    rows = q.shape[0]
    k2, v2 = stacked(k), stacked(v)
    s = dot(q, k2, 1, 1)
    dp = dot(g, v2, 1, 1)
    probs = []
    for h in range(2):
        sh = s[:, h * rows : (h + 1) * rows] * factors[h] + bias
        top = jnp.max(sh, axis=1, keepdims=True)
        e = jnp.exp(sh - top)
        probs.append(e / jnp.sum(e, axis=1, keepdims=True))
    pb = jnp.concatenate([p.astype(BF) for p in probs], axis=1)
    out = dot(pb, v2, 1, 0)
    go = g.astype(F32) * out
    keep = first_head(rows)
    grads = []
    for h in range(2):
        mine = jnp.where(keep, go, 0.0) if h == 0 else jnp.where(keep, 0.0, go)
        delta = jnp.sum(mine, axis=1, keepdims=True)
        dh = dp[:, h * rows : (h + 1) * rows]
        grads.append((probs[h] * (dh - delta) * factors[h]).astype(BF))
    ds = jnp.concatenate(grads, axis=1)
    gq = dot(ds, k2, 1, 0)
    gk = folded(dot(ds, q, 0, 0))
    gv = folded(dot(pb, g, 0, 0))
    return out, gq, gk, gv


def same_line(rows, line):
    a = line(lax.broadcasted_iota(jnp.int32, (rows, rows), 0))
    b = line(lax.broadcasted_iota(jnp.int32, (rows, rows), 1))
    return jnp.where(a == b, 0.0, NEG).astype(F32)


def strided_lines(in_ref, f_ref, wide_ref, bias_ref, add):
    for j in range(4):
        wide_ref[j] = in_ref[:, j].astype(F32).reshape(SIDE, 4, 8, LANES)
    rows = 8 * SIDE
    bias_ref[...] = same_line(rows, lambda i: i % 8)
    factors = (f_ref[0], f_ref[1])

    def step(b, _):
        parts = [wide_ref[j, :, b].reshape(rows, LANES).astype(BF) for j in range(4)]
        for j, r in enumerate(attend(*parts, factors, bias_ref[...])):
            add(j, b, r.reshape(SIDE, 8, LANES))
        return 0

    lax.fori_loop(0, 4, step, 0)


def plane_body(in_ref, f_ref, out_ref, wide_ref, bias_ref, bias_x_ref):
    rows = 4 * SIDE
    bias_x_ref[...] = same_line(rows, lambda i: i // SIDE)
    factors = (f_ref[0], f_ref[1])

    def step(b, _):
        parts = [in_ref[pl.ds(4 * b, 4), j].reshape(rows, LANES) for j in range(4)]
        for j, r in enumerate(attend(*parts, factors, bias_x_ref[...])):
            out_ref[j, pl.ds(4 * b, 4)] = r.reshape(4, 4, 8, LANES)
        return 0

    lax.fori_loop(0, 8, step, 0)

    def add(j, b, r):
        out_ref[j, :, b] += r

    strided_lines(in_ref, f_ref, wide_ref, bias_ref, add)


def depth_body(in_ref, f_ref, out_ref, wide_ref, res_ref, bias_ref):
    def add(j, b, r):
        res_ref[j, :, b] = r

    strided_lines(in_ref, f_ref, wide_ref, bias_ref, add)
    for j in range(4):
        out_ref[:, j] = res_ref[j].reshape(SIDE, SIDE, LANES).astype(BF)


def halves(a):
    high = a.astype(BF)
    return high, (a - high.astype(F32)).astype(BF)


def combine_body(
    at_ref, loc_ref, back_ref, proj_ref, normed_ref, gain_ref, w_ref,
    away_ref, keep_ref, small_ref, g_ref, sum_ref,
):
    core = places(at_ref)[1]
    step = pl.program_id(0)
    rows = normed_ref.shape[0]
    total = jnp.zeros((rows, LANES), F32)
    for j in range(4):
        part = loc_ref[j].reshape(rows, LANES) + back_ref[:, j].astype(F32).reshape(rows, LANES)
        part = part.astype(BF)
        at = (j - 1) % 4
        g_ref[:, at * LANES : (at + 1) * LANES] = part
        if j > 0:
            total += part.astype(F32) * proj_ref[:, j - 1].astype(F32).reshape(rows, LANES)
    for i in range(rows // LANES):
        row = jnp.sum(total[i * LANES : (i + 1) * LANES].T, axis=0, keepdims=True)
        small_ref[pl.ds(step * (rows // LANES) + i, 1)] = row

    @pl.when(step == 0)
    def _():
        sum_ref[...] = jnp.zeros_like(sum_ref)

    def block(h):
        w = w_ref[rows_at(h, LANES), : 3 * LANES]
        part = dot(g_ref[:, : 3 * LANES], w, 1, 1).astype(BF)
        n = normed_ref[:, rows_at(h, LANES)].astype(F32)
        return part, jnp.sum((part.astype(F32) * n).reshape(rows // 8, 8, LANES), axis=0)

    for i in range(4):
        away_ref[i], gain = block(2 * i + 1 - core)
        sum_ref[i] += gain
        keep_ref[i], gain = block(2 * i + core)
        sum_ref[4 + i] += gain

    @pl.when(step == pl.num_programs(0) - 1)
    def _():
        for i in range(8):
            h = 2 * (i % 4) + (1 - core if i < 4 else core)
            gain = jnp.sum(sum_ref[i], axis=0, keepdims=True) / gain_ref[pl.ds(h, 1)]
            small_ref[8 + i : 9 + i] = gain


def pair_body(at_ref, got_ref, keep_ref, small_ref, sgot_ref, *refs):
    sends, tinies, own_ref, both_ref, gown_ref, gain_buf = (
        refs[:3], refs[3:6], refs[6], refs[7], refs[8], refs[9]
    )
    zl = places(at_ref)[0]
    got = sgot_ref[...]
    dots = small_ref[:8] + got[:8]
    both_ref[...] = dots
    high, low = halves(dots)
    gain_buf[...] = jnp.concatenate([small_ref[12:16] + got[8:12]] * 2, axis=0)

    def block(i):
        return keep_ref[i].astype(F32) + got_ref[i].astype(F32)

    def gain(i):
        return jnp.broadcast_to(gain_buf[pl.ds(i, 1)], (8, LANES))

    for d, (ref, tiny) in enumerate(zip(sends, tinies)):
        to = (zl + d + 1) % 4
        ref[:TOK] = block(to).astype(BF)
        ref[TOK : TOK + 16] = jnp.concatenate([high, low], axis=0)
        tiny[...] = jnp.concatenate(halves(gain(to)), axis=0)
    own_ref[...] = block(zl)
    gown_ref[...] = gain(zl)


def tail_of(ref, at):
    return ref[at : at + 8].astype(F32) + ref[at + 8 : at + 16].astype(F32)


def weights_body(normed_ref, go_ref, g_ref, gown_ref, t1_ref, t2_ref, t3_ref, out_ref, gsum_ref):
    gain = gown_ref[...]
    for ref in (t1_ref, t2_ref, t3_ref):
        gain = gain + tail_of(ref, 0)
    gsum_ref[...] = gain
    tail = jnp.concatenate(halves(gain), axis=0)
    three = dot(normed_ref[...], g_ref[:, : 3 * LANES], 0, 0)
    last = dot(go_ref[...], g_ref[:, 3 * LANES :], 0, 0)
    for j in range(4):
        part = three[:, j * LANES : (j + 1) * LANES] if j < 3 else last
        part = part.astype(BF).reshape(2, 4, SIDE, LANES)
        for zh in range(2):
            at = zh * LANES + j * SIDE
            out_ref[:, at : at + SIDE] = part[zh]
    out_ref[:, 2 * LANES :] = jnp.broadcast_to(tail[None], (4, 16, LANES))


def plane_sum_body(at_ref, in_ref, send_ref, own_ref, gain_ref, buf):
    zh = places(at_ref)[3]
    acc = in_ref[0].astype(F32)
    for i in range(1, 16):
        acc = acc + in_ref[i].astype(F32)
    buf[...] = acc
    gain = acc[2 * LANES : 2 * LANES + 8] + acc[2 * LANES + 8 :]
    gain_ref[...] = gain
    send_ref[:LANES] = buf[rows_at(1 - zh, LANES)].astype(BF)
    send_ref[LANES:] = jnp.concatenate(halves(gain), axis=0)
    own_ref[...] = buf[rows_at(zh, LANES)]


def last_body(own_ref, got_ref, gain_ref, q_ref, k_ref, v_ref, o_ref, gout_ref, *, scale):
    acc = (own_ref[...] + got_ref[:128].astype(F32)) * scale
    for j, ref in enumerate((q_ref, k_ref, v_ref)):
        ref[...] = acc[j * SIDE : (j + 1) * SIDE]
    o_ref[...] = acc[3 * SIDE :]
    gain = (gain_ref[...] + tail_of(got_ref, 128)) * scale
    gout_ref[...] = gain[:1]


def norm_body(at_ref, x_ref, gain_ref, own_ref, r1_ref, r2_ref, r3_ref, dots_ref, inv_ref, gx_ref):
    grad = own_ref[...]
    dots = dots_ref[...]
    for ref in (r1_ref, r2_ref, r3_ref):
        grad = grad + ref[:TOK].astype(F32)
        dots = dots + tail_of(ref, TOK)
    cols = [jnp.broadcast_to(dots[i : i + 1], (LANES, LANES)).T for i in range(8)]
    row_dot = jnp.concatenate(cols, axis=0)
    x = x_ref[...].astype(F32)
    inv = inv_ref[...]
    gx = inv * gain_ref[...] * grad - x * (inv * inv) * row_dot * (1.0 / 1024)
    gx_ref[...] = gx.astype(BF)


SMEM = pl.BlockSpec(memory_space=pltpu.SMEM)
VMEM = pl.BlockSpec(memory_space=pltpu.VMEM)


PLANES = [[x * 8 + zh * 4 + y for x in range(4) for y in range(4)] for zh in range(2)]
OVER_Z = [(s, s ^ 4) for s in range(SIDE)]


def in_plane(a):
    return lax.all_to_all(a, "slab", 0, 0, tiled=True, axis_index_groups=PLANES)


def body(
    inputs, norm_gain, query_weight, key_weight, value_weight, out_weight, logit_scale, grad_output
):
    rows, width = inputs.shape
    head_dim = 64
    at = jnp.stack([lax.axis_index("head"), lax.axis_index("slab")]).astype(jnp.int32)
    factors = logit_scale / math.sqrt(head_dim)
    blk = 256
    whole = lambda dims: pl.BlockSpec(dims, lambda i: (0,) * len(dims))
    by_rows = lambda dims: pl.BlockSpec(dims, lambda i: (i,) + (0,) * (len(dims) - 1))

    mine = call(
        pack_body,
        shape((SIDE, 4 * LANES), BF),
        in_specs=[pl.BlockSpec(memory_space=pltpu.HBM)] * 4,
        scratch_shapes=[pltpu.VMEM((4, SIDE, LANES), BF), pltpu.SemaphoreType.DMA((4,))],
    )(*(stay(w) for w in (query_weight, key_weight, value_weight, out_weight.T)))
    other = lax.ppermute(mine, "slab", OVER_Z)
    spread = call(
        pair_up_body, far((16, 2 * SIDE, 4 * LANES), BF), in_specs=[SMEM, VMEM, VMEM]
    )(at, mine, other)
    normed, inv = call(
        norm_stats_body,
        (far((rows, width), BF), far((rows, LANES), F32)),
        grid=(rows // blk,),
        in_specs=[by_rows((blk, width)), whole((1, width))],
        out_specs=(by_rows((blk, width)), by_rows((blk, LANES))),
    )(inputs, norm_gain.reshape(1, width))
    pieces = in_plane(spread)

    proj, weights = call(
        project_body,
        (far((SIDE, 4, SIDE, LANES), BF), far((width, 4 * LANES), BF)),
        grid=(rows // blk,),
        in_specs=[
            by_rows((blk, width)),
            by_rows((blk, width)),
            whole((16, 2 * SIDE, 4 * LANES)),
        ],
        out_specs=(by_rows((blk // SIDE, 4, SIDE, LANES)), whole((width, 4 * LANES))),
    )(stay(normed), stay(grad_output), pieces)

    z_in = lax.all_to_all(proj, "slab", 0, 0, tiled=True)
    big = (4, SIDE, 4, 8, LANES)
    local = call(
        plane_body,
        far(big, F32),
        in_specs=[VMEM, SMEM],
        scratch_shapes=[
            pltpu.VMEM(big, F32),
            pltpu.VMEM((256, 256), F32),
            pltpu.VMEM((128, 128), F32),
        ],
    )(proj, factors)
    z_terms = call(
        depth_body,
        far((SIDE, 4, SIDE, LANES), BF),
        in_specs=[VMEM, SMEM],
        scratch_shapes=[
            pltpu.VMEM(big, F32),
            pltpu.VMEM(big, F32),
            pltpu.VMEM((256, 256), F32),
        ],
    )(z_in, factors)
    back = lax.all_to_all(z_terms, "slab", 0, 0, tiled=True)

    lines = blk // SIDE
    parts4 = pl.BlockSpec((4, blk, LANES), lambda i: (0, i, 0))
    away, keep, small, grads = call(
        combine_body,
        (
            shape((4, TOK, LANES), BF),
            shape((4, TOK, LANES), BF),
            shape((16, LANES), F32),
            shape((TOK, 4 * LANES), BF),
        ),
        grid=(rows // blk,),
        in_specs=[
            SMEM,
            pl.BlockSpec((4, lines, 4, 8, LANES), lambda i: (0, i, 0, 0, 0)),
            by_rows((lines, 4, SIDE, LANES)),
            by_rows((lines, 4, SIDE, LANES)),
            by_rows((blk, width)),
            whole((8, LANES)),
            whole((width, 4 * LANES)),
        ],
        out_specs=(parts4, parts4, whole((16, LANES)), by_rows((blk, 4 * LANES))),
        scratch_shapes=[pltpu.VMEM((8, 8, LANES), F32)],
    )(at, stay(local), back, proj, normed, norm_gain.reshape(8, LANES), stay(weights))

    swap = [(i, i ^ 1) for i in range(8)]
    got = lax.ppermute(away, "head", swap)
    got_small = lax.ppermute(small, "head", swap)
    piece, tiny, row8 = (
        shape((TOK + 16, LANES), BF),
        shape((16, LANES), BF),
        shape((8, LANES), F32),
    )
    *sends, own, dots, gown = call(
        pair_body,
        (piece,) * 3 + (tiny,) * 3 + (shape((TOK, LANES), F32), row8, row8),
        in_specs=[SMEM] + [VMEM] * 4,
        scratch_shapes=[pltpu.VMEM((8, LANES), F32)],
    )(at, got, keep, small, got_small)
    to_zl = lambda d: [(i, (i + 2 * d) % 8) for i in range(8)]
    tinies = [lax.ppermute(s, "head", to_zl(d + 1)) for d, s in enumerate(sends[3:])]
    parts = []
    for d, s in enumerate(sends[:3]):
        parts.append(lax.ppermute(s, "head", to_zl(d + 1)))

    sent, _ = call(
        weights_body,
        (shape((16, 272, LANES), BF), row8),
        grid=(4,),
        in_specs=[
            pl.BlockSpec((rows, 256), lambda i: (0, i)),
            pl.BlockSpec((rows, 256), lambda i: (0, i)),
            whole((rows, 4 * LANES)),
            whole((8, LANES)),
        ]
        + [whole((16, LANES))] * 3,
        out_specs=(by_rows((4, 272, LANES)), whole((8, LANES))),
    )(normed, grad_output, grads, gown, *tinies)
    send, mine, gain = call(
        plane_sum_body,
        (shape((LANES + 16, LANES), BF), shape((LANES, LANES), F32), row8),
        in_specs=[SMEM, VMEM],
        scratch_shapes=[pltpu.VMEM((272, LANES), F32)],
    )(at, in_plane(sent))
    part = shape((SIDE, LANES), F32)
    gqw, gkw, gvw, gow, ggain = call(
        functools.partial(last_body, scale=1.0 / math.sqrt(rows * SIDE)),
        (part, part, part, part, shape((1, LANES), F32)),
    )(mine, lax.ppermute(send, "slab", OVER_Z), gain)

    all_of = lambda dims: pl.BlockSpec(dims, lambda i, h: (0,) * len(dims))
    grad_inputs = pl.pallas_call(
        norm_body,
        out_shape=shape((rows, LANES), BF),
        name="norm_back",
        grid_spec=pltpu.PrefetchScalarGridSpec(
            num_scalar_prefetch=1,
            grid=(1,),
            in_specs=[
                pl.BlockSpec((rows, LANES), lambda i, h: (0, h[0])),
                pl.BlockSpec((1, LANES), lambda i, h: (0, h[0])),
                all_of((TOK, LANES)),
                all_of((TOK + 16, LANES)),
                all_of((TOK + 16, LANES)),
                all_of((TOK + 16, LANES)),
                all_of((8, LANES)),
                all_of((TOK, LANES)),
            ],
            out_specs=all_of((rows, LANES)),
        ),
        compiler_params=pltpu.CompilerParams(vmem_limit_bytes=VM),
    )(at, inputs, norm_gain.reshape(1, width), own, *parts, dots, inv)
    return grad_inputs, ggain.reshape(LANES), gqw, gkw, gvw, gow.T


def solution(mesh):
    in_specs = (
        P("slab", None),
        P(),
        P("slab", "head"),
        P("slab", "head"),
        P("slab", "head"),
        P("head", "slab"),
        P("head"),
        P("slab", None),
    )
    out_specs = (
        P("slab", "head"),
        P("head"),
        P("slab", "head"),
        P("slab", "head"),
        P("slab", "head"),
        P("head", "slab"),
    )

    return jax.shard_map(
        body, mesh=mesh, in_specs=in_specs, out_specs=out_specs, check_vma=False
    )
```

time: 186 us -> 174 us (0.935)
  the two profiles are of different devices: /device:TPU:96 before, /device:TPU:35 now
where the time goes in v3:
time: 174 us; the launch traced here: 173 us
  waiting for transfers between devices  80.2 us (46%)
  starting transfers between devices  46.2 us (27%)
  Pallas kernels  41.5 us (24%)
  local copies, waits for them, and re-layouts  3.93 us (2%)
    all_to_all x1, waiting for transfers between devices, body(): z_in = lax.all_to_all(proj, 'slab', 0, 0, tiled=True)  28.7 us
    all_to_all x2, waiting for transfers between devices, in_plane(): return lax.all_to_all(a, 'slab', 0, 0, tiled=True, axis_index_groups=PLANES)  19.8 us
    ppermute x3, waiting for transfers between devices, body(): parts.append(lax.ppermute(s, 'head', to_zl(d + 1)))  14.3 us
    all_to_all x2, starting transfers between devices, in_plane(): return lax.all_to_all(a, 'slab', 0, 0, tiled=True, axis_index_groups=PLANES)  13.7 us
    pallas_call x1, Pallas kernels, body(): call(plane_body, far(big, F32), in_specs=[VMEM, SMEM], scratch_shapes=[pl...  12 us
    all_to_all x1, waiting for transfers between devices, body(): back = lax.all_to_all(z_terms, 'slab', 0, 0, tiled=True)  11.8 us
    all_to_all x1, starting transfers between devices, body(): z_in = lax.all_to_all(proj, 'slab', 0, 0, tiled=True)  11.6 us
    all_to_all x1, starting transfers between devices, body(): back = lax.all_to_all(z_terms, 'slab', 0, 0, tiled=True)  6.77 us
  transfers between devices with their start and end apart: 14, of which 10 were waited for; matrix products, arithmetic and copies ran while one was open for 0% of the time, Pallas kernels for 10%

profile of v3, /device:TPU:35, one launch (start us, length us, event | category | flops | bytes accessed | tf_op | source)
XLA Modules:
  0.0 172.8 jit_solution(6174483257578981391)
XLA Ops:
  0.7 0.9 shard_map.128.mine_ref
  1.6 6.1 %collective-permute-start = (bf16[32,512]{1,0:T(8,128)(2,1)S(1)}, bf16[32,512]{1,0:T(8,128)(2,1)S(1)}, u32[]{:S(2)}, u32[]{:S(2)}) collective-permute-start(bf16[32,512]{1,0:T(8,128)(2,1)S(1)} %shard_map.128.mine_ref), channel_id=1, source_target_pairs={{0,32},{8,40},{16,48},{24,56},{32,0},{40,8},{48,16},{56,24},{64,96... | collective-permute-start | bytes 98312 | tf_op jit(solution)/shard_map/ppermute | solution.py:355
  7.8 1.2 collective-permute-done.got_ref
  9.0 1.6 shard_map.129
  10.6 6.9 %all-to-all-start = ((bf16[16,64,512]{2,1,0:T(8,128)(2,1)}), bf16[16,64,512]{2,1,0:T(8,128)(2,1)S(1)}, u32[]{:S(2)}, u32[]{:S(2)}) async-start(bf16[16,64,512]{2,1,0:T(8,128)(2,1)} %shard_map.129), calls=%async_computation | async-start | bytes 2097152 | tf_op jit(solution)/shard_map/all_to_all | solution.py:335
  17.5 2.4 %shard_map.127 = (bf16[1024,1024]{1,0:T(8,128)(2,1)}, f32[1024,128]{1,0:T(8,128)}) custom-call(bf16[1024,1024]{1,0:T(8,128)(2,1)S(1)} %copy-done.2, f32[1,1024]{1,0:T(1,128)S(1)} %bitcast.7), custom_call_target="tpu_custom_call" | custom-call | tf_op jit(solution)/shard_map/pallas_call | solution.py:359
  19.9 10.8 %all-to-all-done.pieces_ref = bf16[16,64,512]{2,1,0:T(8,128)(2,1)S(1)} async-done(((bf16[16,64,512]{2,1,0:T(8,128)(2,1)}), bf16[16,64,512]{2,1,0:T(8,128)(2,1)S(1)}, u32[]{:S(2)}, u32[]{:S(2)}) %all-to-all-start) | async-done | bytes 1048608 | tf_op jit(solution)/shard_map/all_to_all | solution.py:335
  30.8 5.3 %shard_map.130 = (bf16[32,4,32,128]{3,2,1,0:T(8,128)(2,1)}, bf16[1024,512]{1,0:T(8,128)(2,1)}) custom-call(bf16[1024,1024]{1,0:T(8,128)(2,1)} %get-tuple-element.32.normed_ref, bf16[1024,1024]{1,0:T(8,128)(2,1)} %go_ref.3, bf16[16,64,512]{2,1,0:T(8,128)(2,1)S(1)} %all-to-all-done.pieces_ref), custom_call_target="tpu_custom_call" | custom-call | tf_op jit(solution)/shard_map/pallas_call | solution.py:368
  36.1 11.6 %all-to-all-start.1 = ((bf16[32,4,32,128]{3,2,1,0:T(8,128)(2,1)}), bf16[32,4,32,128]{3,2,1,0:T(8,128)(2,1)S(1)}, u32[]{:S(2)}, u32[]{:S(2)}) async-start(bf16[32,4,32,128]{3,2,1,0:T(8,128)(2,1)} %get-tuple-element.33.in_ref.proj_ref), calls=%async_computation.1 | async-start | bytes 2097152 | tf_op jit(solution)/shard_map/all_to_all | solution.py:380
  47.7 28.7 %all-to-all-done.1.in_ref = bf16[32,4,32,128]{3,2,1,0:T(8,128)(2,1)S(1)} async-done(((bf16[32,4,32,128]{3,2,1,0:T(8,128)(2,1)}), bf16[32,4,32,128]{3,2,1,0:T(8,128)(2,1)S(1)}, u32[]{:S(2)}, u32[]{:S(2)}) %all-to-all-start.1) | async-done | bytes 1048608 | tf_op jit(solution)/shard_map/all_to_all | solution.py:380
  76.5 5.7 %shard_map.132 = bf16[32,4,32,128]{3,2,1,0:T(8,128)(2,1)} custom-call(bf16[32,4,32,128]{3,2,1,0:T(8,128)(2,1)S(1)} %all-to-all-done.1.in_ref, f32[2]{0:T(128)S(1)} %broadcast_multiply_fusion.f_ref), custom_call_target="tpu_custom_call" | custom-call | tf_op jit(solution)/shard_map/pallas_call | solution.py:392
  82.2 6.8 %all-to-all-start.2 = ((bf16[32,4,32,128]{3,2,1,0:T(8,128)(2,1)}), bf16[32,4,32,128]{3,2,1,0:T(8,128)(2,1)}, u32[]{:S(2)}, u32[]{:S(2)}) async-start(bf16[32,4,32,128]{3,2,1,0:T(8,128)(2,1)} %shard_map.132), calls=%async_computation.2 | async-start | bytes 2097152 | tf_op jit(solution)/shard_map/all_to_all | solution.py:402
  89.0 12.0 %shard_map.131.loc_ref = f32[4,32,4,8,128]{4,3,2,1,0:T(8,128)} custom-call(bf16[32,4,32,128]{3,2,1,0:T(8,128)(2,1)S(1)} %copy-done.1, f32[2]{0:T(128)S(1)} %broadcast_multiply_fusion.f_ref), custom_call_target="tpu_custom_call" | custom-call | tf_op jit(solution)/shard_map/pallas_call | solution.py:382
  101.0 11.8 %all-to-all-done.2.back_ref = bf16[32,4,32,128]{3,2,1,0:T(8,128)(2,1)} async-done(((bf16[32,4,32,128]{3,2,1,0:T(8,128)(2,1)}), bf16[32,4,32,128]{3,2,1,0:T(8,128)(2,1)}, u32[]{:S(2)}, u32[]{:S(2)}) %all-to-all-start.2) | async-done | bytes 1048608 | tf_op jit(solution)/shard_map/all_to_all | solution.py:402
  112.8 5.2 %shard_map.133 = (bf16[4,1024,128]{2,1,0:T(8,128)(2,1)S(1)}, bf16[4,1024,128]{2,1,0:T(8,128)(2,1)S(1)}, f32[16,128]{1,0:T(8,128)S(1)}, bf16[1024,512]{1,0:T(8,128)(2,1)S(1)}) custom-call(s32[2]{0:T(128)S(1)} %pad_add_fusion.at_ref, f32[4,32,4,8,128]{4,3,2,1,0:T(8,128)} %shard_map.131.loc_ref, bf16[32,4,32,128]{3,2,1,0:T(8,128)(2,1)} %all-to-all-done.2.back_ref, ...), custom_call_target="tpu_custom_call" | custom-call | tf_op jit(solution)/shard_map/pallas_call | solution.py:406
  118.0 0.8 collective-permute-start.1
  118.9 2.2 %collective-permute-done.2.sgot_ref = f32[16,128]{1,0:T(8,128)S(1)} collective-permute-done((f32[16,128]{1,0:T(8,128)S(1)}, f32[16,128]{1,0:T(8,128)S(1)}, u32[]{:S(2)}, u32[]{:S(2)}) %collective-permute-start.2) | collective-permute-done | bytes 8224 | tf_op jit(solution)/shard_map/ppermute | solution.py:430
  121.1 1.0 shard_map.134
  123.6 1.3 collective-permute-start.8
  125.4 1.6 collective-permute-done.7.t2_ref
  127.0 3.6 %shard_map.135 = (bf16[16,272,128]{2,1,0:T(8,128)(2,1)S(1)}, f32[8,128]{1,0:T(8,128)}) custom-call(bf16[1024,1024]{1,0:T(8,128)(2,1)S(1)} %copy-done, bf16[1024,1024]{1,0:T(8,128)(2,1)S(1)} %copy-done.4, bf16[1024,512]{1,0:T(8,128)(2,1)S(1)} %get-tuple-element.44.g_ref, f32[8,128]{1,0:T(8,128)S(1)} %get-tuple-element.45.gown_ref, ...), custom_call_target="tpu_custom_call" | custom-call | tf_op jit(solution)/shard_map/pallas_call | solution.py:448
  130.6 1.0 copy-done.5
  131.6 6.8 %all-to-all-start.3 = ((bf16[16,272,128]{2,1,0:T(8,128)(2,1)}), bf16[16,272,128]{2,1,0:T(8,128)(2,1)S(1)}, u32[]{:S(2)}, u32[]{:S(2)}) async-start(bf16[16,272,128]{2,1,0:T(8,128)(2,1)} %copy-done.5), calls=%async_computation.3 | async-start | bytes 2228224 | tf_op jit(solution)/shard_map/all_to_all | solution.py:335
  138.4 1.2 collective-permute-start.3
  139.6 2.1 %collective-permute-start.4 = (bf16[1040,128]{1,0:T(8,128)(2,1)}, bf16[1040,128]{1,0:T(8,128)(2,1)}, u32[]{:S(2)}, u32[]{:S(2)}) collective-permute-start(bf16[1040,128]{1,0:T(8,128)(2,1)} %copy-done.11), channel_id=1, source_target_pairs={{0,4},{1,5},{2,6},{3,7},{4,0},{5,1},{6,2},{7,3},{8,12},{9,13},{10,... | collective-permute-start | bytes 798728 | tf_op jit(solution)/shard_map/ppermute | solution.py:446
  141.7 1.4 collective-permute-start.5
  143.1 9.0 %all-to-all-done.3.in_ref = bf16[16,272,128]{2,1,0:T(8,128)(2,1)S(1)} async-done(((bf16[16,272,128]{2,1,0:T(8,128)(2,1)}), bf16[16,272,128]{2,1,0:T(8,128)(2,1)S(1)}, u32[]{:S(2)}, u32[]{:S(2)}) %all-to-all-start.3) | async-done | bytes 1114144 | tf_op jit(solution)/shard_map/all_to_all | solution.py:335
  153.2 8.4 %collective-permute-done.4.r2_ref = bf16[1040,128]{1,0:T(8,128)(2,1)} collective-permute-done((bf16[1040,128]{1,0:T(8,128)(2,1)}, bf16[1040,128]{1,0:T(8,128)(2,1)}, u32[]{:S(2)}, u32[]{:S(2)}) %collective-permute-start.4) | collective-permute-done | bytes 266272 | tf_op jit(solution)/shard_map/ppermute | solution.py:446
  161.6 5.9 %collective-permute-done.5.r3_ref = bf16[1040,128]{1,0:T(8,128)(2,1)} collective-permute-done((bf16[1040,128]{1,0:T(8,128)(2,1)}, bf16[1040,128]{1,0:T(8,128)(2,1)}, u32[]{:S(2)}, u32[]{:S(2)}) %collective-permute-start.5) | collective-permute-done | bytes 266272 | tf_op jit(solution)/shard_map/ppermute | solution.py:446
  167.5 1.0 copy-done.6
  168.6 1.0 copy-done.8
  169.6 2.5 %norm_back.1 = bf16[1024,128]{1,0:T(8,128)(2,1)} custom-call(s32[2]{0:T(128)S(1)} %pad_add_fusion.at_ref, bf16[1024,1024]{1,0:T(8,128)(2,1)S(1)} %copy-done.3, f32[1,1024]{1,0:T(1,128)S(1)} %bitcast.9, f32[1024,128]{1,0:T(8,128)S(1)} %copy-done.8, bf16[1040,128]{1,0:T(8,128)(2,1)S(1)} %collective-permute-done.3.r1_ref, ...), custom_call_target="tpu_custom_call" | custom-call | tf_op jit(solution)/shard_map/norm_back/pallas_call | solution.py:474
  (38 shorter events, 3.9 us)
Async XLA Ops:
  0.6 16.9 %copy-start.9 = (f32[1024]{0:T(1024)S(1)}, f32[1024]{0:T(1024)}, u32[]{:S(2)}) copy-start(f32[1024]{0:T(1024)} %param.9) | copy-start | bytes 12292
  0.6 16.9 %copy-start.2 = (bf16[1024,1024]{1,0:T(8,128)(2,1)S(1)}, bf16[1024,1024]{1,0:T(8,128)(2,1)}, u32[]{:S(2)}) copy-start(bf16[1024,1024]{1,0:T(8,128)(2,1)} %x_ref.3) | copy-start | bytes 6291460
  1.6 7.4 %collective-permute-start = (bf16[32,512]{1,0:T(8,128)(2,1)S(1)}, bf16[32,512]{1,0:T(8,128)(2,1)S(1)}, u32[]{:S(2)}, u32[]{:S(2)}) collective-permute-start(bf16[32,512]{1,0:T(8,128)(2,1)S(1)} %shard_map.128.mine_ref), channel_id=1, source_target_pairs={{0,32},{8,40},{16,48},{24,56},{32,0},{40,8},{48,16},{56,24},{64,96... | collective-permute-start | bytes 98312 | tf_op jit(solution)/shard_map/ppermute | solution.py:355
  10.6 20.1 %all-to-all-start = ((bf16[16,64,512]{2,1,0:T(8,128)(2,1)}), bf16[16,64,512]{2,1,0:T(8,128)(2,1)S(1)}, u32[]{:S(2)}, u32[]{:S(2)}) async-start(bf16[16,64,512]{2,1,0:T(8,128)(2,1)} %shard_map.129), calls=%async_computation | async-start | bytes 2097152 | tf_op jit(solution)/shard_map/all_to_all | solution.py:335
  36.1 11.6 %copy-start.13 = (f32[2]{0:T(128)S(1)}, f32[2]{0:T(128)}, u32[]{:S(2)}) copy-start(f32[2]{0:T(128)} %param.14) | copy-start | bytes 28
  36.1 40.4 %all-to-all-start.1 = ((bf16[32,4,32,128]{3,2,1,0:T(8,128)(2,1)}), bf16[32,4,32,128]{3,2,1,0:T(8,128)(2,1)S(1)}, u32[]{:S(2)}, u32[]{:S(2)}) async-start(bf16[32,4,32,128]{3,2,1,0:T(8,128)(2,1)} %get-tuple-element.33.in_ref.proj_ref), calls=%async_computation.1 | async-start | bytes 2097152 | tf_op jit(solution)/shard_map/all_to_all | solution.py:380
  47.7 41.2 %copy-start.1 = (bf16[32,4,32,128]{3,2,1,0:T(8,128)(2,1)S(1)}, bf16[32,4,32,128]{3,2,1,0:T(8,128)(2,1)}, u32[]{:S(2)}) copy-start(bf16[32,4,32,128]{3,2,1,0:T(8,128)(2,1)} %get-tuple-element.33.in_ref.proj_ref) | copy-start | bytes 3145732
  82.2 30.6 %all-to-all-start.2 = ((bf16[32,4,32,128]{3,2,1,0:T(8,128)(2,1)}), bf16[32,4,32,128]{3,2,1,0:T(8,128)(2,1)}, u32[]{:S(2)}, u32[]{:S(2)}) async-start(bf16[32,4,32,128]{3,2,1,0:T(8,128)(2,1)} %shard_map.132), calls=%async_computation.2 | async-start | bytes 2097152 | tf_op jit(solution)/shard_map/all_to_all | solution.py:402
  89.0 23.8 %copy-start = (bf16[1024,1024]{1,0:T(8,128)(2,1)S(1)}, bf16[1024,1024]{1,0:T(8,128)(2,1)}, u32[]{:S(2)}) copy-start(bf16[1024,1024]{1,0:T(8,128)(2,1)} %get-tuple-element.32.normed_ref) | copy-start | bytes 6291460
  118.0 9.0 %copy-start.4 = (bf16[1024,1024]{1,0:T(8,128)(2,1)S(1)}, bf16[1024,1024]{1,0:T(8,128)(2,1)}, u32[]{:S(2)}) copy-start(bf16[1024,1024]{1,0:T(8,128)(2,1)} %go_ref.3) | copy-start | bytes 6291460
  118.0 3.1 %collective-permute-start.1 = (bf16[4,1024,128]{2,1,0:T(8,128)(2,1)S(1)}, bf16[4,1024,128]{2,1,0:T(8,128)(2,1)S(1)}, u32[]{:S(2)}, u32[]{:S(2)}) collective-permute-start(bf16[4,1024,128]{2,1,0:T(8,128)(2,1)S(1)} %get-tuple-element.35), channel_id=1, source_target_pairs={{0,1},{1,0},{2,3},{3,2},{4,5},{5,4},{6,7},{7,6},{8,9},{9,8},{10,11... | collective-permute-start | bytes 3145736 | tf_op jit(solution)/shard_map/ppermute | solution.py:429
  118.8 2.3 %collective-permute-start.2 = (f32[16,128]{1,0:T(8,128)S(1)}, f32[16,128]{1,0:T(8,128)S(1)}, u32[]{:S(2)}, u32[]{:S(2)}) collective-permute-start(f32[16,128]{1,0:T(8,128)S(1)} %get-tuple-element.37.small_ref), channel_id=1, source_target_pairs={{0,1},{1,0},{2,3},{3,2},{4,5},{5,4},{6,7},{7,6},{8,9},{9,8},{10,11... | collective-permute-start | bytes 24584 | tf_op jit(solution)/shard_map/ppermute | solution.py:430
  122.1 0.8 copy-start.7
  122.9 7.7 %copy-start.10 = (bf16[1040,128]{1,0:T(8,128)(2,1)}, bf16[1040,128]{1,0:T(8,128)(2,1)S(1)}, u32[]{:S(2)}) copy-start(bf16[1040,128]{1,0:T(8,128)(2,1)S(1)} %get-tuple-element.41) | copy-start | bytes 798724
  122.9 7.7 %copy-start.11 = (bf16[1040,128]{1,0:T(8,128)(2,1)}, bf16[1040,128]{1,0:T(8,128)(2,1)S(1)}, u32[]{:S(2)}) copy-start(bf16[1040,128]{1,0:T(8,128)(2,1)S(1)} %get-tuple-element.40) | copy-start | bytes 798724
  122.9 7.7 %copy-start.12 = (bf16[1040,128]{1,0:T(8,128)(2,1)}, bf16[1040,128]{1,0:T(8,128)(2,1)S(1)}, u32[]{:S(2)}) copy-start(bf16[1040,128]{1,0:T(8,128)(2,1)S(1)} %get-tuple-element.39) | copy-start | bytes 798724
  122.9 2.5 %collective-permute-start.6 = (bf16[16,128]{1,0:T(8,128)(2,1)S(1)}, bf16[16,128]{1,0:T(8,128)(2,1)S(1)}, u32[]{:S(2)}, u32[]{:S(2)}) collective-permute-start(bf16[16,128]{1,0:T(8,128)(2,1)S(1)} %get-tuple-element.46), channel_id=1, source_target_pairs={{0,2},{1,3},{2,4},{3,5},{4,6},{5,7},{6,0},{7,1},{8,10},{9,11},{10,... | collective-permute-start | bytes 12296 | tf_op jit(solution)/shard_map/ppermute | solution.py:443
  123.6 3.4 %collective-permute-start.7 = (bf16[16,128]{1,0:T(8,128)(2,1)S(1)}, bf16[16,128]{1,0:T(8,128)(2,1)S(1)}, u32[]{:S(2)}, u32[]{:S(2)}) collective-permute-start(bf16[16,128]{1,0:T(8,128)(2,1)S(1)} %get-tuple-element.47), channel_id=1, source_target_pairs={{0,4},{1,5},{2,6},{3,7},{4,0},{5,1},{6,2},{7,3},{8,12},{9,13},{10,... | collective-permute-start | bytes 12296 | tf_op jit(solution)/shard_map/ppermute | solution.py:443
  123.6 3.4 %collective-permute-start.8 = (bf16[16,128]{1,0:T(8,128)(2,1)S(1)}, bf16[16,128]{1,0:T(8,128)(2,1)S(1)}, u32[]{:S(2)}, u32[]{:S(2)}) collective-permute-start(bf16[16,128]{1,0:T(8,128)(2,1)S(1)} %get-tuple-element.48), channel_id=1, source_target_pairs={{0,6},{1,7},{2,0},{3,1},{4,2},{5,3},{6,4},{7,5},{8,14},{9,15},{10,... | collective-permute-start | bytes 12296 | tf_op jit(solution)/shard_map/ppermute | solution.py:443
  130.6 1.0 copy-start.5
  131.6 35.9 %copy-start.3 = (bf16[1024,1024]{1,0:T(8,128)(2,1)S(1)}, bf16[1024,1024]{1,0:T(8,128)(2,1)}, u32[]{:S(2)}) copy-start(bf16[1024,1024]{1,0:T(8,128)(2,1)} %x_ref.3) | copy-start | bytes 6291460
  131.6 20.5 %all-to-all-start.3 = ((bf16[16,272,128]{2,1,0:T(8,128)(2,1)}), bf16[16,272,128]{2,1,0:T(8,128)(2,1)S(1)}, u32[]{:S(2)}, u32[]{:S(2)}) async-start(bf16[16,272,128]{2,1,0:T(8,128)(2,1)} %copy-done.5), calls=%async_computation.3 | async-start | bytes 2228224 | tf_op jit(solution)/shard_map/all_to_all | solution.py:335
  138.4 14.8 %collective-permute-start.3 = (bf16[1040,128]{1,0:T(8,128)(2,1)}, bf16[1040,128]{1,0:T(8,128)(2,1)S(1)}, u32[]{:S(2)}, u32[]{:S(2)}) collective-permute-start(bf16[1040,128]{1,0:T(8,128)(2,1)} %copy-done.12), channel_id=1, source_target_pairs={{0,2},{1,3},{2,4},{3,5},{4,6},{5,7},{6,0},{7,1},{8,10},{9,11},{10,... | collective-permute-start | bytes 798728 | tf_op jit(solution)/shard_map/ppermute | solution.py:446
  139.6 22.0 %collective-permute-start.4 = (bf16[1040,128]{1,0:T(8,128)(2,1)}, bf16[1040,128]{1,0:T(8,128)(2,1)}, u32[]{:S(2)}, u32[]{:S(2)}) collective-permute-start(bf16[1040,128]{1,0:T(8,128)(2,1)} %copy-done.11), channel_id=1, source_target_pairs={{0,4},{1,5},{2,6},{3,7},{4,0},{5,1},{6,2},{7,3},{8,12},{9,13},{10,... | collective-permute-start | bytes 798728 | tf_op jit(solution)/shard_map/ppermute | solution.py:446
  141.7 25.8 %collective-permute-start.5 = (bf16[1040,128]{1,0:T(8,128)(2,1)}, bf16[1040,128]{1,0:T(8,128)(2,1)}, u32[]{:S(2)}, u32[]{:S(2)}) collective-permute-start(bf16[1040,128]{1,0:T(8,128)(2,1)} %copy-done.10), channel_id=1, source_target_pairs={{0,6},{1,7},{2,0},{3,1},{4,2},{5,3},{6,4},{7,5},{8,14},{9,15},{10,... | collective-permute-start | bytes 798728 | tf_op jit(solution)/shard_map/ppermute | solution.py:446
  152.8 19.3 %collective-permute-start.9 = (bf16[144,128]{1,0:T(8,128)(2,1)S(1)}, bf16[144,128]{1,0:T(8,128)(2,1)S(1)}, u32[]{:S(2)}, u32[]{:S(2)}) collective-permute-start(bf16[144,128]{1,0:T(8,128)(2,1)S(1)} %get-tuple-element.51), channel_id=1, source_target_pairs={{0,32},{8,40},{16,48},{24,56},{32,0},{40,8},{48,16},{56,24},{64,96... | collective-permute-start | bytes 110600 | tf_op jit(solution)/shard_map/ppermute | solution.py:471
  167.5 1.0 copy-start.6
  168.6 1.0 copy-start.8

commit v4 on v3

--- a/solution.py
+++ b/solution.py
@@ -71,24 +71,29 @@
         out_ref[:, rows_at(place, SIDE)] = jnp.broadcast_to(ref[...][None], (16, *ref.shape))
 
 
-def norm_stats_body(x_ref, gain_ref, normed_ref, inv_ref):
+def norm_stats_body(x_ref, gain_ref, normed_ref, kept_ref, inv_ref):
     x = x_ref[...].astype(F32)
     width = x.shape[1]
     inv = lax.rsqrt(jnp.sum(x * x, axis=1, keepdims=True) / width + 1e-06)
-    normed_ref[...] = (x * inv * gain_ref[...]).astype(BF)
+    normed = (x * inv * gain_ref[...]).astype(BF)
+    normed_ref[...] = normed
+    kept_ref[...] = normed
     inv_ref[...] = jnp.broadcast_to(inv, inv_ref.shape)
 
 
-def project_body(normed_ref, go_ref, pieces_ref, out_ref, w_ref):
+def weights_of(pieces_ref, x):
+    both = [pieces_ref[4 * x : 4 * x + 4, zh * SIDE : (zh + 1) * SIDE] for zh in range(2)]
+    return jnp.concatenate([a.reshape(4 * SIDE, a.shape[-1]) for a in both], axis=0)
+
+
+def project_body(normed_ref, go_ref, pieces_ref, out_ref, wout_ref, w_ref, sem):
+    copy = pltpu.make_async_copy(w_ref, wout_ref, sem)
+
     @pl.when(pl.program_id(0) == 0)
     def _():
         for x in range(4):
-            for zh in range(2):
-                for y in range(4):
-                    d = x * 8 + zh * 4 + y
-                    w_ref[d * SIDE : (d + 1) * SIDE] = pieces_ref[
-                        x * 4 + y, zh * SIDE : (zh + 1) * SIDE
-                    ]
+            w_ref[256 * x : 256 * (x + 1)] = weights_of(pieces_ref, x)
+        copy.start()
 
     rows = normed_ref.shape[0]
     three = dot(normed_ref[...], w_ref[:, : 3 * LANES], 1, 0)
@@ -96,6 +101,10 @@
     for j in range(4):
         part = three[:, j * LANES : (j + 1) * LANES] if j < 3 else last
         out_ref[:, j] = part.astype(BF).reshape(rows // SIDE, SIDE, LANES)
+
+    @pl.when(pl.program_id(0) == pl.num_programs(0) - 1)
+    def _():
+        copy.wait()
 
 
 def first_head(rows):
@@ -149,8 +158,9 @@
 
 
 def strided_lines(in_ref, f_ref, wide_ref, bias_ref, add):
+    count = in_ref.shape[2] // 8
     for j in range(4):
-        wide_ref[j] = in_ref[:, j].astype(F32).reshape(SIDE, 4, 8, LANES)
+        wide_ref[j] = in_ref[:, j].astype(F32).reshape(SIDE, count, 8, LANES)
     rows = 8 * SIDE
     bias_ref[...] = same_line(rows, lambda i: i % 8)
     factors = (f_ref[0], f_ref[1])
@@ -161,7 +171,7 @@
             add(j, b, r.reshape(SIDE, 8, LANES))
         return 0
 
-    lax.fori_loop(0, 4, step, 0)
+    lax.fori_loop(0, count, step, 0, unroll=True)
 
 
 def plane_body(in_ref, f_ref, out_ref, wide_ref, bias_ref, bias_x_ref):
@@ -175,7 +185,7 @@
             out_ref[j, pl.ds(4 * b, 4)] = r.reshape(4, 4, 8, LANES)
         return 0
 
-    lax.fori_loop(0, 8, step, 0)
+    lax.fori_loop(0, 8, step, 0, unroll=4)
 
     def add(j, b, r):
         out_ref[j, :, b] += r
@@ -189,7 +199,7 @@
 
     strided_lines(in_ref, f_ref, wide_ref, bias_ref, add)
     for j in range(4):
-        out_ref[:, j] = res_ref[j].reshape(SIDE, SIDE, LANES).astype(BF)
+        out_ref[:, j] = res_ref[j].reshape(SIDE, out_ref.shape[2], LANES).astype(BF)
 
 
 def halves(a):
@@ -198,46 +208,44 @@
 
 
 def combine_body(
-    at_ref, loc_ref, back_ref, proj_ref, normed_ref, gain_ref, w_ref,
+    at_ref, loc_ref, back_ref, normed_ref, gain_ref, w_ref,
     away_ref, keep_ref, small_ref, g_ref, sum_ref,
 ):
     core = places(at_ref)[1]
     step = pl.program_id(0)
     rows = normed_ref.shape[0]
-    total = jnp.zeros((rows, LANES), F32)
     for j in range(4):
         part = loc_ref[j].reshape(rows, LANES) + back_ref[:, j].astype(F32).reshape(rows, LANES)
-        part = part.astype(BF)
         at = (j - 1) % 4
-        g_ref[:, at * LANES : (at + 1) * LANES] = part
-        if j > 0:
-            total += part.astype(F32) * proj_ref[:, j - 1].astype(F32).reshape(rows, LANES)
+        g_ref[:, at * LANES : (at + 1) * LANES] = part.astype(BF)
+
+    @pl.when(step == 0)
+    def _():
+        sum_ref[...] = jnp.zeros_like(sum_ref)
+
+    grads = g_ref[:, : 3 * LANES]
+    total = jnp.zeros((rows, LANES), F32)
+    for i in range(4):
+        spots = [rows_at(2 * i + core, LANES), rows_at(2 * i + 1 - core, LANES)]
+        w = jnp.concatenate([w_ref[s] for s in spots], axis=0)
+        part = dot(grads, w, 1, 1).astype(BF)
+        keep_ref[i] = part[:, :LANES]
+        away_ref[i] = part[:, LANES:]
+        n = jnp.concatenate([normed_ref[:, s] for s in spots], axis=1)
+        both = part.astype(F32) * n.astype(F32)
+        total += both[:, :LANES] + both[:, LANES:]
+        sum_ref[i] += jnp.sum(both.reshape(rows // 8, 8, 2 * LANES), axis=0)
     for i in range(rows // LANES):
         row = jnp.sum(total[i * LANES : (i + 1) * LANES].T, axis=0, keepdims=True)
         small_ref[pl.ds(step * (rows // LANES) + i, 1)] = row
-
-    @pl.when(step == 0)
-    def _():
-        sum_ref[...] = jnp.zeros_like(sum_ref)
-
-    def block(h):
-        w = w_ref[rows_at(h, LANES), : 3 * LANES]
-        part = dot(g_ref[:, : 3 * LANES], w, 1, 1).astype(BF)
-        n = normed_ref[:, rows_at(h, LANES)].astype(F32)
-        return part, jnp.sum((part.astype(F32) * n).reshape(rows // 8, 8, LANES), axis=0)
-
-    for i in range(4):
-        away_ref[i], gain = block(2 * i + 1 - core)
-        sum_ref[i] += gain
-        keep_ref[i], gain = block(2 * i + core)
-        sum_ref[4 + i] += gain
 
     @pl.when(step == pl.num_programs(0) - 1)
     def _():
         for i in range(8):
             h = 2 * (i % 4) + (1 - core if i < 4 else core)
-            gain = jnp.sum(sum_ref[i], axis=0, keepdims=True) / gain_ref[pl.ds(h, 1)]
-            small_ref[8 + i : 9 + i] = gain
+            both = jnp.sum(sum_ref[i % 4], axis=0, keepdims=True)
+            mine = both[:, LANES:] if i < 4 else both[:, :LANES]
+            small_ref[8 + i : 9 + i] = mine / gain_ref[pl.ds(h, 1)]
 
 
 def pair_body(at_ref, got_ref, keep_ref, small_ref, sgot_ref, *refs):
@@ -270,12 +278,7 @@
     return ref[at : at + 8].astype(F32) + ref[at + 8 : at + 16].astype(F32)
 
 
-def weights_body(normed_ref, go_ref, g_ref, gown_ref, t1_ref, t2_ref, t3_ref, out_ref, gsum_ref):
-    gain = gown_ref[...]
-    for ref in (t1_ref, t2_ref, t3_ref):
-        gain = gain + tail_of(ref, 0)
-    gsum_ref[...] = gain
-    tail = jnp.concatenate(halves(gain), axis=0)
+def weights_body(normed_ref, go_ref, g_ref, out_ref):
     three = dot(normed_ref[...], g_ref[:, : 3 * LANES], 0, 0)
     last = dot(go_ref[...], g_ref[:, 3 * LANES :], 0, 0)
     for j in range(4):
@@ -284,7 +287,18 @@
         for zh in range(2):
             at = zh * LANES + j * SIDE
             out_ref[:, at : at + SIDE] = part[zh]
-    out_ref[:, 2 * LANES :] = jnp.broadcast_to(tail[None], (4, 16, LANES))
+
+
+def tail_body(whole_ref, gown_ref, t1_ref, t2_ref, t3_ref, out_ref, buf, sem):
+    del whole_ref
+    gain = gown_ref[...]
+    for ref in (t1_ref, t2_ref, t3_ref):
+        gain = gain + tail_of(ref, 0)
+    tail = jnp.concatenate(halves(gain), axis=0)
+    buf[...] = jnp.broadcast_to(tail[None], (16, 16, LANES))
+    copy = pltpu.make_async_copy(buf, out_ref.at[:, 2 * LANES :], sem)
+    copy.start()
+    copy.wait()
 
 
 def plane_sum_body(at_ref, in_ref, send_ref, own_ref, gain_ref, buf):
@@ -354,14 +368,14 @@
     )(*(stay(w) for w in (query_weight, key_weight, value_weight, out_weight.T)))
     other = lax.ppermute(mine, "slab", OVER_Z)
     spread = call(
-        pair_up_body, far((16, 2 * SIDE, 4 * LANES), BF), in_specs=[SMEM, VMEM, VMEM]
+        pair_up_body, shape((16, 2 * SIDE, 4 * LANES), BF), in_specs=[SMEM, VMEM, VMEM]
     )(at, mine, other)
-    normed, inv = call(
+    early, normed, inv = call(
         norm_stats_body,
-        (far((rows, width), BF), far((rows, LANES), F32)),
+        (shape((rows, width), BF), far((rows, width), BF), far((rows, LANES), F32)),
         grid=(rows // blk,),
         in_specs=[by_rows((blk, width)), whole((1, width))],
-        out_specs=(by_rows((blk, width)), by_rows((blk, LANES))),
+        out_specs=(by_rows((blk, width)), by_rows((blk, width)), by_rows((blk, LANES))),
     )(inputs, norm_gain.reshape(1, width))
     pieces = in_plane(spread)
 
@@ -374,8 +388,12 @@
             by_rows((blk, width)),
             whole((16, 2 * SIDE, 4 * LANES)),
         ],
-        out_specs=(by_rows((blk // SIDE, 4, SIDE, LANES)), whole((width, 4 * LANES))),
-    )(stay(normed), stay(grad_output), pieces)
+        out_specs=(
+            by_rows((blk // SIDE, 4, SIDE, LANES)),
+            pl.BlockSpec(memory_space=pltpu.HBM),
+        ),
+        scratch_shapes=[pltpu.VMEM((width, 4 * LANES), BF), pltpu.SemaphoreType.DMA],
+    )(early, grad_output, pieces)
 
     z_in = lax.all_to_all(proj, "slab", 0, 0, tiled=True)
     big = (4, SIDE, 4, 8, LANES)
@@ -388,14 +406,16 @@
             pltpu.VMEM((256, 256), F32),
             pltpu.VMEM((128, 128), F32),
         ],
-    )(proj, factors)
+    )(stay(proj), factors)
     z_terms = call(
         depth_body,
         far((SIDE, 4, SIDE, LANES), BF),
-        in_specs=[VMEM, SMEM],
+        grid=(2,),
+        in_specs=[pl.BlockSpec((SIDE, 4, 16, LANES), lambda i: (0, 0, i, 0)), SMEM],
+        out_specs=pl.BlockSpec((SIDE, 4, 16, LANES), lambda i: (0, 0, i, 0)),
         scratch_shapes=[
-            pltpu.VMEM(big, F32),
-            pltpu.VMEM(big, F32),
+            pltpu.VMEM((4, SIDE, 2, 8, LANES), F32),
+            pltpu.VMEM((4, SIDE, 2, 8, LANES), F32),
             pltpu.VMEM((256, 256), F32),
         ],
     )(z_in, factors)
@@ -416,14 +436,13 @@
             SMEM,
             pl.BlockSpec((4, lines, 4, 8, LANES), lambda i: (0, i, 0, 0, 0)),
             by_rows((lines, 4, SIDE, LANES)),
-            by_rows((lines, 4, SIDE, LANES)),
             by_rows((blk, width)),
             whole((8, LANES)),
-            whole((width, 4 * LANES)),
+            whole((width, 3 * LANES)),
         ],
         out_specs=(parts4, parts4, whole((16, LANES)), by_rows((blk, 4 * LANES))),
-        scratch_shapes=[pltpu.VMEM((8, 8, LANES), F32)],
-    )(at, stay(local), back, proj, normed, norm_gain.reshape(8, LANES), stay(weights))
+        scratch_shapes=[pltpu.VMEM((4, 8, 2 * LANES), F32)],
+    )(at, stay(local), back, stay(normed), norm_gain.reshape(8, LANES), stay(weights))
 
     swap = [(i, i ^ 1) for i in range(8)]
     got = lax.ppermute(away, "head", swap)
@@ -445,19 +464,26 @@
     for d, s in enumerate(sends[:3]):
         parts.append(lax.ppermute(s, "head", to_zl(d + 1)))
 
-    sent, _ = call(
+    sent = call(
         weights_body,
-        (shape((16, 272, LANES), BF), row8),
+        shape((16, 272, LANES), BF),
         grid=(4,),
         in_specs=[
             pl.BlockSpec((rows, 256), lambda i: (0, i)),
             pl.BlockSpec((rows, 256), lambda i: (0, i)),
             whole((rows, 4 * LANES)),
-            whole((8, LANES)),
-        ]
-        + [whole((16, LANES))] * 3,
-        out_specs=(by_rows((4, 272, LANES)), whole((8, LANES))),
-    )(normed, grad_output, grads, gown, *tinies)
+        ],
+        out_specs=by_rows((4, 272, LANES)),
+    )(normed, grad_output, grads)
+    anywhere = pl.BlockSpec(memory_space=pl.ANY)
+    sent = call(
+        tail_body,
+        shape((16, 272, LANES), BF),
+        in_specs=[anywhere] + [VMEM] * 4,
+        out_specs=anywhere,
+        scratch_shapes=[pltpu.VMEM((16, 16, LANES), BF), pltpu.SemaphoreType.DMA],
+        input_output_aliases={0: 0},
+    )(sent, gown, *tinies)
     send, mine, gain = call(
         plane_sum_body,
         (shape((LANES + 16, LANES), BF), shape((LANES, LANES), F32), row8),

time: 174 us -> 170 us (0.977)
  the two profiles are of different devices: /device:TPU:35 before, /device:TPU:34 now
where the time goes in v4:
time: 170 us; the launch traced here: 169 us
  waiting for transfers between devices  75 us (44%)
  starting transfers between devices  47.4 us (28%)
  Pallas kernels  37.6 us (22%)
  local copies, waits for them, and re-layouts  8.44 us (5%)
    all_to_all x1, waiting for transfers between devices, body(): z_in = lax.all_to_all(proj, 'slab', 0, 0, tiled=True)  28.7 us
    all_to_all x2, waiting for transfers between devices, in_plane(): return lax.all_to_all(a, 'slab', 0, 0, tiled=True, axis_index_groups=PLANES)  19.7 us
    all_to_all x2, starting transfers between devices, in_plane(): return lax.all_to_all(a, 'slab', 0, 0, tiled=True, axis_index_groups=PLANES)  15 us
    ppermute x3, waiting for transfers between devices, body(): parts.append(lax.ppermute(s, 'head', to_zl(d + 1)))  11.4 us
    all_to_all x1, waiting for transfers between devices, body(): back = lax.all_to_all(z_terms, 'slab', 0, 0, tiled=True)  11.2 us
    pallas_call x1, Pallas kernels, body(): call(plane_body, far(big, F32), in_specs=[VMEM, SMEM], scratch_shapes=[pl...  11.1 us
    all_to_all x1, starting transfers between devices, body(): z_in = lax.all_to_all(proj, 'slab', 0, 0, tiled=True)  10.7 us
    unnamed x30, local copies, waits for them, and re-layouts  8.44 us
  transfers between devices with their start and end apart: 14, of which 9 were waited for; matrix products, arithmetic and copies ran while one was open for 0% of the time, Pallas kernels for 12%

profile of v4, /device:TPU:34, one launch (start us, length us, event | category | flops | bytes accessed | tf_op | source)
XLA Modules:
  0.0 169.4 jit_solution(17726567086195682745)
XLA Ops:
  1.4 6.4 %collective-permute-start = (bf16[32,512]{1,0:T(8,128)(2,1)S(1)}, bf16[32,512]{1,0:T(8,128)(2,1)S(1)}, u32[]{:S(2)}, u32[]{:S(2)}) collective-permute-start(bf16[32,512]{1,0:T(8,128)(2,1)S(1)} %shard_map.128.mine_ref), channel_id=1, source_target_pairs={{0,32},{8,40},{16,48},{24,56},{32,0},{40,8},{48,16},{56,24},{64,96... | collective-permute-start | bytes 98312 | tf_op jit(solution)/shard_map/ppermute | solution.py:369
  7.9 1.8 %collective-permute-done.got_ref = bf16[32,512]{1,0:T(8,128)(2,1)S(1)} collective-permute-done((bf16[32,512]{1,0:T(8,128)(2,1)S(1)}, bf16[32,512]{1,0:T(8,128)(2,1)S(1)}, u32[]{:S(2)}, u32[]{:S(2)}) %collective-permute-start) | collective-permute-done | bytes 32800 | tf_op jit(solution)/shard_map/ppermute | solution.py:369
  10.4 1.0 copy-done.4
  11.4 7.6 %all-to-all-start = ((bf16[16,64,512]{2,1,0:T(8,128)(2,1)}), bf16[16,64,512]{2,1,0:T(8,128)(2,1)S(1)}, u32[]{:S(2)}, u32[]{:S(2)}) async-start(bf16[16,64,512]{2,1,0:T(8,128)(2,1)} %copy-done.4), calls=%async_computation | async-start | bytes 2097152 | tf_op jit(solution)/shard_map/all_to_all | solution.py:349
  19.0 1.6 copy-done.1
  20.6 2.4 %shard_map.127 = (bf16[1024,1024]{1,0:T(8,128)(2,1)S(1)}, bf16[1024,1024]{1,0:T(8,128)(2,1)}, f32[1024,128]{1,0:T(8,128)}) custom-call(bf16[1024,1024]{1,0:T(8,128)(2,1)S(1)} %copy-done.1, f32[1,1024]{1,0:T(1,128)S(1)} %bitcast.7), custom_call_target="tpu_custom_call" | custom-call | tf_op jit(solution)/shard_map/pallas_call | solution.py:373
  22.9 1.3 copy-done.5
  24.3 9.1 %all-to-all-done.pieces_ref = bf16[16,64,512]{2,1,0:T(8,128)(2,1)S(1)} async-done(((bf16[16,64,512]{2,1,0:T(8,128)(2,1)}), bf16[16,64,512]{2,1,0:T(8,128)(2,1)S(1)}, u32[]{:S(2)}, u32[]{:S(2)}) %all-to-all-start) | async-done | bytes 1048608 | tf_op jit(solution)/shard_map/all_to_all | solution.py:349
  33.4 1.6 copy-done.6
  35.0 3.2 %shard_map.130 = (bf16[32,4,32,128]{3,2,1,0:T(8,128)(2,1)}, bf16[1024,512]{1,0:T(8,128)(2,1)}) custom-call(bf16[1024,1024]{1,0:T(8,128)(2,1)S(1)} %copy-done.6, bf16[1024,1024]{1,0:T(8,128)(2,1)S(1)} %copy-done, bf16[16,64,512]{2,1,0:T(8,128)(2,1)S(1)} %all-to-all-done.pieces_ref), custom_call_target="tpu_custom_call" | custom-call | tf_op jit(solution)/shard_map/pallas_call | solution.py:382
  38.2 10.7 %all-to-all-start.1 = ((bf16[32,4,32,128]{3,2,1,0:T(8,128)(2,1)}), bf16[32,4,32,128]{3,2,1,0:T(8,128)(2,1)S(1)}, u32[]{:S(2)}, u32[]{:S(2)}) async-start(bf16[32,4,32,128]{3,2,1,0:T(8,128)(2,1)} %get-tuple-element.33.in_ref), calls=%async_computation.1 | async-start | bytes 2097152 | tf_op jit(solution)/shard_map/all_to_all | solution.py:398
  48.9 28.7 %all-to-all-done.1.in_ref = bf16[32,4,32,128]{3,2,1,0:T(8,128)(2,1)S(1)} async-done(((bf16[32,4,32,128]{3,2,1,0:T(8,128)(2,1)}), bf16[32,4,32,128]{3,2,1,0:T(8,128)(2,1)S(1)}, u32[]{:S(2)}, u32[]{:S(2)}) %all-to-all-start.1) | async-done | bytes 1048608 | tf_op jit(solution)/shard_map/all_to_all | solution.py:398
  77.7 5.1 %shard_map.132 = bf16[32,4,32,128]{3,2,1,0:T(8,128)(2,1)} custom-call(bf16[32,4,32,128]{3,2,1,0:T(8,128)(2,1)S(1)} %all-to-all-done.1.in_ref, f32[2]{0:T(128)S(1)} %broadcast_multiply_fusion.f_ref), custom_call_target="tpu_custom_call" | custom-call | tf_op jit(solution)/shard_map/pallas_call | solution.py:410
  82.8 6.4 %all-to-all-start.2 = ((bf16[32,4,32,128]{3,2,1,0:T(8,128)(2,1)}), bf16[32,4,32,128]{3,2,1,0:T(8,128)(2,1)S(1)}, u32[]{:S(2)}, u32[]{:S(2)}) async-start(bf16[32,4,32,128]{3,2,1,0:T(8,128)(2,1)} %shard_map.132), calls=%async_computation.2 | async-start | bytes 2097152 | tf_op jit(solution)/shard_map/all_to_all | solution.py:422
  89.2 11.1 %shard_map.131.loc_ref = f32[4,32,4,8,128]{4,3,2,1,0:T(8,128)} custom-call(bf16[32,4,32,128]{3,2,1,0:T(8,128)(2,1)} %get-tuple-element.33.in_ref, f32[2]{0:T(128)S(1)} %broadcast_multiply_fusion.f_ref), custom_call_target="tpu_custom_call" | custom-call | tf_op jit(solution)/shard_map/pallas_call | solution.py:400
  100.3 11.2 %all-to-all-done.2.back_ref = bf16[32,4,32,128]{3,2,1,0:T(8,128)(2,1)S(1)} async-done(((bf16[32,4,32,128]{3,2,1,0:T(8,128)(2,1)}), bf16[32,4,32,128]{3,2,1,0:T(8,128)(2,1)S(1)}, u32[]{:S(2)}, u32[]{:S(2)}) %all-to-all-start.2) | async-done | bytes 1048608 | tf_op jit(solution)/shard_map/all_to_all | solution.py:422
  111.6 5.0 %shard_map.133 = (bf16[4,1024,128]{2,1,0:T(8,128)(2,1)S(1)}, bf16[4,1024,128]{2,1,0:T(8,128)(2,1)S(1)}, f32[16,128]{1,0:T(8,128)S(1)}, bf16[1024,512]{1,0:T(8,128)(2,1)S(1)}) custom-call(s32[2]{0:T(128)S(1)} %pad_add_fusion.at_ref, f32[4,32,4,8,128]{4,3,2,1,0:T(8,128)} %shard_map.131.loc_ref, bf16[32,4,32,128]{3,2,1,0:T(8,128)(2,1)S(1)} %all-to-all-done.2.back_ref, ...), custom_call_target="tpu_custom_call" | custom-call | tf_op jit(solution)/shard_map/pallas_call | solution.py:426
  117.2 2.2 %collective-permute-done.2.sgot_ref = f32[16,128]{1,0:T(8,128)S(1)} collective-permute-done((f32[16,128]{1,0:T(8,128)S(1)}, f32[16,128]{1,0:T(8,128)S(1)}, u32[]{:S(2)}, u32[]{:S(2)}) %collective-permute-start.2) | collective-permute-done | bytes 8224 | tf_op jit(solution)/shard_map/ppermute | solution.py:449
  119.4 1.0 shard_map.134
  120.4 0.8 copy-done.8
  121.2 1.0 collective-permute-start.6
  122.2 1.7 %collective-permute-start.8 = (bf16[16,128]{1,0:T(8,128)(2,1)S(1)}, bf16[16,128]{1,0:T(8,128)(2,1)S(1)}, u32[]{:S(2)}, u32[]{:S(2)}) collective-permute-start(bf16[16,128]{1,0:T(8,128)(2,1)S(1)} %get-tuple-element.49), channel_id=1, source_target_pairs={{0,6},{1,7},{2,0},{3,1},{4,2},{5,3},{6,4},{7,5},{8,14},{9,15},{10,... | collective-permute-start | bytes 12296 | tf_op jit(solution)/shard_map/ppermute | solution.py:462
  123.9 3.8 %shard_map.135.whole_ref = bf16[16,272,128]{2,1,0:T(8,128)(2,1)} custom-call(bf16[1024,1024]{1,0:T(8,128)(2,1)S(1)} %copy-done.3, bf16[1024,1024]{1,0:T(8,128)(2,1)S(1)} %copy-done, bf16[1024,512]{1,0:T(8,128)(2,1)S(1)} %get-tuple-element.45.g_ref), custom_call_target="tpu_custom_call" | custom-call | tf_op jit(solution)/shard_map/pallas_call | solution.py:467
  128.5 7.4 %all-to-all-start.3 = ((bf16[16,272,128]{2,1,0:T(8,128)(2,1)}), bf16[16,272,128]{2,1,0:T(8,128)(2,1)S(1)}, u32[]{:S(2)}, u32[]{:S(2)}) async-start(bf16[16,272,128]{2,1,0:T(8,128)(2,1)} %shard_map.136), calls=%async_computation.3 | async-start | bytes 2228224 | tf_op jit(solution)/shard_map/all_to_all | solution.py:349
  136.6 4.3 %collective-permute-start.4 = (bf16[1040,128]{1,0:T(8,128)(2,1)}, bf16[1040,128]{1,0:T(8,128)(2,1)}, u32[]{:S(2)}, u32[]{:S(2)}) collective-permute-start(bf16[1040,128]{1,0:T(8,128)(2,1)} %copy-done.12), channel_id=1, source_target_pairs={{0,4},{1,5},{2,6},{3,7},{4,0},{5,1},{6,2},{7,3},{8,12},{9,13},{10,... | collective-permute-start | bytes 798728 | tf_op jit(solution)/shard_map/ppermute | solution.py:465
  140.8 10.5 %all-to-all-done.3.in_ref = bf16[16,272,128]{2,1,0:T(8,128)(2,1)S(1)} async-done(((bf16[16,272,128]{2,1,0:T(8,128)(2,1)}), bf16[16,272,128]{2,1,0:T(8,128)(2,1)S(1)}, u32[]{:S(2)}, u32[]{:S(2)}) %all-to-all-start.3) | async-done | bytes 1114144 | tf_op jit(solution)/shard_map/all_to_all | solution.py:349
  152.7 2.8 %collective-permute-done.3.r1_ref = bf16[1040,128]{1,0:T(8,128)(2,1)S(1)} collective-permute-done((bf16[1040,128]{1,0:T(8,128)(2,1)}, bf16[1040,128]{1,0:T(8,128)(2,1)S(1)}, u32[]{:S(2)}, u32[]{:S(2)}) %collective-permute-start.3) | collective-permute-done | bytes 266272 | tf_op jit(solution)/shard_map/ppermute | solution.py:465
  155.6 4.9 %collective-permute-done.4.r2_ref = bf16[1040,128]{1,0:T(8,128)(2,1)} collective-permute-done((bf16[1040,128]{1,0:T(8,128)(2,1)}, bf16[1040,128]{1,0:T(8,128)(2,1)}, u32[]{:S(2)}, u32[]{:S(2)}) %collective-permute-start.4) | collective-permute-done | bytes 266272 | tf_op jit(solution)/shard_map/ppermute | solution.py:465
  160.5 3.7 %collective-permute-done.5.r3_ref = bf16[1040,128]{1,0:T(8,128)(2,1)} collective-permute-done((bf16[1040,128]{1,0:T(8,128)(2,1)}, bf16[1040,128]{1,0:T(8,128)(2,1)}, u32[]{:S(2)}, u32[]{:S(2)}) %collective-permute-start.5) | collective-permute-done | bytes 266272 | tf_op jit(solution)/shard_map/ppermute | solution.py:465
  164.1 1.0 copy-done.7
  165.2 1.0 copy-done.9
  166.2 2.5 %norm_back.1 = bf16[1024,128]{1,0:T(8,128)(2,1)} custom-call(s32[2]{0:T(128)S(1)} %pad_add_fusion.at_ref, bf16[1024,1024]{1,0:T(8,128)(2,1)S(1)} %copy-done.2, f32[1,1024]{1,0:T(1,128)S(1)} %bitcast.9, f32[1024,128]{1,0:T(8,128)S(1)} %copy-done.9, bf16[1040,128]{1,0:T(8,128)(2,1)S(1)} %collective-permute-done.3.r1_ref, ...), custom_call_target="tpu_custom_call" | custom-call | tf_op jit(solution)/shard_map/norm_back/pallas_call | solution.py:500
  (41 shorter events, 5.5 us)
Async XLA Ops:
  0.6 18.3 %copy-start.10 = (f32[1024]{0:T(1024)S(1)}, f32[1024]{0:T(1024)}, u32[]{:S(2)}) copy-start(f32[1024]{0:T(1024)} %param.9) | copy-start | bytes 12292
  1.4 8.3 %collective-permute-start = (bf16[32,512]{1,0:T(8,128)(2,1)S(1)}, bf16[32,512]{1,0:T(8,128)(2,1)S(1)}, u32[]{:S(2)}, u32[]{:S(2)}) collective-permute-start(bf16[32,512]{1,0:T(8,128)(2,1)S(1)} %shard_map.128.mine_ref), channel_id=1, source_target_pairs={{0,32},{8,40},{16,48},{24,56},{32,0},{40,8},{48,16},{56,24},{64,96... | collective-permute-start | bytes 98312 | tf_op jit(solution)/shard_map/ppermute | solution.py:369
  10.3 1.0 copy-start.4
  11.4 22.0 %copy-start = (bf16[1024,1024]{1,0:T(8,128)(2,1)S(1)}, bf16[1024,1024]{1,0:T(8,128)(2,1)}, u32[]{:S(2)}) copy-start(bf16[1024,1024]{1,0:T(8,128)(2,1)} %go_ref.3) | copy-start | bytes 6291460
  11.4 22.0 %all-to-all-start = ((bf16[16,64,512]{2,1,0:T(8,128)(2,1)}), bf16[16,64,512]{2,1,0:T(8,128)(2,1)S(1)}, u32[]{:S(2)}, u32[]{:S(2)}) async-start(bf16[16,64,512]{2,1,0:T(8,128)(2,1)} %copy-done.4), calls=%async_computation | async-start | bytes 2097152 | tf_op jit(solution)/shard_map/all_to_all | solution.py:349
  19.0 1.6 copy-start.1
  22.9 1.3 copy-start.5
  33.4 1.6 copy-start.6
  38.2 10.7 %copy-start.14 = (f32[2]{0:T(128)S(1)}, f32[2]{0:T(128)}, u32[]{:S(2)}) copy-start(f32[2]{0:T(128)} %param.14) | copy-start | bytes 28
  38.2 39.4 %all-to-all-start.1 = ((bf16[32,4,32,128]{3,2,1,0:T(8,128)(2,1)}), bf16[32,4,32,128]{3,2,1,0:T(8,128)(2,1)S(1)}, u32[]{:S(2)}, u32[]{:S(2)}) async-start(bf16[32,4,32,128]{3,2,1,0:T(8,128)(2,1)} %get-tuple-element.33.in_ref), calls=%async_computation.1 | async-start | bytes 2097152 | tf_op jit(solution)/shard_map/all_to_all | solution.py:398
  82.8 28.8 %all-to-all-start.2 = ((bf16[32,4,32,128]{3,2,1,0:T(8,128)(2,1)}), bf16[32,4,32,128]{3,2,1,0:T(8,128)(2,1)S(1)}, u32[]{:S(2)}, u32[]{:S(2)}) async-start(bf16[32,4,32,128]{3,2,1,0:T(8,128)(2,1)} %shard_map.132), calls=%async_computation.2 | async-start | bytes 2097152 | tf_op jit(solution)/shard_map/all_to_all | solution.py:422
  116.6 7.3 %copy-start.3 = (bf16[1024,1024]{1,0:T(8,128)(2,1)S(1)}, bf16[1024,1024]{1,0:T(8,128)(2,1)}, u32[]{:S(2)}) copy-start(bf16[1024,1024]{1,0:T(8,128)(2,1)} %get-tuple-element.34.normed_ref) | copy-start | bytes 6291460
  116.6 2.8 %collective-permute-start.1 = (bf16[4,1024,128]{2,1,0:T(8,128)(2,1)S(1)}, bf16[4,1024,128]{2,1,0:T(8,128)(2,1)S(1)}, u32[]{:S(2)}, u32[]{:S(2)}) collective-permute-start(bf16[4,1024,128]{2,1,0:T(8,128)(2,1)S(1)} %get-tuple-element.36), channel_id=1, source_target_pairs={{0,1},{1,0},{2,3},{3,2},{4,5},{5,4},{6,7},{7,6},{8,9},{9,8},{10,11... | collective-permute-start | bytes 3145736 | tf_op jit(solution)/shard_map/ppermute | solution.py:448
  116.7 2.7 %collective-permute-start.2 = (f32[16,128]{1,0:T(8,128)S(1)}, f32[16,128]{1,0:T(8,128)S(1)}, u32[]{:S(2)}, u32[]{:S(2)}) collective-permute-start(f32[16,128]{1,0:T(8,128)S(1)} %get-tuple-element.38.small_ref), channel_id=1, source_target_pairs={{0,1},{1,0},{2,3},{3,2},{4,5},{5,4},{6,7},{7,6},{8,9},{9,8},{10,11... | collective-permute-start | bytes 24584 | tf_op jit(solution)/shard_map/ppermute | solution.py:449
  120.3 0.8 copy-start.8
  121.2 6.6 %copy-start.11 = (bf16[1040,128]{1,0:T(8,128)(2,1)}, bf16[1040,128]{1,0:T(8,128)(2,1)S(1)}, u32[]{:S(2)}) copy-start(bf16[1040,128]{1,0:T(8,128)(2,1)S(1)} %get-tuple-element.42) | copy-start | bytes 798724
  121.2 6.6 %copy-start.12 = (bf16[1040,128]{1,0:T(8,128)(2,1)}, bf16[1040,128]{1,0:T(8,128)(2,1)S(1)}, u32[]{:S(2)}) copy-start(bf16[1040,128]{1,0:T(8,128)(2,1)S(1)} %get-tuple-element.41) | copy-start | bytes 798724
  121.2 6.6 %copy-start.13 = (bf16[1040,128]{1,0:T(8,128)(2,1)}, bf16[1040,128]{1,0:T(8,128)(2,1)S(1)}, u32[]{:S(2)}) copy-start(bf16[1040,128]{1,0:T(8,128)(2,1)S(1)} %get-tuple-element.40) | copy-start | bytes 798724
  121.2 6.6 %collective-permute-start.6 = (bf16[16,128]{1,0:T(8,128)(2,1)S(1)}, bf16[16,128]{1,0:T(8,128)(2,1)S(1)}, u32[]{:S(2)}, u32[]{:S(2)}) collective-permute-start(bf16[16,128]{1,0:T(8,128)(2,1)S(1)} %get-tuple-element.47), channel_id=1, source_target_pairs={{0,2},{1,3},{2,4},{3,5},{4,6},{5,7},{6,0},{7,1},{8,10},{9,11},{10,... | collective-permute-start | bytes 12296 | tf_op jit(solution)/shard_map/ppermute | solution.py:462
  122.2 5.6 %collective-permute-start.7 = (bf16[16,128]{1,0:T(8,128)(2,1)S(1)}, bf16[16,128]{1,0:T(8,128)(2,1)S(1)}, u32[]{:S(2)}, u32[]{:S(2)}) collective-permute-start(bf16[16,128]{1,0:T(8,128)(2,1)S(1)} %get-tuple-element.48), channel_id=1, source_target_pairs={{0,4},{1,5},{2,6},{3,7},{4,0},{5,1},{6,2},{7,3},{8,12},{9,13},{10,... | collective-permute-start | bytes 12296 | tf_op jit(solution)/shard_map/ppermute | solution.py:462
  122.2 5.6 %collective-permute-start.8 = (bf16[16,128]{1,0:T(8,128)(2,1)S(1)}, bf16[16,128]{1,0:T(8,128)(2,1)S(1)}, u32[]{:S(2)}, u32[]{:S(2)}) collective-permute-start(bf16[16,128]{1,0:T(8,128)(2,1)S(1)} %get-tuple-element.49), channel_id=1, source_target_pairs={{0,6},{1,7},{2,0},{3,1},{4,2},{5,3},{6,4},{7,5},{8,14},{9,15},{10,... | collective-permute-start | bytes 12296 | tf_op jit(solution)/shard_map/ppermute | solution.py:462
  128.4 35.7 %copy-start.2 = (bf16[1024,1024]{1,0:T(8,128)(2,1)S(1)}, bf16[1024,1024]{1,0:T(8,128)(2,1)}, u32[]{:S(2)}) copy-start(bf16[1024,1024]{1,0:T(8,128)(2,1)} %x_ref.3) | copy-start | bytes 6291460
  128.5 22.9 %all-to-all-start.3 = ((bf16[16,272,128]{2,1,0:T(8,128)(2,1)}), bf16[16,272,128]{2,1,0:T(8,128)(2,1)S(1)}, u32[]{:S(2)}, u32[]{:S(2)}) async-start(bf16[16,272,128]{2,1,0:T(8,128)(2,1)} %shard_map.136), calls=%async_computation.3 | async-start | bytes 2228224 | tf_op jit(solution)/shard_map/all_to_all | solution.py:349
  135.8 19.8 %collective-permute-start.3 = (bf16[1040,128]{1,0:T(8,128)(2,1)}, bf16[1040,128]{1,0:T(8,128)(2,1)S(1)}, u32[]{:S(2)}, u32[]{:S(2)}) collective-permute-start(bf16[1040,128]{1,0:T(8,128)(2,1)} %copy-done.13), channel_id=1, source_target_pairs={{0,2},{1,3},{2,4},{3,5},{4,6},{5,7},{6,0},{7,1},{8,10},{9,11},{10,... | collective-permute-start | bytes 798728 | tf_op jit(solution)/shard_map/ppermute | solution.py:465
  136.6 23.9 %collective-permute-start.4 = (bf16[1040,128]{1,0:T(8,128)(2,1)}, bf16[1040,128]{1,0:T(8,128)(2,1)}, u32[]{:S(2)}, u32[]{:S(2)}) collective-permute-start(bf16[1040,128]{1,0:T(8,128)(2,1)} %copy-done.12), channel_id=1, source_target_pairs={{0,4},{1,5},{2,6},{3,7},{4,0},{5,1},{6,2},{7,3},{8,12},{9,13},{10,... | collective-permute-start | bytes 798728 | tf_op jit(solution)/shard_map/ppermute | solution.py:465
  140.8 23.3 %collective-permute-start.5 = (bf16[1040,128]{1,0:T(8,128)(2,1)}, bf16[1040,128]{1,0:T(8,128)(2,1)}, u32[]{:S(2)}, u32[]{:S(2)}) collective-permute-start(bf16[1040,128]{1,0:T(8,128)(2,1)} %copy-done.11), channel_id=1, source_target_pairs={{0,6},{1,7},{2,0},{3,1},{4,2},{5,3},{6,4},{7,5},{8,14},{9,15},{10,... | collective-permute-start | bytes 798728 | tf_op jit(solution)/shard_map/ppermute | solution.py:465
  152.1 16.7 %collective-permute-start.9 = (bf16[144,128]{1,0:T(8,128)(2,1)S(1)}, bf16[144,128]{1,0:T(8,128)(2,1)S(1)}, u32[]{:S(2)}, u32[]{:S(2)}) collective-permute-start(bf16[144,128]{1,0:T(8,128)(2,1)S(1)} %get-tuple-element.51), channel_id=1, source_target_pairs={{0,32},{8,40},{16,48},{24,56},{32,0},{40,8},{48,16},{56,24},{64,96... | collective-permute-start | bytes 110600 | tf_op jit(solution)/shard_map/ppermute | solution.py:497
  164.1 1.0 copy-start.7
  165.2 1.0 copy-start.9

commit v5 on v4

--- a/solution.py
+++ b/solution.py
@@ -123,32 +123,43 @@
     return jnp.where(first_head(rows), a[:rows], a[rows:])
 
 
-def attend(q, k, v, g, factors, bias):
-    rows = q.shape[0]
-    k2, v2 = stacked(k), stacked(v)
-    s = dot(q, k2, 1, 1)
-    dp = dot(g, v2, 1, 1)
-    probs = []
-    for h in range(2):
-        sh = s[:, h * rows : (h + 1) * rows] * factors[h] + bias
-        top = jnp.max(sh, axis=1, keepdims=True)
-        e = jnp.exp(sh - top)
-        probs.append(e / jnp.sum(e, axis=1, keepdims=True))
-    pb = jnp.concatenate([p.astype(BF) for p in probs], axis=1)
-    out = dot(pb, v2, 1, 0)
-    go = g.astype(F32) * out
+def attend(blocks, factors, bias):
+    rows = bias.shape[0]
     keep = first_head(rows)
-    grads = []
-    for h in range(2):
-        mine = jnp.where(keep, go, 0.0) if h == 0 else jnp.where(keep, 0.0, go)
-        delta = jnp.sum(mine, axis=1, keepdims=True)
-        dh = dp[:, h * rows : (h + 1) * rows]
-        grads.append((probs[h] * (dh - delta) * factors[h]).astype(BF))
-    ds = jnp.concatenate(grads, axis=1)
-    gq = dot(ds, k2, 1, 0)
-    gk = folded(dot(ds, q, 0, 0))
-    gv = folded(dot(pb, g, 0, 0))
-    return out, gq, gk, gv
+    cut = [slice(0, rows), slice(rows, 2 * rows)]
+    k2 = [stacked(k) for _, k, _, _ in blocks]
+    v2 = [stacked(v) for _, _, v, _ in blocks]
+    s = [dot(blk[0], k, 1, 1) for blk, k in zip(blocks, k2)]
+    dp = [dot(blk[3], v, 1, 1) for blk, v in zip(blocks, v2)]
+    s = [[m[:, c] * f + bias for c, f in zip(cut, factors)] for m in s]
+    top = [[jnp.max(m, axis=1, keepdims=True) for m in pair] for pair in s]
+    e = [[jnp.exp(m - t) for m, t in zip(*both)] for both in zip(s, top)]
+    total = [[1.0 / jnp.sum(m, axis=1, keepdims=True) for m in pair] for pair in e]
+    p = [[m * t for m, t in zip(*both)] for both in zip(e, total)]
+    pb = [jnp.concatenate([m.astype(BF) for m in pair], axis=1) for pair in p]
+    out = [dot(m, v, 1, 0) for m, v in zip(pb, v2)]
+    go = [blk[3].astype(F32) * o for blk, o in zip(blocks, out)]
+    delta = [
+        [
+            jnp.sum(jnp.where(keep, m, 0.0), axis=1, keepdims=True),
+            jnp.sum(jnp.where(keep, 0.0, m), axis=1, keepdims=True),
+        ]
+        for m in go
+    ]
+    ds = [
+        jnp.concatenate(
+            [
+                (ph * (d[:, c] - t) * f).astype(BF)
+                for ph, t, c, f in zip(pair, deltas, cut, factors)
+            ],
+            axis=1,
+        )
+        for pair, d, deltas in zip(p, dp, delta)
+    ]
+    gv = [folded(dot(m, blk[3], 0, 0)) for m, blk in zip(pb, blocks)]
+    gq = [dot(m, k, 1, 0) for m, k in zip(ds, k2)]
+    gk = [folded(dot(m, blk[0], 0, 0)) for m, blk in zip(ds, blocks)]
+    return list(zip(out, gq, gk, gv))
 
 
 def same_line(rows, line):
@@ -167,7 +178,7 @@
 
     def step(b, _):
         parts = [wide_ref[j, :, b].reshape(rows, LANES).astype(BF) for j in range(4)]
-        for j, r in enumerate(attend(*parts, factors, bias_ref[...])):
+        for j, r in enumerate(attend([parts], factors, bias_ref[...])[0]):
             add(j, b, r.reshape(SIDE, 8, LANES))
         return 0
 
@@ -181,7 +192,7 @@
 
     def step(b, _):
         parts = [in_ref[pl.ds(4 * b, 4), j].reshape(rows, LANES) for j in range(4)]
-        for j, r in enumerate(attend(*parts, factors, bias_x_ref[...])):
+        for j, r in enumerate(attend([parts], factors, bias_x_ref[...])[0]):
             out_ref[j, pl.ds(4 * b, 4)] = r.reshape(4, 4, 8, LANES)
         return 0
 
@@ -193,13 +204,23 @@
     strided_lines(in_ref, f_ref, wide_ref, bias_ref, add)
 
 
-def depth_body(in_ref, f_ref, out_ref, wide_ref, res_ref, bias_ref):
-    def add(j, b, r):
-        res_ref[j, :, b] = r
-
-    strided_lines(in_ref, f_ref, wide_ref, bias_ref, add)
-    for j in range(4):
-        out_ref[:, j] = res_ref[j].reshape(SIDE, out_ref.shape[2], LANES).astype(BF)
+def depth_body(in_ref, f_ref, out_ref, flat_ref, res_ref, bias_ref):
+    across = in_ref.shape[2]
+    for j in range(4):
+        flat_ref[j] = in_ref[:, j].astype(F32).reshape(SIDE * across, LANES)
+    bias_ref[...] = same_line(4 * SIDE, lambda i: i // SIDE)
+    factors = (f_ref[0], f_ref[1])
+    spots = [[pl.ds(4 * b + i, SIDE, across) for i in range(4)] for b in range(across // 4)]
+    blocks = [
+        [jnp.concatenate([flat_ref[j, s] for s in four], axis=0).astype(BF) for j in range(4)]
+        for four in spots
+    ]
+    for four, results in zip(spots, attend(blocks, factors, bias_ref[...])):
+        for j, r in enumerate(results):
+            for i, s in enumerate(four):
+                res_ref[j, s] = r[i * SIDE : (i + 1) * SIDE]
+    for j in range(4):
+        out_ref[:, j] = res_ref[j].reshape(SIDE, across, LANES).astype(BF)
 
 
 def halves(a):
@@ -209,11 +230,12 @@
 
 def combine_body(
     at_ref, loc_ref, back_ref, normed_ref, gain_ref, w_ref,
-    away_ref, keep_ref, small_ref, g_ref, sum_ref,
+    away_ref, keep_ref, small_ref, g_ref, kept_ref, sum_ref,
 ):
     core = places(at_ref)[1]
     step = pl.program_id(0)
     rows = normed_ref.shape[0]
+    kept_ref[...] = normed_ref[...]
     for j in range(4):
         part = loc_ref[j].reshape(rows, LANES) + back_ref[:, j].astype(F32).reshape(rows, LANES)
         at = (j - 1) % 4
@@ -283,10 +305,11 @@
     last = dot(go_ref[...], g_ref[:, 3 * LANES :], 0, 0)
     for j in range(4):
         part = three[:, j * LANES : (j + 1) * LANES] if j < 3 else last
-        part = part.astype(BF).reshape(2, 4, SIDE, LANES)
-        for zh in range(2):
-            at = zh * LANES + j * SIDE
-            out_ref[:, at : at + SIDE] = part[zh]
+        part = part.astype(BF).reshape(2, 2, 4, SIDE, LANES)
+        for x in range(2):
+            for zh in range(2):
+                at = zh * LANES + j * SIDE
+                out_ref[4 * x : 4 * x + 4, at : at + SIDE] = part[x, zh]
 
 
 def tail_body(whole_ref, gown_ref, t1_ref, t2_ref, t3_ref, out_ref, buf, sem):
@@ -301,17 +324,24 @@
     copy.wait()
 
 
-def plane_sum_body(at_ref, in_ref, send_ref, own_ref, gain_ref, buf):
+def sum_over(in_ref, at):
+    acc = in_ref[0, at].astype(F32)
+    for i in range(1, 16):
+        acc = acc + in_ref[i, at].astype(F32)
+    return acc
+
+
+def plane_sum_body(at_ref, in_ref, send_ref, gain_ref):
     zh = places(at_ref)[3]
-    acc = in_ref[0].astype(F32)
-    for i in range(1, 16):
-        acc = acc + in_ref[i].astype(F32)
-    buf[...] = acc
-    gain = acc[2 * LANES : 2 * LANES + 8] + acc[2 * LANES + 8 :]
+    gain = sum_over(in_ref, slice(2 * LANES, 2 * LANES + 16))
+    gain = gain[:8] + gain[8:]
     gain_ref[...] = gain
-    send_ref[:LANES] = buf[rows_at(1 - zh, LANES)].astype(BF)
+    send_ref[:LANES] = sum_over(in_ref, rows_at(1 - zh, LANES)).astype(BF)
     send_ref[LANES:] = jnp.concatenate(halves(gain), axis=0)
-    own_ref[...] = buf[rows_at(zh, LANES)]
+
+
+def own_sum_body(at_ref, in_ref, own_ref):
+    own_ref[...] = sum_over(in_ref, rows_at(places(at_ref)[3], LANES))
 
 
 def last_body(own_ref, got_ref, gain_ref, q_ref, k_ref, v_ref, o_ref, gout_ref, *, scale):
@@ -379,17 +409,18 @@
     )(inputs, norm_gain.reshape(1, width))
     pieces = in_plane(spread)
 
+    wide = 2 * blk
     proj, weights = call(
         project_body,
         (far((SIDE, 4, SIDE, LANES), BF), far((width, 4 * LANES), BF)),
-        grid=(rows // blk,),
+        grid=(rows // wide,),
         in_specs=[
-            by_rows((blk, width)),
-            by_rows((blk, width)),
+            by_rows((wide, width)),
+            by_rows((wide, width)),
             whole((16, 2 * SIDE, 4 * LANES)),
         ],
         out_specs=(
-            by_rows((blk // SIDE, 4, SIDE, LANES)),
+            by_rows((wide // SIDE, 4, SIDE, LANES)),
             pl.BlockSpec(memory_space=pltpu.HBM),
         ),
         scratch_shapes=[pltpu.VMEM((width, 4 * LANES), BF), pltpu.SemaphoreType.DMA],
@@ -414,22 +445,23 @@
         in_specs=[pl.BlockSpec((SIDE, 4, 16, LANES), lambda i: (0, 0, i, 0)), SMEM],
         out_specs=pl.BlockSpec((SIDE, 4, 16, LANES), lambda i: (0, 0, i, 0)),
         scratch_shapes=[
-            pltpu.VMEM((4, SIDE, 2, 8, LANES), F32),
-            pltpu.VMEM((4, SIDE, 2, 8, LANES), F32),
-            pltpu.VMEM((256, 256), F32),
+            pltpu.VMEM((4, SIDE * 16, LANES), F32),
+            pltpu.VMEM((4, SIDE * 16, LANES), F32),
+            pltpu.VMEM((128, 128), F32),
         ],
     )(z_in, factors)
     back = lax.all_to_all(z_terms, "slab", 0, 0, tiled=True)
 
     lines = blk // SIDE
     parts4 = pl.BlockSpec((4, blk, LANES), lambda i: (0, i, 0))
-    away, keep, small, grads = call(
+    away, keep, small, grads, early = call(
         combine_body,
         (
             shape((4, TOK, LANES), BF),
             shape((4, TOK, LANES), BF),
             shape((16, LANES), F32),
             shape((TOK, 4 * LANES), BF),
+            shape((rows, width), BF),
         ),
         grid=(rows // blk,),
         in_specs=[
@@ -440,7 +472,13 @@
             whole((8, LANES)),
             whole((width, 3 * LANES)),
         ],
-        out_specs=(parts4, parts4, whole((16, LANES)), by_rows((blk, 4 * LANES))),
+        out_specs=(
+            parts4,
+            parts4,
+            whole((16, LANES)),
+            by_rows((blk, 4 * LANES)),
+            by_rows((blk, width)),
+        ),
         scratch_shapes=[pltpu.VMEM((4, 8, 2 * LANES), F32)],
     )(at, stay(local), back, stay(normed), norm_gain.reshape(8, LANES), stay(weights))
 
@@ -467,14 +505,14 @@
     sent = call(
         weights_body,
         shape((16, 272, LANES), BF),
-        grid=(4,),
+        grid=(2,),
         in_specs=[
-            pl.BlockSpec((rows, 256), lambda i: (0, i)),
-            pl.BlockSpec((rows, 256), lambda i: (0, i)),
+            pl.BlockSpec((rows, 512), lambda i: (0, i)),
+            pl.BlockSpec((rows, 512), lambda i: (0, i)),
             whole((rows, 4 * LANES)),
         ],
-        out_specs=by_rows((4, 272, LANES)),
-    )(normed, grad_output, grads)
+        out_specs=by_rows((8, 272, LANES)),
+    )(early, grad_output, grads)
     anywhere = pl.BlockSpec(memory_space=pl.ANY)
     sent = call(
         tail_body,
@@ -484,17 +522,19 @@
         scratch_shapes=[pltpu.VMEM((16, 16, LANES), BF), pltpu.SemaphoreType.DMA],
         input_output_aliases={0: 0},
     )(sent, gown, *tinies)
-    send, mine, gain = call(
-        plane_sum_body,
-        (shape((LANES + 16, LANES), BF), shape((LANES, LANES), F32), row8),
-        in_specs=[SMEM, VMEM],
-        scratch_shapes=[pltpu.VMEM((272, LANES), F32)],
-    )(at, in_plane(sent))
+    pieces = in_plane(sent)
+    send, gain = call(
+        plane_sum_body, (shape((LANES + 16, LANES), BF), row8), in_specs=[SMEM, VMEM]
+    )(at, pieces)
+    other = lax.ppermute(send, "slab", OVER_Z)
+    mine = call(
+        own_sum_body, shape((LANES, LANES), F32), in_specs=[SMEM, VMEM]
+    )(at, pieces)
     part = shape((SIDE, LANES), F32)
     gqw, gkw, gvw, gow, ggain = call(
         functools.partial(last_body, scale=1.0 / math.sqrt(rows * SIDE)),
         (part, part, part, part, shape((1, LANES), F32)),
-    )(mine, lax.ppermute(send, "slab", OVER_Z), gain)
+    )(mine, other, gain)
 
     all_of = lambda dims: pl.BlockSpec(dims, lambda i, h: (0,) * len(dims))
     grad_inputs = pl.pallas_call(

time: 170 us -> 168 us (0.988)
  Pallas kernels: 37.6 us -> 35.9 us
    unnamed x30 -> x28, local copies, waits for them, and re-layouts: 8.44 us -> 7.65 us
    pallas_call x2 -> x3, Pallas kernels: 4.52 us -> 4.5 us  [the longest x1 3.24 us: body(): call(weights_body, shape((16, 272, LANES), BF), grid=(2,), in_specs=[pl.B...]
where the time goes in v5:
time: 168 us; the launch traced here: 167 us
  waiting for transfers between devices  75.2 us (45%)
  starting transfers between devices  47.9 us (29%)
  Pallas kernels  35.9 us (21%)
  local copies, waits for them, and re-layouts  7.65 us (5%)
    all_to_all x1, waiting for transfers between devices, body(): z_in = lax.all_to_all(proj, 'slab', 0, 0, tiled=True)  28.7 us
    all_to_all x2, waiting for transfers between devices, in_plane(): return lax.all_to_all(a, 'slab', 0, 0, tiled=True, axis_index_groups=PLANES)  19.3 us
    all_to_all x2, starting transfers between devices, in_plane(): return lax.all_to_all(a, 'slab', 0, 0, tiled=True, axis_index_groups=PLANES)  15 us
    all_to_all x1, waiting for transfers between devices, body(): back = lax.all_to_all(z_terms, 'slab', 0, 0, tiled=True)  11.6 us
    ppermute x3, waiting for transfers between devices, body(): parts.append(lax.ppermute(s, 'head', to_zl(d + 1)))  11.5 us
    pallas_call x1, Pallas kernels, body(): call(plane_body, far(big, F32), in_specs=[VMEM, SMEM], scratch_shapes=[pl...  10.7 us
    all_to_all x1, starting transfers between devices, body(): z_in = lax.all_to_all(proj, 'slab', 0, 0, tiled=True)  10.7 us
    unnamed x28, local copies, waits for them, and re-layouts  7.65 us
  transfers between devices with their start and end apart: 14, of which 9 were waited for; matrix products, arithmetic and copies ran while one was open for 0% of the time, Pallas kernels for 12%

profile of v5, /device:TPU:34, one launch (start us, length us, event | category | flops | bytes accessed | tf_op | source)
XLA Modules:
  0.0 167.5 jit_solution(16695798417825851638)
XLA Ops:
  1.4 6.4 %collective-permute-start = (bf16[32,512]{1,0:T(8,128)(2,1)S(1)}, bf16[32,512]{1,0:T(8,128)(2,1)S(1)}, u32[]{:S(2)}, u32[]{:S(2)}) collective-permute-start(bf16[32,512]{1,0:T(8,128)(2,1)S(1)} %shard_map.128.mine_ref), channel_id=1, source_target_pairs={{0,32},{8,40},{16,48},{24,56},{32,0},{40,8},{48,16},{56,24},{64,96... | collective-permute-start | bytes 98312 | tf_op jit(solution)/shard_map/ppermute | solution.py:399
  7.9 1.8 %collective-permute-done.got_ref = bf16[32,512]{1,0:T(8,128)(2,1)S(1)} collective-permute-done((bf16[32,512]{1,0:T(8,128)(2,1)S(1)}, bf16[32,512]{1,0:T(8,128)(2,1)S(1)}, u32[]{:S(2)}, u32[]{:S(2)}) %collective-permute-start) | collective-permute-done | bytes 32800 | tf_op jit(solution)/shard_map/ppermute | solution.py:399
  10.4 1.0 copy-done.3
  11.4 7.6 %all-to-all-start = ((bf16[16,64,512]{2,1,0:T(8,128)(2,1)}), bf16[16,64,512]{2,1,0:T(8,128)(2,1)S(1)}, u32[]{:S(2)}, u32[]{:S(2)}) async-start(bf16[16,64,512]{2,1,0:T(8,128)(2,1)} %copy-done.3), calls=%async_computation | async-start | bytes 2097152 | tf_op jit(solution)/shard_map/all_to_all | solution.py:379
  19.0 1.6 copy-done.1
  20.6 2.4 %shard_map.127 = (bf16[1024,1024]{1,0:T(8,128)(2,1)S(1)}, bf16[1024,1024]{1,0:T(8,128)(2,1)}, f32[1024,128]{1,0:T(8,128)}) custom-call(bf16[1024,1024]{1,0:T(8,128)(2,1)S(1)} %copy-done.1, f32[1,1024]{1,0:T(1,128)S(1)} %bitcast.7), custom_call_target="tpu_custom_call" | custom-call | tf_op jit(solution)/shard_map/pallas_call | solution.py:403
  23.0 1.3 copy-done.4
  24.3 9.1 %all-to-all-done.pieces_ref = bf16[16,64,512]{2,1,0:T(8,128)(2,1)S(1)} async-done(((bf16[16,64,512]{2,1,0:T(8,128)(2,1)}), bf16[16,64,512]{2,1,0:T(8,128)(2,1)S(1)}, u32[]{:S(2)}, u32[]{:S(2)}) %all-to-all-start) | async-done | bytes 1048608 | tf_op jit(solution)/shard_map/all_to_all | solution.py:379
  33.4 1.6 copy-done.5
  35.0 2.9 %shard_map.130 = (bf16[32,4,32,128]{3,2,1,0:T(8,128)(2,1)}, bf16[1024,512]{1,0:T(8,128)(2,1)}) custom-call(bf16[1024,1024]{1,0:T(8,128)(2,1)S(1)} %copy-done.5, bf16[1024,1024]{1,0:T(8,128)(2,1)S(1)} %copy-done, bf16[16,64,512]{2,1,0:T(8,128)(2,1)S(1)} %all-to-all-done.pieces_ref), custom_call_target="tpu_custom_call" | custom-call | tf_op jit(solution)/shard_map/pallas_call | solution.py:413
  37.9 10.7 %all-to-all-start.1 = ((bf16[32,4,32,128]{3,2,1,0:T(8,128)(2,1)}), bf16[32,4,32,128]{3,2,1,0:T(8,128)(2,1)S(1)}, u32[]{:S(2)}, u32[]{:S(2)}) async-start(bf16[32,4,32,128]{3,2,1,0:T(8,128)(2,1)} %get-tuple-element.33.in_ref), calls=%async_computation.1 | async-start | bytes 2097152 | tf_op jit(solution)/shard_map/all_to_all | solution.py:429
  48.6 28.7 %all-to-all-done.1.in_ref = bf16[32,4,32,128]{3,2,1,0:T(8,128)(2,1)S(1)} async-done(((bf16[32,4,32,128]{3,2,1,0:T(8,128)(2,1)}), bf16[32,4,32,128]{3,2,1,0:T(8,128)(2,1)S(1)}, u32[]{:S(2)}, u32[]{:S(2)}) %all-to-all-start.1) | async-done | bytes 1048608 | tf_op jit(solution)/shard_map/all_to_all | solution.py:429
  77.4 4.1 %shard_map.132 = bf16[32,4,32,128]{3,2,1,0:T(8,128)(2,1)} custom-call(bf16[32,4,32,128]{3,2,1,0:T(8,128)(2,1)S(1)} %all-to-all-done.1.in_ref, f32[2]{0:T(128)S(1)} %broadcast_multiply_fusion.f_ref), custom_call_target="tpu_custom_call" | custom-call | tf_op jit(solution)/shard_map/pallas_call | solution.py:441
  81.4 6.4 %all-to-all-start.2 = ((bf16[32,4,32,128]{3,2,1,0:T(8,128)(2,1)}), bf16[32,4,32,128]{3,2,1,0:T(8,128)(2,1)S(1)}, u32[]{:S(2)}, u32[]{:S(2)}) async-start(bf16[32,4,32,128]{3,2,1,0:T(8,128)(2,1)} %shard_map.132), calls=%async_computation.2 | async-start | bytes 2097152 | tf_op jit(solution)/shard_map/all_to_all | solution.py:453
  87.9 10.7 %shard_map.131.loc_ref = f32[4,32,4,8,128]{4,3,2,1,0:T(8,128)} custom-call(bf16[32,4,32,128]{3,2,1,0:T(8,128)(2,1)} %get-tuple-element.33.in_ref, f32[2]{0:T(128)S(1)} %broadcast_multiply_fusion.f_ref), custom_call_target="tpu_custom_call" | custom-call | tf_op jit(solution)/shard_map/pallas_call | solution.py:431
  98.6 11.6 %all-to-all-done.2.back_ref = bf16[32,4,32,128]{3,2,1,0:T(8,128)(2,1)S(1)} async-done(((bf16[32,4,32,128]{3,2,1,0:T(8,128)(2,1)}), bf16[32,4,32,128]{3,2,1,0:T(8,128)(2,1)S(1)}, u32[]{:S(2)}, u32[]{:S(2)}) %all-to-all-start.2) | async-done | bytes 1048608 | tf_op jit(solution)/shard_map/all_to_all | solution.py:453
  110.2 5.1 %shard_map.133 = (bf16[4,1024,128]{2,1,0:T(8,128)(2,1)S(1)}, bf16[4,1024,128]{2,1,0:T(8,128)(2,1)S(1)}, f32[16,128]{1,0:T(8,128)S(1)}, bf16[1024,512]{1,0:T(8,128)(2,1)S(1)}, bf16[1024,1024]{1,0:T(8,128)(2,1)S(1)}) custom-call(s32[2]{0:T(128)S(1)} %pad_add_fusion.at_ref, f32[4,32,4,8,128]{4,3,2,1,0:T(8,128)} %shard_map.131.loc_ref, ...), custom_call_target="tpu_custom_call" | custom-call | tf_op jit(solution)/shard_map/pallas_call | solution.py:457
  115.9 2.2 %collective-permute-done.2.sgot_ref = f32[16,128]{1,0:T(8,128)S(1)} collective-permute-done((f32[16,128]{1,0:T(8,128)S(1)}, f32[16,128]{1,0:T(8,128)S(1)}, u32[]{:S(2)}, u32[]{:S(2)}) %collective-permute-start.2) | collective-permute-done | bytes 8224 | tf_op jit(solution)/shard_map/ppermute | solution.py:487
  118.1 1.0 shard_map.134
  119.1 1.1 collective-permute-start.6
  120.2 1.7 %collective-permute-start.8 = (bf16[16,128]{1,0:T(8,128)(2,1)S(1)}, bf16[16,128]{1,0:T(8,128)(2,1)S(1)}, u32[]{:S(2)}, u32[]{:S(2)}) collective-permute-start(bf16[16,128]{1,0:T(8,128)(2,1)S(1)} %get-tuple-element.50), channel_id=1, source_target_pairs={{0,6},{1,7},{2,0},{3,1},{4,2},{5,3},{6,4},{7,5},{8,14},{9,15},{10,... | collective-permute-start | bytes 12296 | tf_op jit(solution)/shard_map/ppermute | solution.py:500
  121.9 3.2 %shard_map.135.whole_ref = bf16[16,272,128]{2,1,0:T(8,128)(2,1)} custom-call(bf16[1024,1024]{1,0:T(8,128)(2,1)S(1)} %get-tuple-element.45.normed_ref, bf16[1024,1024]{1,0:T(8,128)(2,1)S(1)} %copy-done, bf16[1024,512]{1,0:T(8,128)(2,1)S(1)} %get-tuple-element.46.g_ref), custom_call_target="tpu_custom_call" | custom-call | tf_op jit(solution)/shard_map/pallas_call | solution.py:505
  125.9 7.4 %all-to-all-start.3 = ((bf16[16,272,128]{2,1,0:T(8,128)(2,1)}), bf16[16,272,128]{2,1,0:T(8,128)(2,1)S(1)}, u32[]{:S(2)}, u32[]{:S(2)}) async-start(bf16[16,272,128]{2,1,0:T(8,128)(2,1)} %shard_map.136), calls=%async_computation.3 | async-start | bytes 2228224 | tf_op jit(solution)/shard_map/all_to_all | solution.py:379
  133.3 1.0 collective-permute-start.3
  134.3 4.0 %collective-permute-start.4 = (bf16[1040,128]{1,0:T(8,128)(2,1)}, bf16[1040,128]{1,0:T(8,128)(2,1)}, u32[]{:S(2)}, u32[]{:S(2)}) collective-permute-start(bf16[1040,128]{1,0:T(8,128)(2,1)} %copy-done.11), channel_id=1, source_target_pairs={{0,4},{1,5},{2,6},{3,7},{4,0},{5,1},{6,2},{7,3},{8,12},{9,13},{10,... | collective-permute-start | bytes 798728 | tf_op jit(solution)/shard_map/ppermute | solution.py:503
  138.6 10.2 %all-to-all-done.3.in_ref = bf16[16,272,128]{2,1,0:T(8,128)(2,1)S(1)} async-done(((bf16[16,272,128]{2,1,0:T(8,128)(2,1)}), bf16[16,272,128]{2,1,0:T(8,128)(2,1)S(1)}, u32[]{:S(2)}, u32[]{:S(2)}) %all-to-all-start.3) | async-done | bytes 1114144 | tf_op jit(solution)/shard_map/all_to_all | solution.py:379
  150.1 3.1 %collective-permute-done.3.r1_ref = bf16[1040,128]{1,0:T(8,128)(2,1)S(1)} collective-permute-done((bf16[1040,128]{1,0:T(8,128)(2,1)}, bf16[1040,128]{1,0:T(8,128)(2,1)S(1)}, u32[]{:S(2)}, u32[]{:S(2)}) %collective-permute-start.3) | collective-permute-done | bytes 266272 | tf_op jit(solution)/shard_map/ppermute | solution.py:503
  153.2 4.7 %collective-permute-done.4.r2_ref = bf16[1040,128]{1,0:T(8,128)(2,1)} collective-permute-done((bf16[1040,128]{1,0:T(8,128)(2,1)}, bf16[1040,128]{1,0:T(8,128)(2,1)}, u32[]{:S(2)}, u32[]{:S(2)}) %collective-permute-start.4) | collective-permute-done | bytes 266272 | tf_op jit(solution)/shard_map/ppermute | solution.py:503
  157.9 3.7 %collective-permute-done.5.r3_ref = bf16[1040,128]{1,0:T(8,128)(2,1)} collective-permute-done((bf16[1040,128]{1,0:T(8,128)(2,1)}, bf16[1040,128]{1,0:T(8,128)(2,1)}, u32[]{:S(2)}, u32[]{:S(2)}) %collective-permute-start.5) | collective-permute-done | bytes 266272 | tf_op jit(solution)/shard_map/ppermute | solution.py:503
  161.6 1.0 copy-done.6
  162.6 1.0 copy-done.8
  163.7 2.5 %norm_back.1 = bf16[1024,128]{1,0:T(8,128)(2,1)} custom-call(s32[2]{0:T(128)S(1)} %pad_add_fusion.at_ref, bf16[1024,1024]{1,0:T(8,128)(2,1)S(1)} %copy-done.2, f32[1,1024]{1,0:T(1,128)S(1)} %bitcast.9, f32[1024,128]{1,0:T(8,128)S(1)} %copy-done.8, bf16[1040,128]{1,0:T(8,128)(2,1)S(1)} %collective-permute-done.3.r1_ref, ...), custom_call_target="tpu_custom_call" | custom-call | tf_op jit(solution)/shard_map/norm_back/pallas_call | solution.py:540
  (40 shorter events, 5.6 us)
Async XLA Ops:
  0.6 18.4 %copy-start.9 = (f32[1024]{0:T(1024)S(1)}, f32[1024]{0:T(1024)}, u32[]{:S(2)}) copy-start(f32[1024]{0:T(1024)} %param.9) | copy-start | bytes 12292
  1.4 8.3 %collective-permute-start = (bf16[32,512]{1,0:T(8,128)(2,1)S(1)}, bf16[32,512]{1,0:T(8,128)(2,1)S(1)}, u32[]{:S(2)}, u32[]{:S(2)}) collective-permute-start(bf16[32,512]{1,0:T(8,128)(2,1)S(1)} %shard_map.128.mine_ref), channel_id=1, source_target_pairs={{0,32},{8,40},{16,48},{24,56},{32,0},{40,8},{48,16},{56,24},{64,96... | collective-permute-start | bytes 98312 | tf_op jit(solution)/shard_map/ppermute | solution.py:399
  10.3 1.0 copy-start.3
  11.4 22.0 %copy-start = (bf16[1024,1024]{1,0:T(8,128)(2,1)S(1)}, bf16[1024,1024]{1,0:T(8,128)(2,1)}, u32[]{:S(2)}) copy-start(bf16[1024,1024]{1,0:T(8,128)(2,1)} %go_ref.3) | copy-start | bytes 6291460
  11.4 22.0 %all-to-all-start = ((bf16[16,64,512]{2,1,0:T(8,128)(2,1)}), bf16[16,64,512]{2,1,0:T(8,128)(2,1)S(1)}, u32[]{:S(2)}, u32[]{:S(2)}) async-start(bf16[16,64,512]{2,1,0:T(8,128)(2,1)} %copy-done.3), calls=%async_computation | async-start | bytes 2097152 | tf_op jit(solution)/shard_map/all_to_all | solution.py:379
  19.0 1.6 copy-start.1
  23.0 1.3 copy-start.4
  33.4 1.6 copy-start.5
  37.9 10.7 %copy-start.13 = (f32[2]{0:T(128)S(1)}, f32[2]{0:T(128)}, u32[]{:S(2)}) copy-start(f32[2]{0:T(128)} %param.14) | copy-start | bytes 28
  37.9 39.4 %all-to-all-start.1 = ((bf16[32,4,32,128]{3,2,1,0:T(8,128)(2,1)}), bf16[32,4,32,128]{3,2,1,0:T(8,128)(2,1)S(1)}, u32[]{:S(2)}, u32[]{:S(2)}) async-start(bf16[32,4,32,128]{3,2,1,0:T(8,128)(2,1)} %get-tuple-element.33.in_ref), calls=%async_computation.1 | async-start | bytes 2097152 | tf_op jit(solution)/shard_map/all_to_all | solution.py:429
  81.4 28.8 %all-to-all-start.2 = ((bf16[32,4,32,128]{3,2,1,0:T(8,128)(2,1)}), bf16[32,4,32,128]{3,2,1,0:T(8,128)(2,1)S(1)}, u32[]{:S(2)}, u32[]{:S(2)}) async-start(bf16[32,4,32,128]{3,2,1,0:T(8,128)(2,1)} %shard_map.132), calls=%async_computation.2 | async-start | bytes 2097152 | tf_op jit(solution)/shard_map/all_to_all | solution.py:453
  115.3 2.8 %collective-permute-start.1 = (bf16[4,1024,128]{2,1,0:T(8,128)(2,1)S(1)}, bf16[4,1024,128]{2,1,0:T(8,128)(2,1)S(1)}, u32[]{:S(2)}, u32[]{:S(2)}) collective-permute-start(bf16[4,1024,128]{2,1,0:T(8,128)(2,1)S(1)} %get-tuple-element.36), channel_id=1, source_target_pairs={{0,1},{1,0},{2,3},{3,2},{4,5},{5,4},{6,7},{7,6},{8,9},{9,8},{10,11... | collective-permute-start | bytes 3145736 | tf_op jit(solution)/shard_map/ppermute | solution.py:486
  115.4 2.7 %collective-permute-start.2 = (f32[16,128]{1,0:T(8,128)S(1)}, f32[16,128]{1,0:T(8,128)S(1)}, u32[]{:S(2)}, u32[]{:S(2)}) collective-permute-start(f32[16,128]{1,0:T(8,128)S(1)} %get-tuple-element.38.small_ref), channel_id=1, source_target_pairs={{0,1},{1,0},{2,3},{3,2},{4,5},{5,4},{6,7},{7,6},{8,9},{9,8},{10,11... | collective-permute-start | bytes 24584 | tf_op jit(solution)/shard_map/ppermute | solution.py:487
  119.1 6.1 %copy-start.7 = (f32[1024,128]{1,0:T(8,128)}, f32[1024,128]{1,0:T(8,128)S(1)}, u32[]{:S(2)}) copy-start(f32[1024,128]{1,0:T(8,128)S(1)} %get-tuple-element.39.own_ref) | copy-start | bytes 1572868
  119.1 6.1 %copy-start.10 = (bf16[1040,128]{1,0:T(8,128)(2,1)}, bf16[1040,128]{1,0:T(8,128)(2,1)S(1)}, u32[]{:S(2)}) copy-start(bf16[1040,128]{1,0:T(8,128)(2,1)S(1)} %get-tuple-element.42) | copy-start | bytes 798724
  119.1 6.1 %copy-start.11 = (bf16[1040,128]{1,0:T(8,128)(2,1)}, bf16[1040,128]{1,0:T(8,128)(2,1)S(1)}, u32[]{:S(2)}) copy-start(bf16[1040,128]{1,0:T(8,128)(2,1)S(1)} %get-tuple-element.41) | copy-start | bytes 798724
  119.1 6.1 %copy-start.12 = (bf16[1040,128]{1,0:T(8,128)(2,1)}, bf16[1040,128]{1,0:T(8,128)(2,1)S(1)}, u32[]{:S(2)}) copy-start(bf16[1040,128]{1,0:T(8,128)(2,1)S(1)} %get-tuple-element.40) | copy-start | bytes 798724
  119.1 6.1 %collective-permute-start.6 = (bf16[16,128]{1,0:T(8,128)(2,1)S(1)}, bf16[16,128]{1,0:T(8,128)(2,1)S(1)}, u32[]{:S(2)}, u32[]{:S(2)}) collective-permute-start(bf16[16,128]{1,0:T(8,128)(2,1)S(1)} %get-tuple-element.48), channel_id=1, source_target_pairs={{0,2},{1,3},{2,4},{3,5},{4,6},{5,7},{6,0},{7,1},{8,10},{9,11},{10,... | collective-permute-start | bytes 12296 | tf_op jit(solution)/shard_map/ppermute | solution.py:500
  120.2 5.0 %collective-permute-start.7 = (bf16[16,128]{1,0:T(8,128)(2,1)S(1)}, bf16[16,128]{1,0:T(8,128)(2,1)S(1)}, u32[]{:S(2)}, u32[]{:S(2)}) collective-permute-start(bf16[16,128]{1,0:T(8,128)(2,1)S(1)} %get-tuple-element.49), channel_id=1, source_target_pairs={{0,4},{1,5},{2,6},{3,7},{4,0},{5,1},{6,2},{7,3},{8,12},{9,13},{10,... | collective-permute-start | bytes 12296 | tf_op jit(solution)/shard_map/ppermute | solution.py:500
  120.2 5.0 %collective-permute-start.8 = (bf16[16,128]{1,0:T(8,128)(2,1)S(1)}, bf16[16,128]{1,0:T(8,128)(2,1)S(1)}, u32[]{:S(2)}, u32[]{:S(2)}) collective-permute-start(bf16[16,128]{1,0:T(8,128)(2,1)S(1)} %get-tuple-element.50), channel_id=1, source_target_pairs={{0,6},{1,7},{2,0},{3,1},{4,2},{5,3},{6,4},{7,5},{8,14},{9,15},{10,... | collective-permute-start | bytes 12296 | tf_op jit(solution)/shard_map/ppermute | solution.py:500
  125.9 35.7 %copy-start.2 = (bf16[1024,1024]{1,0:T(8,128)(2,1)S(1)}, bf16[1024,1024]{1,0:T(8,128)(2,1)}, u32[]{:S(2)}) copy-start(bf16[1024,1024]{1,0:T(8,128)(2,1)} %x_ref.3) | copy-start | bytes 6291460
  125.9 22.9 %all-to-all-start.3 = ((bf16[16,272,128]{2,1,0:T(8,128)(2,1)}), bf16[16,272,128]{2,1,0:T(8,128)(2,1)S(1)}, u32[]{:S(2)}, u32[]{:S(2)}) async-start(bf16[16,272,128]{2,1,0:T(8,128)(2,1)} %shard_map.136), calls=%async_computation.3 | async-start | bytes 2228224 | tf_op jit(solution)/shard_map/all_to_all | solution.py:379
  133.3 19.9 %collective-permute-start.3 = (bf16[1040,128]{1,0:T(8,128)(2,1)}, bf16[1040,128]{1,0:T(8,128)(2,1)S(1)}, u32[]{:S(2)}, u32[]{:S(2)}) collective-permute-start(bf16[1040,128]{1,0:T(8,128)(2,1)} %copy-done.12), channel_id=1, source_target_pairs={{0,2},{1,3},{2,4},{3,5},{4,6},{5,7},{6,0},{7,1},{8,10},{9,11},{10,... | collective-permute-start | bytes 798728 | tf_op jit(solution)/shard_map/ppermute | solution.py:503
  134.3 23.6 %collective-permute-start.4 = (bf16[1040,128]{1,0:T(8,128)(2,1)}, bf16[1040,128]{1,0:T(8,128)(2,1)}, u32[]{:S(2)}, u32[]{:S(2)}) collective-permute-start(bf16[1040,128]{1,0:T(8,128)(2,1)} %copy-done.11), channel_id=1, source_target_pairs={{0,4},{1,5},{2,6},{3,7},{4,0},{5,1},{6,2},{7,3},{8,12},{9,13},{10,... | collective-permute-start | bytes 798728 | tf_op jit(solution)/shard_map/ppermute | solution.py:503
  138.3 23.3 %collective-permute-start.5 = (bf16[1040,128]{1,0:T(8,128)(2,1)}, bf16[1040,128]{1,0:T(8,128)(2,1)}, u32[]{:S(2)}, u32[]{:S(2)}) collective-permute-start(bf16[1040,128]{1,0:T(8,128)(2,1)} %copy-done.10), channel_id=1, source_target_pairs={{0,6},{1,7},{2,0},{3,1},{4,2},{5,3},{6,4},{7,5},{8,14},{9,15},{10,... | collective-permute-start | bytes 798728 | tf_op jit(solution)/shard_map/ppermute | solution.py:503
  149.5 17.4 %collective-permute-start.9 = (bf16[144,128]{1,0:T(8,128)(2,1)S(1)}, bf16[144,128]{1,0:T(8,128)(2,1)S(1)}, u32[]{:S(2)}, u32[]{:S(2)}) collective-permute-start(bf16[144,128]{1,0:T(8,128)(2,1)S(1)} %get-tuple-element.51), channel_id=1, source_target_pairs={{0,32},{8,40},{16,48},{24,56},{32,0},{40,8},{48,16},{56,24},{64,96... | collective-permute-start | bytes 110600 | tf_op jit(solution)/shard_map/ppermute | solution.py:529
  161.6 1.0 copy-start.6
  162.6 1.0 copy-start.8

commit v6 on v5

--- a/solution.py
+++ b/solution.py
@@ -100,7 +100,9 @@
     last = dot(go_ref[...], w_ref[:, 3 * LANES :], 1, 0)
     for j in range(4):
         part = three[:, j * LANES : (j + 1) * LANES] if j < 3 else last
-        out_ref[:, j] = part.astype(BF).reshape(rows // SIDE, SIDE, LANES)
+        part = part.astype(BF).reshape(rows // 256, 2, 4, SIDE, LANES)
+        for zh in range(2):
+            out_ref[zh, :, :, j] = part[:, zh]
 
     @pl.when(pl.program_id(0) == pl.num_programs(0) - 1)
     def _():
@@ -237,7 +239,7 @@
     rows = normed_ref.shape[0]
     kept_ref[...] = normed_ref[...]
     for j in range(4):
-        part = loc_ref[j].reshape(rows, LANES) + back_ref[:, j].astype(F32).reshape(rows, LANES)
+        part = loc_ref[j].reshape(rows, LANES) + back_ref[:, :, :, j].astype(F32).reshape(rows, LANES)
         at = (j - 1) % 4
         g_ref[:, at * LANES : (at + 1) * LANES] = part.astype(BF)
 
@@ -373,6 +375,13 @@
 
 PLANES = [[x * 8 + zh * 4 + y for x in range(4) for y in range(4)] for zh in range(2)]
 OVER_Z = [(s, s ^ 4) for s in range(SIDE)]
+
+
+HALVES = [[x * 8 + zh * 4 + y for zh in range(2) for x in range(4) for y in range(4)]]
+
+
+def over_slab(a):
+    return lax.all_to_all(a, "slab", 0, 0, tiled=True, axis_index_groups=HALVES)
 
 
 def in_plane(a):
@@ -412,7 +421,7 @@
     wide = 2 * blk
     proj, weights = call(
         project_body,
-        (far((SIDE, 4, SIDE, LANES), BF), far((width, 4 * LANES), BF)),
+        (far((2, 4, 4, 4, SIDE, LANES), BF), far((width, 4 * LANES), BF)),
         grid=(rows // wide,),
         in_specs=[
             by_rows((wide, width)),
@@ -420,13 +429,14 @@
             whole((16, 2 * SIDE, 4 * LANES)),
         ],
         out_specs=(
-            by_rows((wide // SIDE, 4, SIDE, LANES)),
+            pl.BlockSpec((2, wide // 256, 4, 4, SIDE, LANES), lambda i: (0, i, 0, 0, 0, 0)),
             pl.BlockSpec(memory_space=pltpu.HBM),
         ),
         scratch_shapes=[pltpu.VMEM((width, 4 * LANES), BF), pltpu.SemaphoreType.DMA],
     )(early, grad_output, pieces)
 
-    z_in = lax.all_to_all(proj, "slab", 0, 0, tiled=True)
+    proj = proj.reshape(SIDE, 4, SIDE, LANES)
+    z_in = over_slab(proj)
     big = (4, SIDE, 4, 8, LANES)
     local = call(
         plane_body,
@@ -450,9 +460,9 @@
             pltpu.VMEM((128, 128), F32),
         ],
     )(z_in, factors)
-    back = lax.all_to_all(z_terms, "slab", 0, 0, tiled=True)
-
-    lines = blk // SIDE
+    back = over_slab(z_terms).reshape(2, 4, 4, 4, SIDE, LANES)
+    local = local.reshape(4, 2, 4, 4, 4, 8, LANES)
+
     parts4 = pl.BlockSpec((4, blk, LANES), lambda i: (0, i, 0))
     away, keep, small, grads, early = call(
         combine_body,
@@ -466,8 +476,8 @@
         grid=(rows // blk,),
         in_specs=[
             SMEM,
-            pl.BlockSpec((4, lines, 4, 8, LANES), lambda i: (0, i, 0, 0, 0)),
-            by_rows((lines, 4, SIDE, LANES)),
+            pl.BlockSpec((4, 2, 1, 4, 4, 8, LANES), lambda i: (0, 0, i, 0, 0, 0, 0)),
+            pl.BlockSpec((2, 1, 4, 4, SIDE, LANES), lambda i: (0, i, 0, 0, 0, 0)),
             by_rows((blk, width)),
             whole((8, LANES)),
             whole((width, 3 * LANES)),

time: 168 us -> 166 us (0.988)
  starting transfers between devices: 47.9 us -> 45.8 us
    all_to_all x2, starting transfers between devices: 15 us -> 13.3 us  [in_plane(): return lax.all_to_all(a, 'slab', 0, 0, tiled=True, axis_index_groups=PLANES)]
where the time goes in v6:
time: 166 us; the launch traced here: 165 us
  waiting for transfers between devices  74.9 us (45%)
  starting transfers between devices  45.8 us (28%)
  Pallas kernels  35.8 us (22%)
  local copies, waits for them, and re-layouts  7.65 us (5%)
    all_to_all x2, waiting for transfers between devices, over_slab(): return lax.all_to_all(a, 'slab', 0, 0, tiled=True, axis_index_groups=HALVES)  40.2 us
    all_to_all x2, waiting for transfers between devices, in_plane(): return lax.all_to_all(a, 'slab', 0, 0, tiled=True, axis_index_groups=PLANES)  19.3 us
    all_to_all x2, starting transfers between devices, over_slab(): return lax.all_to_all(a, 'slab', 0, 0, tiled=True, axis_index_groups=HALVES)  16.7 us
    all_to_all x2, starting transfers between devices, in_plane(): return lax.all_to_all(a, 'slab', 0, 0, tiled=True, axis_index_groups=PLANES)  13.3 us
    ppermute x3, waiting for transfers between devices, body(): parts.append(lax.ppermute(s, 'head', to_zl(d + 1)))  11.5 us
    pallas_call x1, Pallas kernels, body(): call(plane_body, far(big, F32), in_specs=[VMEM, SMEM], scratch_shapes=[pl...  10.7 us
    unnamed x28, local copies, waits for them, and re-layouts  7.65 us
    ppermute x1, starting transfers between devices, body(): other = lax.ppermute(mine, 'slab', OVER_Z)  6.38 us
  transfers between devices with their start and end apart: 14, of which 9 were waited for; matrix products, arithmetic and copies ran while one was open for 0% of the time, Pallas kernels for 12%

profile of v6, /device:TPU:34, one launch (start us, length us, event | category | flops | bytes accessed | tf_op | source)
XLA Modules:
  0.0 165.1 jit_solution(14353404826513788370)
XLA Ops:
  1.4 6.4 %collective-permute-start = (bf16[32,512]{1,0:T(8,128)(2,1)S(1)}, bf16[32,512]{1,0:T(8,128)(2,1)S(1)}, u32[]{:S(2)}, u32[]{:S(2)}) collective-permute-start(bf16[32,512]{1,0:T(8,128)(2,1)S(1)} %shard_map.128.mine_ref), channel_id=1, source_target_pairs={{0,32},{8,40},{16,48},{24,56},{32,0},{40,8},{48,16},{56,24},{64,96... | collective-permute-start | bytes 98312 | tf_op jit(solution)/shard_map/ppermute | solution.py:408
  7.9 1.8 %collective-permute-done.got_ref = bf16[32,512]{1,0:T(8,128)(2,1)S(1)} collective-permute-done((bf16[32,512]{1,0:T(8,128)(2,1)S(1)}, bf16[32,512]{1,0:T(8,128)(2,1)S(1)}, u32[]{:S(2)}, u32[]{:S(2)}) %collective-permute-start) | collective-permute-done | bytes 32800 | tf_op jit(solution)/shard_map/ppermute | solution.py:408
  10.4 1.0 copy-done.3
  11.4 7.6 %all-to-all-start = ((bf16[16,64,512]{2,1,0:T(8,128)(2,1)}), bf16[16,64,512]{2,1,0:T(8,128)(2,1)S(1)}, u32[]{:S(2)}, u32[]{:S(2)}) async-start(bf16[16,64,512]{2,1,0:T(8,128)(2,1)} %copy-done.3), calls=%async_computation | async-start | bytes 2097152 | tf_op jit(solution)/shard_map/all_to_all | solution.py:388
  19.0 1.6 copy-done.1
  20.6 2.4 %shard_map.127 = (bf16[1024,1024]{1,0:T(8,128)(2,1)S(1)}, bf16[1024,1024]{1,0:T(8,128)(2,1)}, f32[1024,128]{1,0:T(8,128)}) custom-call(bf16[1024,1024]{1,0:T(8,128)(2,1)S(1)} %copy-done.1, f32[1,1024]{1,0:T(1,128)S(1)} %bitcast.11), custom_call_target="tpu_custom_call" | custom-call | tf_op jit(solution)/shard_map/pallas_call | solution.py:412
  23.0 1.3 copy-done.4
  24.3 9.1 %all-to-all-done.pieces_ref = bf16[16,64,512]{2,1,0:T(8,128)(2,1)S(1)} async-done(((bf16[16,64,512]{2,1,0:T(8,128)(2,1)}), bf16[16,64,512]{2,1,0:T(8,128)(2,1)S(1)}, u32[]{:S(2)}, u32[]{:S(2)}) %all-to-all-start) | async-done | bytes 1048608 | tf_op jit(solution)/shard_map/all_to_all | solution.py:388
  33.4 1.6 copy-done.5
  35.0 2.9 %shard_map.130 = (bf16[2,4,4,4,32,128]{5,4,3,2,1,0:T(8,128)(2,1)}, bf16[1024,512]{1,0:T(8,128)(2,1)}) custom-call(bf16[1024,1024]{1,0:T(8,128)(2,1)S(1)} %copy-done.5, bf16[1024,1024]{1,0:T(8,128)(2,1)S(1)} %copy-done, bf16[16,64,512]{2,1,0:T(8,128)(2,1)S(1)} %all-to-all-done.pieces_ref), custom_call_target="tpu_custom_call" | custom-call | tf_op jit(solution)/shard_map/pallas_call | solution.py:422
  37.9 10.7 %all-to-all-start.1 = ((bf16[32,4,32,128]{3,2,1,0:T(8,128)(2,1)}), bf16[32,4,32,128]{3,2,1,0:T(8,128)(2,1)S(1)}, u32[]{:S(2)}, u32[]{:S(2)}) async-start(bf16[32,4,32,128]{3,2,1,0:T(8,128)(2,1)} %bitcast.15), calls=%async_computation.1 | async-start | bytes 2097152 | tf_op jit(solution)/shard_map/all_to_all | solution.py:384
  48.6 28.8 %all-to-all-done.1.in_ref = bf16[32,4,32,128]{3,2,1,0:T(8,128)(2,1)S(1)} async-done(((bf16[32,4,32,128]{3,2,1,0:T(8,128)(2,1)}), bf16[32,4,32,128]{3,2,1,0:T(8,128)(2,1)S(1)}, u32[]{:S(2)}, u32[]{:S(2)}) %all-to-all-start.1) | async-done | bytes 1048608 | tf_op jit(solution)/shard_map/all_to_all | solution.py:384
  77.4 4.1 %shard_map.132 = bf16[32,4,32,128]{3,2,1,0:T(8,128)(2,1)} custom-call(bf16[32,4,32,128]{3,2,1,0:T(8,128)(2,1)S(1)} %all-to-all-done.1.in_ref, f32[2]{0:T(128)S(1)} %broadcast_multiply_fusion.f_ref), custom_call_target="tpu_custom_call" | custom-call | tf_op jit(solution)/shard_map/pallas_call | solution.py:451
  81.4 6.1 %all-to-all-start.2 = ((bf16[32,4,32,128]{3,2,1,0:T(8,128)(2,1)}), bf16[32,4,32,128]{3,2,1,0:T(8,128)(2,1)S(1)}, u32[]{:S(2)}, u32[]{:S(2)}) async-start(bf16[32,4,32,128]{3,2,1,0:T(8,128)(2,1)} %shard_map.132), calls=%async_computation.2 | async-start | bytes 2097152 | tf_op jit(solution)/shard_map/all_to_all | solution.py:384
  87.5 10.7 %shard_map.131 = f32[4,32,4,8,128]{4,3,2,1,0:T(8,128)} custom-call(bf16[32,4,32,128]{3,2,1,0:T(8,128)(2,1)} %bitcast.16, f32[2]{0:T(128)S(1)} %broadcast_multiply_fusion.f_ref), custom_call_target="tpu_custom_call" | custom-call | tf_op jit(solution)/shard_map/pallas_call | solution.py:441
  98.2 11.4 %all-to-all-done.2 = bf16[32,4,32,128]{3,2,1,0:T(8,128)(2,1)S(1)} async-done(((bf16[32,4,32,128]{3,2,1,0:T(8,128)(2,1)}), bf16[32,4,32,128]{3,2,1,0:T(8,128)(2,1)S(1)}, u32[]{:S(2)}, u32[]{:S(2)}) %all-to-all-start.2) | async-done | bytes 1048608 | tf_op jit(solution)/shard_map/all_to_all | solution.py:384
  109.6 5.1 %shard_map.133 = (bf16[4,1024,128]{2,1,0:T(8,128)(2,1)S(1)}, bf16[4,1024,128]{2,1,0:T(8,128)(2,1)S(1)}, f32[16,128]{1,0:T(8,128)S(1)}, bf16[1024,512]{1,0:T(8,128)(2,1)S(1)}, bf16[1024,1024]{1,0:T(8,128)(2,1)S(1)}) custom-call(s32[2]{0:T(128)S(1)} %pad_add_fusion.at_ref, f32[4,2,4,4,4,8,128]{6,5,4,3,2,1,0:T(8,128)} %bitcast.14, ...), custom_call_target="tpu_custom_call" | custom-call | tf_op jit(solution)/shard_map/pallas_call | solution.py:467
  115.3 2.2 %collective-permute-done.2.sgot_ref = f32[16,128]{1,0:T(8,128)S(1)} collective-permute-done((f32[16,128]{1,0:T(8,128)S(1)}, f32[16,128]{1,0:T(8,128)S(1)}, u32[]{:S(2)}, u32[]{:S(2)}) %collective-permute-start.2) | collective-permute-done | bytes 8224 | tf_op jit(solution)/shard_map/ppermute | solution.py:497
  117.5 1.0 shard_map.134
  118.5 1.1 collective-permute-start.6
  119.6 1.7 %collective-permute-start.8 = (bf16[16,128]{1,0:T(8,128)(2,1)S(1)}, bf16[16,128]{1,0:T(8,128)(2,1)S(1)}, u32[]{:S(2)}, u32[]{:S(2)}) collective-permute-start(bf16[16,128]{1,0:T(8,128)(2,1)S(1)} %get-tuple-element.50), channel_id=1, source_target_pairs={{0,6},{1,7},{2,0},{3,1},{4,2},{5,3},{6,4},{7,5},{8,14},{9,15},{10,... | collective-permute-start | bytes 12296 | tf_op jit(solution)/shard_map/ppermute | solution.py:510
  121.3 3.2 %shard_map.135.whole_ref = bf16[16,272,128]{2,1,0:T(8,128)(2,1)} custom-call(bf16[1024,1024]{1,0:T(8,128)(2,1)S(1)} %get-tuple-element.45.normed_ref, bf16[1024,1024]{1,0:T(8,128)(2,1)S(1)} %copy-done, bf16[1024,512]{1,0:T(8,128)(2,1)S(1)} %get-tuple-element.46.g_ref), custom_call_target="tpu_custom_call" | custom-call | tf_op jit(solution)/shard_map/pallas_call | solution.py:515
  125.2 5.7 %all-to-all-start.3 = ((bf16[16,272,128]{2,1,0:T(8,128)(2,1)}), bf16[16,272,128]{2,1,0:T(8,128)(2,1)S(1)}, u32[]{:S(2)}, u32[]{:S(2)}) async-start(bf16[16,272,128]{2,1,0:T(8,128)(2,1)} %shard_map.136), calls=%async_computation.3 | async-start | bytes 2228224 | tf_op jit(solution)/shard_map/all_to_all | solution.py:388
  130.9 1.6 collective-permute-start.3
  132.5 3.4 %collective-permute-start.4 = (bf16[1040,128]{1,0:T(8,128)(2,1)}, bf16[1040,128]{1,0:T(8,128)(2,1)}, u32[]{:S(2)}, u32[]{:S(2)}) collective-permute-start(bf16[1040,128]{1,0:T(8,128)(2,1)} %copy-done.11), channel_id=1, source_target_pairs={{0,4},{1,5},{2,6},{3,7},{4,0},{5,1},{6,2},{7,3},{8,12},{9,13},{10,... | collective-permute-start | bytes 798728 | tf_op jit(solution)/shard_map/ppermute | solution.py:513
  136.2 10.2 %all-to-all-done.3.in_ref = bf16[16,272,128]{2,1,0:T(8,128)(2,1)S(1)} async-done(((bf16[16,272,128]{2,1,0:T(8,128)(2,1)}), bf16[16,272,128]{2,1,0:T(8,128)(2,1)S(1)}, u32[]{:S(2)}, u32[]{:S(2)}) %all-to-all-start.3) | async-done | bytes 1114144 | tf_op jit(solution)/shard_map/all_to_all | solution.py:388
  147.7 4.5 %collective-permute-done.3.r1_ref = bf16[1040,128]{1,0:T(8,128)(2,1)S(1)} collective-permute-done((bf16[1040,128]{1,0:T(8,128)(2,1)}, bf16[1040,128]{1,0:T(8,128)(2,1)S(1)}, u32[]{:S(2)}, u32[]{:S(2)}) %collective-permute-start.3) | collective-permute-done | bytes 266272 | tf_op jit(solution)/shard_map/ppermute | solution.py:513
  152.1 4.0 %collective-permute-done.4.r2_ref = bf16[1040,128]{1,0:T(8,128)(2,1)} collective-permute-done((bf16[1040,128]{1,0:T(8,128)(2,1)}, bf16[1040,128]{1,0:T(8,128)(2,1)}, u32[]{:S(2)}, u32[]{:S(2)}) %collective-permute-start.4) | collective-permute-done | bytes 266272 | tf_op jit(solution)/shard_map/ppermute | solution.py:513
  156.1 3.1 %collective-permute-done.5.r3_ref = bf16[1040,128]{1,0:T(8,128)(2,1)} collective-permute-done((bf16[1040,128]{1,0:T(8,128)(2,1)}, bf16[1040,128]{1,0:T(8,128)(2,1)}, u32[]{:S(2)}, u32[]{:S(2)}) %collective-permute-start.5) | collective-permute-done | bytes 266272 | tf_op jit(solution)/shard_map/ppermute | solution.py:513
  159.2 1.0 copy-done.6
  160.2 1.0 copy-done.8
  161.3 2.5 %norm_back.1 = bf16[1024,128]{1,0:T(8,128)(2,1)} custom-call(s32[2]{0:T(128)S(1)} %pad_add_fusion.at_ref, bf16[1024,1024]{1,0:T(8,128)(2,1)S(1)} %copy-done.2, f32[1,1024]{1,0:T(1,128)S(1)} %bitcast.13, f32[1024,128]{1,0:T(8,128)S(1)} %copy-done.8, bf16[1040,128]{1,0:T(8,128)(2,1)S(1)} %collective-permute-done.3.r1_ref, ...), custom_call_target="tpu_custom_call" | custom-call | tf_op jit(solution)/shard_map/norm_back/pallas_call | solution.py:550
  (40 shorter events, 5.7 us)
Async XLA Ops:
  0.6 18.4 %copy-start.9 = (f32[1024]{0:T(1024)S(1)}, f32[1024]{0:T(1024)}, u32[]{:S(2)}) copy-start(f32[1024]{0:T(1024)} %param.9) | copy-start | bytes 12292
  1.4 8.3 %collective-permute-start = (bf16[32,512]{1,0:T(8,128)(2,1)S(1)}, bf16[32,512]{1,0:T(8,128)(2,1)S(1)}, u32[]{:S(2)}, u32[]{:S(2)}) collective-permute-start(bf16[32,512]{1,0:T(8,128)(2,1)S(1)} %shard_map.128.mine_ref), channel_id=1, source_target_pairs={{0,32},{8,40},{16,48},{24,56},{32,0},{40,8},{48,16},{56,24},{64,96... | collective-permute-start | bytes 98312 | tf_op jit(solution)/shard_map/ppermute | solution.py:408
  10.3 1.0 copy-start.3
  11.4 22.0 %copy-start = (bf16[1024,1024]{1,0:T(8,128)(2,1)S(1)}, bf16[1024,1024]{1,0:T(8,128)(2,1)}, u32[]{:S(2)}) copy-start(bf16[1024,1024]{1,0:T(8,128)(2,1)} %go_ref.3) | copy-start | bytes 6291460
  11.4 22.0 %all-to-all-start = ((bf16[16,64,512]{2,1,0:T(8,128)(2,1)}), bf16[16,64,512]{2,1,0:T(8,128)(2,1)S(1)}, u32[]{:S(2)}, u32[]{:S(2)}) async-start(bf16[16,64,512]{2,1,0:T(8,128)(2,1)} %copy-done.3), calls=%async_computation | async-start | bytes 2097152 | tf_op jit(solution)/shard_map/all_to_all | solution.py:388
  19.0 1.6 copy-start.1
  23.0 1.3 copy-start.4
  33.4 1.6 copy-start.5
  37.9 10.7 %copy-start.13 = (f32[2]{0:T(128)S(1)}, f32[2]{0:T(128)}, u32[]{:S(2)}) copy-start(f32[2]{0:T(128)} %param.14) | copy-start | bytes 28
  37.9 39.5 %all-to-all-start.1 = ((bf16[32,4,32,128]{3,2,1,0:T(8,128)(2,1)}), bf16[32,4,32,128]{3,2,1,0:T(8,128)(2,1)S(1)}, u32[]{:S(2)}, u32[]{:S(2)}) async-start(bf16[32,4,32,128]{3,2,1,0:T(8,128)(2,1)} %bitcast.15), calls=%async_computation.1 | async-start | bytes 2097152 | tf_op jit(solution)/shard_map/all_to_all | solution.py:384
  81.4 28.2 %all-to-all-start.2 = ((bf16[32,4,32,128]{3,2,1,0:T(8,128)(2,1)}), bf16[32,4,32,128]{3,2,1,0:T(8,128)(2,1)S(1)}, u32[]{:S(2)}, u32[]{:S(2)}) async-start(bf16[32,4,32,128]{3,2,1,0:T(8,128)(2,1)} %shard_map.132), calls=%async_computation.2 | async-start | bytes 2097152 | tf_op jit(solution)/shard_map/all_to_all | solution.py:384
  114.7 2.8 %collective-permute-start.1 = (bf16[4,1024,128]{2,1,0:T(8,128)(2,1)S(1)}, bf16[4,1024,128]{2,1,0:T(8,128)(2,1)S(1)}, u32[]{:S(2)}, u32[]{:S(2)}) collective-permute-start(bf16[4,1024,128]{2,1,0:T(8,128)(2,1)S(1)} %get-tuple-element.36), channel_id=1, source_target_pairs={{0,1},{1,0},{2,3},{3,2},{4,5},{5,4},{6,7},{7,6},{8,9},{9,8},{10,11... | collective-permute-start | bytes 3145736 | tf_op jit(solution)/shard_map/ppermute | solution.py:496
  114.8 2.7 %collective-permute-start.2 = (f32[16,128]{1,0:T(8,128)S(1)}, f32[16,128]{1,0:T(8,128)S(1)}, u32[]{:S(2)}, u32[]{:S(2)}) collective-permute-start(f32[16,128]{1,0:T(8,128)S(1)} %get-tuple-element.38.small_ref), channel_id=1, source_target_pairs={{0,1},{1,0},{2,3},{3,2},{4,5},{5,4},{6,7},{7,6},{8,9},{9,8},{10,11... | collective-permute-start | bytes 24584 | tf_op jit(solution)/shard_map/ppermute | solution.py:497
  118.4 6.1 %copy-start.7 = (f32[1024,128]{1,0:T(8,128)}, f32[1024,128]{1,0:T(8,128)S(1)}, u32[]{:S(2)}) copy-start(f32[1024,128]{1,0:T(8,128)S(1)} %get-tuple-element.39.own_ref) | copy-start | bytes 1572868
  118.4 6.1 %copy-start.10 = (bf16[1040,128]{1,0:T(8,128)(2,1)}, bf16[1040,128]{1,0:T(8,128)(2,1)S(1)}, u32[]{:S(2)}) copy-start(bf16[1040,128]{1,0:T(8,128)(2,1)S(1)} %get-tuple-element.42) | copy-start | bytes 798724
  118.4 6.0 %copy-start.11 = (bf16[1040,128]{1,0:T(8,128)(2,1)}, bf16[1040,128]{1,0:T(8,128)(2,1)S(1)}, u32[]{:S(2)}) copy-start(bf16[1040,128]{1,0:T(8,128)(2,1)S(1)} %get-tuple-element.41) | copy-start | bytes 798724
  118.5 6.0 %copy-start.12 = (bf16[1040,128]{1,0:T(8,128)(2,1)}, bf16[1040,128]{1,0:T(8,128)(2,1)S(1)}, u32[]{:S(2)}) copy-start(bf16[1040,128]{1,0:T(8,128)(2,1)S(1)} %get-tuple-element.40) | copy-start | bytes 798724
  118.5 6.0 %collective-permute-start.6 = (bf16[16,128]{1,0:T(8,128)(2,1)S(1)}, bf16[16,128]{1,0:T(8,128)(2,1)S(1)}, u32[]{:S(2)}, u32[]{:S(2)}) collective-permute-start(bf16[16,128]{1,0:T(8,128)(2,1)S(1)} %get-tuple-element.48), channel_id=1, source_target_pairs={{0,2},{1,3},{2,4},{3,5},{4,6},{5,7},{6,0},{7,1},{8,10},{9,11},{10,... | collective-permute-start | bytes 12296 | tf_op jit(solution)/shard_map/ppermute | solution.py:510
  119.5 5.0 %collective-permute-start.7 = (bf16[16,128]{1,0:T(8,128)(2,1)S(1)}, bf16[16,128]{1,0:T(8,128)(2,1)S(1)}, u32[]{:S(2)}, u32[]{:S(2)}) collective-permute-start(bf16[16,128]{1,0:T(8,128)(2,1)S(1)} %get-tuple-element.49), channel_id=1, source_target_pairs={{0,4},{1,5},{2,6},{3,7},{4,0},{5,1},{6,2},{7,3},{8,12},{9,13},{10,... | collective-permute-start | bytes 12296 | tf_op jit(solution)/shard_map/ppermute | solution.py:510
  119.6 5.0 %collective-permute-start.8 = (bf16[16,128]{1,0:T(8,128)(2,1)S(1)}, bf16[16,128]{1,0:T(8,128)(2,1)S(1)}, u32[]{:S(2)}, u32[]{:S(2)}) collective-permute-start(bf16[16,128]{1,0:T(8,128)(2,1)S(1)} %get-tuple-element.50), channel_id=1, source_target_pairs={{0,6},{1,7},{2,0},{3,1},{4,2},{5,3},{6,4},{7,5},{8,14},{9,15},{10,... | collective-permute-start | bytes 12296 | tf_op jit(solution)/shard_map/ppermute | solution.py:510
  125.2 34.0 %copy-start.2 = (bf16[1024,1024]{1,0:T(8,128)(2,1)S(1)}, bf16[1024,1024]{1,0:T(8,128)(2,1)}, u32[]{:S(2)}) copy-start(bf16[1024,1024]{1,0:T(8,128)(2,1)} %x_ref.3) | copy-start | bytes 6291460
  125.2 21.2 %all-to-all-start.3 = ((bf16[16,272,128]{2,1,0:T(8,128)(2,1)}), bf16[16,272,128]{2,1,0:T(8,128)(2,1)S(1)}, u32[]{:S(2)}, u32[]{:S(2)}) async-start(bf16[16,272,128]{2,1,0:T(8,128)(2,1)} %shard_map.136), calls=%async_computation.3 | async-start | bytes 2228224 | tf_op jit(solution)/shard_map/all_to_all | solution.py:388
  130.9 21.3 %collective-permute-start.3 = (bf16[1040,128]{1,0:T(8,128)(2,1)}, bf16[1040,128]{1,0:T(8,128)(2,1)S(1)}, u32[]{:S(2)}, u32[]{:S(2)}) collective-permute-start(bf16[1040,128]{1,0:T(8,128)(2,1)} %copy-done.12), channel_id=1, source_target_pairs={{0,2},{1,3},{2,4},{3,5},{4,6},{5,7},{6,0},{7,1},{8,10},{9,11},{10,... | collective-permute-start | bytes 798728 | tf_op jit(solution)/shard_map/ppermute | solution.py:513
  132.5 23.6 %collective-permute-start.4 = (bf16[1040,128]{1,0:T(8,128)(2,1)}, bf16[1040,128]{1,0:T(8,128)(2,1)}, u32[]{:S(2)}, u32[]{:S(2)}) collective-permute-start(bf16[1040,128]{1,0:T(8,128)(2,1)} %copy-done.11), channel_id=1, source_target_pairs={{0,4},{1,5},{2,6},{3,7},{4,0},{5,1},{6,2},{7,3},{8,12},{9,13},{10,... | collective-permute-start | bytes 798728 | tf_op jit(solution)/shard_map/ppermute | solution.py:513
  135.9 23.3 %collective-permute-start.5 = (bf16[1040,128]{1,0:T(8,128)(2,1)}, bf16[1040,128]{1,0:T(8,128)(2,1)}, u32[]{:S(2)}, u32[]{:S(2)}) collective-permute-start(bf16[1040,128]{1,0:T(8,128)(2,1)} %copy-done.10), channel_id=1, source_target_pairs={{0,6},{1,7},{2,0},{3,1},{4,2},{5,3},{6,4},{7,5},{8,14},{9,15},{10,... | collective-permute-start | bytes 798728 | tf_op jit(solution)/shard_map/ppermute | solution.py:513
  147.1 17.4 %collective-permute-start.9 = (bf16[144,128]{1,0:T(8,128)(2,1)S(1)}, bf16[144,128]{1,0:T(8,128)(2,1)S(1)}, u32[]{:S(2)}, u32[]{:S(2)}) collective-permute-start(bf16[144,128]{1,0:T(8,128)(2,1)S(1)} %get-tuple-element.51), channel_id=1, source_target_pairs={{0,32},{8,40},{16,48},{24,56},{32,0},{40,8},{48,16},{56,24},{64,96... | collective-permute-start | bytes 110600 | tf_op jit(solution)/shard_map/ppermute | solution.py:539
  159.2 1.0 copy-start.6
  160.2 1.0 copy-start.8

commit v7 on v6

--- a/solution.py
+++ b/solution.py
@@ -239,7 +239,14 @@
     rows = normed_ref.shape[0]
     kept_ref[...] = normed_ref[...]
     for j in range(4):
-        part = loc_ref[j].reshape(rows, LANES) + back_ref[:, :, :, j].astype(F32).reshape(rows, LANES)
+        part = jnp.concatenate(
+            [
+                loc_ref[j, :, x].reshape(256, LANES)
+                + back_ref[:, x, :, j].astype(F32).reshape(256, LANES)
+                for x in range(rows // 256)
+            ],
+            axis=0,
+        )
         at = (j - 1) % 4
         g_ref[:, at * LANES : (at + 1) * LANES] = part.astype(BF)
 
@@ -463,7 +470,7 @@
     back = over_slab(z_terms).reshape(2, 4, 4, 4, SIDE, LANES)
     local = local.reshape(4, 2, 4, 4, 4, 8, LANES)
 
-    parts4 = pl.BlockSpec((4, blk, LANES), lambda i: (0, i, 0))
+    parts4 = pl.BlockSpec((4, wide, LANES), lambda i: (0, i, 0))
     away, keep, small, grads, early = call(
         combine_body,
         (
@@ -473,12 +480,12 @@
             shape((TOK, 4 * LANES), BF),
             shape((rows, width), BF),
         ),
-        grid=(rows // blk,),
+        grid=(rows // wide,),
         in_specs=[
             SMEM,
-            pl.BlockSpec((4, 2, 1, 4, 4, 8, LANES), lambda i: (0, 0, i, 0, 0, 0, 0)),
-            pl.BlockSpec((2, 1, 4, 4, SIDE, LANES), lambda i: (0, i, 0, 0, 0, 0)),
-            by_rows((blk, width)),
+            pl.BlockSpec((4, 2, 2, 4, 4, 8, LANES), lambda i: (0, 0, i, 0, 0, 0, 0)),
+            pl.BlockSpec((2, 2, 4, 4, SIDE, LANES), lambda i: (0, i, 0, 0, 0, 0)),
+            by_rows((wide, width)),
             whole((8, LANES)),
             whole((width, 3 * LANES)),
         ],
@@ -486,8 +493,8 @@
             parts4,
             parts4,
             whole((16, LANES)),
-            by_rows((blk, 4 * LANES)),
-            by_rows((blk, width)),
+            by_rows((wide, 4 * LANES)),
+            by_rows((wide, width)),
         ),
         scratch_shapes=[pltpu.VMEM((4, 8, 2 * LANES), F32)],
     )(at, stay(local), back, stay(normed), norm_gain.reshape(8, LANES), stay(weights))

time: 166 us -> 165 us (level)
  no operation moved by 1% of the time
where the time goes in v7:
time: 165 us; the launch traced here: 164 us
  waiting for transfers between devices  75.1 us (46%)
  starting transfers between devices  45.8 us (28%)
  Pallas kernels  34.9 us (21%)
  local copies, waits for them, and re-layouts  7.65 us (5%)
    all_to_all x2, waiting for transfers between devices, over_slab(): return lax.all_to_all(a, 'slab', 0, 0, tiled=True, axis_index_groups=HALVES)  40.2 us
    all_to_all x2, waiting for transfers between devices, in_plane(): return lax.all_to_all(a, 'slab', 0, 0, tiled=True, axis_index_groups=PLANES)  19.3 us
    all_to_all x2, starting transfers between devices, over_slab(): return lax.all_to_all(a, 'slab', 0, 0, tiled=True, axis_index_groups=HALVES)  16.7 us
    all_to_all x2, starting transfers between devices, in_plane(): return lax.all_to_all(a, 'slab', 0, 0, tiled=True, axis_index_groups=PLANES)  13.4 us
    ppermute x3, waiting for transfers between devices, body(): parts.append(lax.ppermute(s, 'head', to_zl(d + 1)))  11.7 us
    pallas_call x1, Pallas kernels, body(): call(plane_body, far(big, F32), in_specs=[VMEM, SMEM], scratch_shapes=[pl...  10.7 us
    unnamed x28, local copies, waits for them, and re-layouts  7.65 us
    ppermute x1, starting transfers between devices, body(): other = lax.ppermute(mine, 'slab', OVER_Z)  6.38 us
  transfers between devices with their start and end apart: 14, of which 9 were waited for; matrix products, arithmetic and copies ran while one was open for 0% of the time, Pallas kernels for 12%

profile of v7, /device:TPU:34, one launch (start us, length us, event | category | flops | bytes accessed | tf_op | source)
XLA Modules:
  0.0 164.4 jit_solution(11140117977744336925)
XLA Ops:
  1.4 6.4 %collective-permute-start = (bf16[32,512]{1,0:T(8,128)(2,1)S(1)}, bf16[32,512]{1,0:T(8,128)(2,1)S(1)}, u32[]{:S(2)}, u32[]{:S(2)}) collective-permute-start(bf16[32,512]{1,0:T(8,128)(2,1)S(1)} %shard_map.128.mine_ref), channel_id=1, source_target_pairs={{0,32},{8,40},{16,48},{24,56},{32,0},{40,8},{48,16},{56,24},{64,96... | collective-permute-start | bytes 98312 | tf_op jit(solution)/shard_map/ppermute | solution.py:415
  7.9 1.8 %collective-permute-done.got_ref = bf16[32,512]{1,0:T(8,128)(2,1)S(1)} collective-permute-done((bf16[32,512]{1,0:T(8,128)(2,1)S(1)}, bf16[32,512]{1,0:T(8,128)(2,1)S(1)}, u32[]{:S(2)}, u32[]{:S(2)}) %collective-permute-start) | collective-permute-done | bytes 32800 | tf_op jit(solution)/shard_map/ppermute | solution.py:415
  10.4 1.0 copy-done.3
  11.4 7.6 %all-to-all-start = ((bf16[16,64,512]{2,1,0:T(8,128)(2,1)}), bf16[16,64,512]{2,1,0:T(8,128)(2,1)S(1)}, u32[]{:S(2)}, u32[]{:S(2)}) async-start(bf16[16,64,512]{2,1,0:T(8,128)(2,1)} %copy-done.3), calls=%async_computation | async-start | bytes 2097152 | tf_op jit(solution)/shard_map/all_to_all | solution.py:395
  19.0 1.6 copy-done.1
  20.6 2.4 %shard_map.127 = (bf16[1024,1024]{1,0:T(8,128)(2,1)S(1)}, bf16[1024,1024]{1,0:T(8,128)(2,1)}, f32[1024,128]{1,0:T(8,128)}) custom-call(bf16[1024,1024]{1,0:T(8,128)(2,1)S(1)} %copy-done.1, f32[1,1024]{1,0:T(1,128)S(1)} %bitcast.11), custom_call_target="tpu_custom_call" | custom-call | tf_op jit(solution)/shard_map/pallas_call | solution.py:419
  23.0 1.3 copy-done.4
  24.3 9.1 %all-to-all-done.pieces_ref = bf16[16,64,512]{2,1,0:T(8,128)(2,1)S(1)} async-done(((bf16[16,64,512]{2,1,0:T(8,128)(2,1)}), bf16[16,64,512]{2,1,0:T(8,128)(2,1)S(1)}, u32[]{:S(2)}, u32[]{:S(2)}) %all-to-all-start) | async-done | bytes 1048608 | tf_op jit(solution)/shard_map/all_to_all | solution.py:395
  33.4 1.6 copy-done.5
  35.0 2.9 %shard_map.130 = (bf16[2,4,4,4,32,128]{5,4,3,2,1,0:T(8,128)(2,1)}, bf16[1024,512]{1,0:T(8,128)(2,1)}) custom-call(bf16[1024,1024]{1,0:T(8,128)(2,1)S(1)} %copy-done.5, bf16[1024,1024]{1,0:T(8,128)(2,1)S(1)} %copy-done, bf16[16,64,512]{2,1,0:T(8,128)(2,1)S(1)} %all-to-all-done.pieces_ref), custom_call_target="tpu_custom_call" | custom-call | tf_op jit(solution)/shard_map/pallas_call | solution.py:429
  37.9 10.7 %all-to-all-start.1 = ((bf16[32,4,32,128]{3,2,1,0:T(8,128)(2,1)}), bf16[32,4,32,128]{3,2,1,0:T(8,128)(2,1)S(1)}, u32[]{:S(2)}, u32[]{:S(2)}) async-start(bf16[32,4,32,128]{3,2,1,0:T(8,128)(2,1)} %bitcast.15), calls=%async_computation.1 | async-start | bytes 2097152 | tf_op jit(solution)/shard_map/all_to_all | solution.py:391
  48.6 28.8 %all-to-all-done.1.in_ref = bf16[32,4,32,128]{3,2,1,0:T(8,128)(2,1)S(1)} async-done(((bf16[32,4,32,128]{3,2,1,0:T(8,128)(2,1)}), bf16[32,4,32,128]{3,2,1,0:T(8,128)(2,1)S(1)}, u32[]{:S(2)}, u32[]{:S(2)}) %all-to-all-start.1) | async-done | bytes 1048608 | tf_op jit(solution)/shard_map/all_to_all | solution.py:391
  77.4 4.1 %shard_map.132 = bf16[32,4,32,128]{3,2,1,0:T(8,128)(2,1)} custom-call(bf16[32,4,32,128]{3,2,1,0:T(8,128)(2,1)S(1)} %all-to-all-done.1.in_ref, f32[2]{0:T(128)S(1)} %broadcast_multiply_fusion.f_ref), custom_call_target="tpu_custom_call" | custom-call | tf_op jit(solution)/shard_map/pallas_call | solution.py:458
  81.4 6.1 %all-to-all-start.2 = ((bf16[32,4,32,128]{3,2,1,0:T(8,128)(2,1)}), bf16[32,4,32,128]{3,2,1,0:T(8,128)(2,1)S(1)}, u32[]{:S(2)}, u32[]{:S(2)}) async-start(bf16[32,4,32,128]{3,2,1,0:T(8,128)(2,1)} %shard_map.132), calls=%async_computation.2 | async-start | bytes 2097152 | tf_op jit(solution)/shard_map/all_to_all | solution.py:391
  87.5 10.7 %shard_map.131 = f32[4,32,4,8,128]{4,3,2,1,0:T(8,128)} custom-call(bf16[32,4,32,128]{3,2,1,0:T(8,128)(2,1)} %bitcast.16, f32[2]{0:T(128)S(1)} %broadcast_multiply_fusion.f_ref), custom_call_target="tpu_custom_call" | custom-call | tf_op jit(solution)/shard_map/pallas_call | solution.py:448
  98.2 11.4 %all-to-all-done.2 = bf16[32,4,32,128]{3,2,1,0:T(8,128)(2,1)S(1)} async-done(((bf16[32,4,32,128]{3,2,1,0:T(8,128)(2,1)}), bf16[32,4,32,128]{3,2,1,0:T(8,128)(2,1)S(1)}, u32[]{:S(2)}, u32[]{:S(2)}) %all-to-all-start.2) | async-done | bytes 1048608 | tf_op jit(solution)/shard_map/all_to_all | solution.py:391
  109.6 4.2 %shard_map.133 = (bf16[4,1024,128]{2,1,0:T(8,128)(2,1)S(1)}, bf16[4,1024,128]{2,1,0:T(8,128)(2,1)S(1)}, f32[16,128]{1,0:T(8,128)S(1)}, bf16[1024,512]{1,0:T(8,128)(2,1)S(1)}, bf16[1024,1024]{1,0:T(8,128)(2,1)S(1)}) custom-call(s32[2]{0:T(128)S(1)} %pad_add_fusion.at_ref, f32[4,2,4,4,4,8,128]{6,5,4,3,2,1,0:T(8,128)} %bitcast.14, ...), custom_call_target="tpu_custom_call" | custom-call | tf_op jit(solution)/shard_map/pallas_call | solution.py:474
  114.4 2.2 %collective-permute-done.2.sgot_ref = f32[16,128]{1,0:T(8,128)S(1)} collective-permute-done((f32[16,128]{1,0:T(8,128)S(1)}, f32[16,128]{1,0:T(8,128)S(1)}, u32[]{:S(2)}, u32[]{:S(2)}) %collective-permute-start.2) | collective-permute-done | bytes 8224 | tf_op jit(solution)/shard_map/ppermute | solution.py:504
  116.6 1.0 shard_map.134
  117.6 1.3 collective-permute-start.6
  118.9 1.6 collective-permute-start.8
  120.4 3.2 %shard_map.135.whole_ref = bf16[16,272,128]{2,1,0:T(8,128)(2,1)} custom-call(bf16[1024,1024]{1,0:T(8,128)(2,1)S(1)} %get-tuple-element.45.normed_ref, bf16[1024,1024]{1,0:T(8,128)(2,1)S(1)} %copy-done, bf16[1024,512]{1,0:T(8,128)(2,1)S(1)} %get-tuple-element.46.g_ref), custom_call_target="tpu_custom_call" | custom-call | tf_op jit(solution)/shard_map/pallas_call | solution.py:522
  124.4 5.8 %all-to-all-start.3 = ((bf16[16,272,128]{2,1,0:T(8,128)(2,1)}), bf16[16,272,128]{2,1,0:T(8,128)(2,1)S(1)}, u32[]{:S(2)}, u32[]{:S(2)}) async-start(bf16[16,272,128]{2,1,0:T(8,128)(2,1)} %shard_map.136), calls=%async_computation.3 | async-start | bytes 2228224 | tf_op jit(solution)/shard_map/all_to_all | solution.py:395
  130.1 1.7 %collective-permute-start.3 = (bf16[1040,128]{1,0:T(8,128)(2,1)}, bf16[1040,128]{1,0:T(8,128)(2,1)S(1)}, u32[]{:S(2)}, u32[]{:S(2)}) collective-permute-start(bf16[1040,128]{1,0:T(8,128)(2,1)} %copy-done.12), channel_id=1, source_target_pairs={{0,2},{1,3},{2,4},{3,5},{4,6},{5,7},{6,0},{7,1},{8,10},{9,11},{10,... | collective-permute-start | bytes 798728 | tf_op jit(solution)/shard_map/ppermute | solution.py:520
  131.8 3.4 %collective-permute-start.4 = (bf16[1040,128]{1,0:T(8,128)(2,1)}, bf16[1040,128]{1,0:T(8,128)(2,1)}, u32[]{:S(2)}, u32[]{:S(2)}) collective-permute-start(bf16[1040,128]{1,0:T(8,128)(2,1)} %copy-done.11), channel_id=1, source_target_pairs={{0,4},{1,5},{2,6},{3,7},{4,0},{5,1},{6,2},{7,3},{8,12},{9,13},{10,... | collective-permute-start | bytes 798728 | tf_op jit(solution)/shard_map/ppermute | solution.py:520
  135.5 10.2 %all-to-all-done.3.in_ref = bf16[16,272,128]{2,1,0:T(8,128)(2,1)S(1)} async-done(((bf16[16,272,128]{2,1,0:T(8,128)(2,1)}), bf16[16,272,128]{2,1,0:T(8,128)(2,1)S(1)}, u32[]{:S(2)}, u32[]{:S(2)}) %all-to-all-start.3) | async-done | bytes 1114144 | tf_op jit(solution)/shard_map/all_to_all | solution.py:395
  146.8 4.6 %collective-permute-done.3.r1_ref = bf16[1040,128]{1,0:T(8,128)(2,1)S(1)} collective-permute-done((bf16[1040,128]{1,0:T(8,128)(2,1)}, bf16[1040,128]{1,0:T(8,128)(2,1)S(1)}, u32[]{:S(2)}, u32[]{:S(2)}) %collective-permute-start.3) | collective-permute-done | bytes 266272 | tf_op jit(solution)/shard_map/ppermute | solution.py:520
  151.4 4.0 %collective-permute-done.4.r2_ref = bf16[1040,128]{1,0:T(8,128)(2,1)} collective-permute-done((bf16[1040,128]{1,0:T(8,128)(2,1)}, bf16[1040,128]{1,0:T(8,128)(2,1)}, u32[]{:S(2)}, u32[]{:S(2)}) %collective-permute-start.4) | collective-permute-done | bytes 266272 | tf_op jit(solution)/shard_map/ppermute | solution.py:520
  155.4 3.1 %collective-permute-done.5.r3_ref = bf16[1040,128]{1,0:T(8,128)(2,1)} collective-permute-done((bf16[1040,128]{1,0:T(8,128)(2,1)}, bf16[1040,128]{1,0:T(8,128)(2,1)}, u32[]{:S(2)}, u32[]{:S(2)}) %collective-permute-start.5) | collective-permute-done | bytes 266272 | tf_op jit(solution)/shard_map/ppermute | solution.py:520
  158.5 1.0 copy-done.6
  159.5 1.0 copy-done.8
  160.6 2.5 %norm_back.1 = bf16[1024,128]{1,0:T(8,128)(2,1)} custom-call(s32[2]{0:T(128)S(1)} %pad_add_fusion.at_ref, bf16[1024,1024]{1,0:T(8,128)(2,1)S(1)} %copy-done.2, f32[1,1024]{1,0:T(1,128)S(1)} %bitcast.13, f32[1024,128]{1,0:T(8,128)S(1)} %copy-done.8, bf16[1040,128]{1,0:T(8,128)(2,1)S(1)} %collective-permute-done.3.r1_ref, ...), custom_call_target="tpu_custom_call" | custom-call | tf_op jit(solution)/shard_map/norm_back/pallas_call | solution.py:557
  (40 shorter events, 5.5 us)
Async XLA Ops:
  0.6 18.4 %copy-start.9 = (f32[1024]{0:T(1024)S(1)}, f32[1024]{0:T(1024)}, u32[]{:S(2)}) copy-start(f32[1024]{0:T(1024)} %param.9) | copy-start | bytes 12292
  1.4 8.3 %collective-permute-start = (bf16[32,512]{1,0:T(8,128)(2,1)S(1)}, bf16[32,512]{1,0:T(8,128)(2,1)S(1)}, u32[]{:S(2)}, u32[]{:S(2)}) collective-permute-start(bf16[32,512]{1,0:T(8,128)(2,1)S(1)} %shard_map.128.mine_ref), channel_id=1, source_target_pairs={{0,32},{8,40},{16,48},{24,56},{32,0},{40,8},{48,16},{56,24},{64,96... | collective-permute-start | bytes 98312 | tf_op jit(solution)/shard_map/ppermute | solution.py:415
  10.3 1.0 copy-start.3
  11.4 22.0 %copy-start = (bf16[1024,1024]{1,0:T(8,128)(2,1)S(1)}, bf16[1024,1024]{1,0:T(8,128)(2,1)}, u32[]{:S(2)}) copy-start(bf16[1024,1024]{1,0:T(8,128)(2,1)} %go_ref.3) | copy-start | bytes 6291460
  11.4 22.0 %all-to-all-start = ((bf16[16,64,512]{2,1,0:T(8,128)(2,1)}), bf16[16,64,512]{2,1,0:T(8,128)(2,1)S(1)}, u32[]{:S(2)}, u32[]{:S(2)}) async-start(bf16[16,64,512]{2,1,0:T(8,128)(2,1)} %copy-done.3), calls=%async_computation | async-start | bytes 2097152 | tf_op jit(solution)/shard_map/all_to_all | solution.py:395
  19.0 1.6 copy-start.1
  23.0 1.3 copy-start.4
  33.4 1.6 copy-start.5
  37.9 10.7 %copy-start.13 = (f32[2]{0:T(128)S(1)}, f32[2]{0:T(128)}, u32[]{:S(2)}) copy-start(f32[2]{0:T(128)} %param.14) | copy-start | bytes 28
  37.9 39.5 %all-to-all-start.1 = ((bf16[32,4,32,128]{3,2,1,0:T(8,128)(2,1)}), bf16[32,4,32,128]{3,2,1,0:T(8,128)(2,1)S(1)}, u32[]{:S(2)}, u32[]{:S(2)}) async-start(bf16[32,4,32,128]{3,2,1,0:T(8,128)(2,1)} %bitcast.15), calls=%async_computation.1 | async-start | bytes 2097152 | tf_op jit(solution)/shard_map/all_to_all | solution.py:391
  81.4 28.2 %all-to-all-start.2 = ((bf16[32,4,32,128]{3,2,1,0:T(8,128)(2,1)}), bf16[32,4,32,128]{3,2,1,0:T(8,128)(2,1)S(1)}, u32[]{:S(2)}, u32[]{:S(2)}) async-start(bf16[32,4,32,128]{3,2,1,0:T(8,128)(2,1)} %shard_map.132), calls=%async_computation.2 | async-start | bytes 2097152 | tf_op jit(solution)/shard_map/all_to_all | solution.py:391
  113.8 2.8 %collective-permute-start.1 = (bf16[4,1024,128]{2,1,0:T(8,128)(2,1)S(1)}, bf16[4,1024,128]{2,1,0:T(8,128)(2,1)S(1)}, u32[]{:S(2)}, u32[]{:S(2)}) collective-permute-start(bf16[4,1024,128]{2,1,0:T(8,128)(2,1)S(1)} %get-tuple-element.36), channel_id=1, source_target_pairs={{0,1},{1,0},{2,3},{3,2},{4,5},{5,4},{6,7},{7,6},{8,9},{9,8},{10,11... | collective-permute-start | bytes 3145736 | tf_op jit(solution)/shard_map/ppermute | solution.py:503
  113.9 2.7 %collective-permute-start.2 = (f32[16,128]{1,0:T(8,128)S(1)}, f32[16,128]{1,0:T(8,128)S(1)}, u32[]{:S(2)}, u32[]{:S(2)}) collective-permute-start(f32[16,128]{1,0:T(8,128)S(1)} %get-tuple-element.38.small_ref), channel_id=1, source_target_pairs={{0,1},{1,0},{2,3},{3,2},{4,5},{5,4},{6,7},{7,6},{8,9},{9,8},{10,11... | collective-permute-start | bytes 24584 | tf_op jit(solution)/shard_map/ppermute | solution.py:504
  117.6 6.1 %copy-start.7 = (f32[1024,128]{1,0:T(8,128)}, f32[1024,128]{1,0:T(8,128)S(1)}, u32[]{:S(2)}) copy-start(f32[1024,128]{1,0:T(8,128)S(1)} %get-tuple-element.39.own_ref) | copy-start | bytes 1572868
  117.6 6.1 %copy-start.10 = (bf16[1040,128]{1,0:T(8,128)(2,1)}, bf16[1040,128]{1,0:T(8,128)(2,1)S(1)}, u32[]{:S(2)}) copy-start(bf16[1040,128]{1,0:T(8,128)(2,1)S(1)} %get-tuple-element.42) | copy-start | bytes 798724
  117.6 6.1 %copy-start.11 = (bf16[1040,128]{1,0:T(8,128)(2,1)}, bf16[1040,128]{1,0:T(8,128)(2,1)S(1)}, u32[]{:S(2)}) copy-start(bf16[1040,128]{1,0:T(8,128)(2,1)S(1)} %get-tuple-element.41) | copy-start | bytes 798724
  117.6 6.0 %copy-start.12 = (bf16[1040,128]{1,0:T(8,128)(2,1)}, bf16[1040,128]{1,0:T(8,128)(2,1)S(1)}, u32[]{:S(2)}) copy-start(bf16[1040,128]{1,0:T(8,128)(2,1)S(1)} %get-tuple-element.40) | copy-start | bytes 798724
  117.6 6.0 %collective-permute-start.6 = (bf16[16,128]{1,0:T(8,128)(2,1)S(1)}, bf16[16,128]{1,0:T(8,128)(2,1)S(1)}, u32[]{:S(2)}, u32[]{:S(2)}) collective-permute-start(bf16[16,128]{1,0:T(8,128)(2,1)S(1)} %get-tuple-element.48), channel_id=1, source_target_pairs={{0,2},{1,3},{2,4},{3,5},{4,6},{5,7},{6,0},{7,1},{8,10},{9,11},{10,... | collective-permute-start | bytes 12296 | tf_op jit(solution)/shard_map/ppermute | solution.py:517
  118.9 4.8 %collective-permute-start.7 = (bf16[16,128]{1,0:T(8,128)(2,1)S(1)}, bf16[16,128]{1,0:T(8,128)(2,1)S(1)}, u32[]{:S(2)}, u32[]{:S(2)}) collective-permute-start(bf16[16,128]{1,0:T(8,128)(2,1)S(1)} %get-tuple-element.49), channel_id=1, source_target_pairs={{0,4},{1,5},{2,6},{3,7},{4,0},{5,1},{6,2},{7,3},{8,12},{9,13},{10,... | collective-permute-start | bytes 12296 | tf_op jit(solution)/shard_map/ppermute | solution.py:517
  118.9 4.8 %collective-permute-start.8 = (bf16[16,128]{1,0:T(8,128)(2,1)S(1)}, bf16[16,128]{1,0:T(8,128)(2,1)S(1)}, u32[]{:S(2)}, u32[]{:S(2)}) collective-permute-start(bf16[16,128]{1,0:T(8,128)(2,1)S(1)} %get-tuple-element.50), channel_id=1, source_target_pairs={{0,6},{1,7},{2,0},{3,1},{4,2},{5,3},{6,4},{7,5},{8,14},{9,15},{10,... | collective-permute-start | bytes 12296 | tf_op jit(solution)/shard_map/ppermute | solution.py:517
  124.3 34.2 %copy-start.2 = (bf16[1024,1024]{1,0:T(8,128)(2,1)S(1)}, bf16[1024,1024]{1,0:T(8,128)(2,1)}, u32[]{:S(2)}) copy-start(bf16[1024,1024]{1,0:T(8,128)(2,1)} %x_ref.3) | copy-start | bytes 6291460
  124.4 21.4 %all-to-all-start.3 = ((bf16[16,272,128]{2,1,0:T(8,128)(2,1)}), bf16[16,272,128]{2,1,0:T(8,128)(2,1)S(1)}, u32[]{:S(2)}, u32[]{:S(2)}) async-start(bf16[16,272,128]{2,1,0:T(8,128)(2,1)} %shard_map.136), calls=%async_computation.3 | async-start | bytes 2228224 | tf_op jit(solution)/shard_map/all_to_all | solution.py:395
  130.1 21.3 %collective-permute-start.3 = (bf16[1040,128]{1,0:T(8,128)(2,1)}, bf16[1040,128]{1,0:T(8,128)(2,1)S(1)}, u32[]{:S(2)}, u32[]{:S(2)}) collective-permute-start(bf16[1040,128]{1,0:T(8,128)(2,1)} %copy-done.12), channel_id=1, source_target_pairs={{0,2},{1,3},{2,4},{3,5},{4,6},{5,7},{6,0},{7,1},{8,10},{9,11},{10,... | collective-permute-start | bytes 798728 | tf_op jit(solution)/shard_map/ppermute | solution.py:520
  131.8 23.6 %collective-permute-start.4 = (bf16[1040,128]{1,0:T(8,128)(2,1)}, bf16[1040,128]{1,0:T(8,128)(2,1)}, u32[]{:S(2)}, u32[]{:S(2)}) collective-permute-start(bf16[1040,128]{1,0:T(8,128)(2,1)} %copy-done.11), channel_id=1, source_target_pairs={{0,4},{1,5},{2,6},{3,7},{4,0},{5,1},{6,2},{7,3},{8,12},{9,13},{10,... | collective-permute-start | bytes 798728 | tf_op jit(solution)/shard_map/ppermute | solution.py:520
  135.2 23.3 %collective-permute-start.5 = (bf16[1040,128]{1,0:T(8,128)(2,1)}, bf16[1040,128]{1,0:T(8,128)(2,1)}, u32[]{:S(2)}, u32[]{:S(2)}) collective-permute-start(bf16[1040,128]{1,0:T(8,128)(2,1)} %copy-done.10), channel_id=1, source_target_pairs={{0,6},{1,7},{2,0},{3,1},{4,2},{5,3},{6,4},{7,5},{8,14},{9,15},{10,... | collective-permute-start | bytes 798728 | tf_op jit(solution)/shard_map/ppermute | solution.py:520
  146.3 17.4 %collective-permute-start.9 = (bf16[144,128]{1,0:T(8,128)(2,1)S(1)}, bf16[144,128]{1,0:T(8,128)(2,1)S(1)}, u32[]{:S(2)}, u32[]{:S(2)}) collective-permute-start(bf16[144,128]{1,0:T(8,128)(2,1)S(1)} %get-tuple-element.51), channel_id=1, source_target_pairs={{0,32},{8,40},{16,48},{24,56},{32,0},{40,8},{48,16},{56,24},{64,96... | collective-permute-start | bytes 110600 | tf_op jit(solution)/shard_map/ppermute | solution.py:546
  158.5 1.0 copy-start.6
  159.5 1.0 copy-start.8
